TPU v7x, 128 devices: a whole 4x4x4 slice. The times are simulated.
128 devices in a mesh: row: 16 (over z_lo, y, core), col: 8 (over x, z_hi).
Axes of the slice: x: 4, y: 4, z: 4 (z_hi: 2, z_lo: 2; z = z_hi * 2 + z_lo), core: 2. Of those that a mesh axis runs over, the one named last changes fastest.
Arguments:
- fixed_matrix_encodings: int32 [8192, 53248], P('row', 'col'), may hold values from 0 to 254, as said below
- line_restore_multiplier: float32 [8192], P('row'), may hold values from 0.001 to 0.01
- central_up_matrix: float32 [8192, 16], P('row', 'col'), may hold values from -1.5 to 1.5
- central_down_matrix: float32 [16, 53248], P('row', 'col'), may hold values from -1.5 to 1.5
- running_mean_up: float32 [8192, 16], P('row', 'col'), may hold values from -1.8 to 1.8
- squared_average_up: float32 [8192, 16], P('row', 'col'), may hold values from 0.05 to 0.5
- running_mean_down: float32 [16, 53248], P('row', 'col'), may hold values from -1.8 to 1.8
- squared_average_down: float32 [16, 53248], P('row', 'col'), may hold values from 0.05 to 0.5
- participant_change_up: bfloat16 [128, 8192, 16], P(('row', 'col')), may hold values from -192 to 192
- participant_change_down: bfloat16 [128, 16, 53248], P(('row', 'col')), may hold values from -192 to 192
- client_tallies: int32 [128, 2], P(('row', 'col')), may hold values from 1 to 64
Outputs:
- combined_normalized_entries: bfloat16 [8192, 53248], P('row', 'col')
- fresh_line_multipliers: float32 [8192], P('row')
- lora_b_next: float32 [8192, 16], P('row', 'col')
- lora_a_next: float32 [16, 53248], P('row', 'col')
- moment_b_next: float32 [8192, 16], P('row', 'col')
- second_b_next: float32 [8192, 16], P('row', 'col')
- moment_a_next: float32 [16, 53248], P('row', 'col')
- second_a_next: float32 [16, 53248], P('row', 'col')
Inputs may be any that keep to these rules, and one draw needn't show every extreme that they name: `fixed_matrix_encodings`: FP8 e4m3 bit patterns; the not-a-number patterns 127 and 255 never occur.
All inputs are finite; a program needn't handle non-finite values. Where the computation divides by a largest or mean magnitude, that divisor is 1e-20 or more.
Results may differ from a plain program's by a relative error of at most 0.0053.
Values may be sent and summed in bfloat16 or wider, within the bound.
No kernel may reach another device: no remote copies, remote signals or barrier semaphores. Data moves between devices by JAX's collectives and lax.ppermute only.
A program may use at most 128 MiB of HBM per device.

v0:
```python
import math

import jax
import jax.numpy as jnp
from jax import lax
from jax.sharding import PartitionSpec as P

first_decay = 0.9
second_decay = 0.99
server_rate = 0.1
adam_floor = 0.001
adapter_scale = 2.0
count_scale = 64.0
fp8_top = 448.0
peak_eps = 1e-06


def cut_along(shard, dim, length):
    dims = shard.shape
    tiles = shard.reshape(*dims[:dim], length, dims[dim] // length, *dims[dim + 1 :])
    return jnp.moveaxis(tiles, dim, 0)


def sent_and_summed(shard, axis, dim):
    length = lax.axis_size(axis)
    tiles = lax.all_to_all(cut_along(shard, dim, length), axis, 0, 0, tiled=True)
    return jnp.sum(tiles.astype(jnp.float32), axis=0)


def sent_together(arrays, axis, dim, along):
    ends, at = ([], 0)
    for a in arrays[:-1]:
        at += a.shape[along]
        ends.append(at)
    both = jnp.concatenate(arrays, axis=along)
    return tuple(jnp.split(sent_and_summed(both, axis, dim), ends, axis=along))


def sent_together_2(arrays, axis, dim, along):
    widths = [math.prod(a.shape[along:]) for a in arrays]
    both = jnp.concatenate(
        [a.reshape(*a.shape[:along], w) for a, w in zip(arrays, widths)], axis=along
    )
    whole = sent_and_summed(both, axis, dim)
    tiles = jnp.split(whole, [sum(widths[:k]) for k in range(1, len(widths))], axis=along)
    return tuple((b.reshape(*whole.shape[:along], *a.shape[along:]) for a, b in zip(arrays, tiles)))


def in_order(tiles, dim):
    dims = list(tiles.shape[1:])
    dims[dim] *= tiles.shape[0]
    return jnp.moveaxis(tiles, 0, dim).reshape(dims)


def sent_to_all(shard, axis):
    length = lax.axis_size(axis)
    return lax.all_to_all(
        jnp.broadcast_to(shard[None], (length, *shard.shape)), axis, 0, 0, tiled=True
    )


def gathered_copies(shard, axis, dim):
    return in_order(sent_to_all(shard, axis), dim)


def over_copies(shard, axis):
    everything = sent_to_all(shard, axis)
    return jnp.max(everything, axis=0)


def decode(codes):
    sign_bit = codes // 128
    exponent = codes // 8 % 16
    mantissa = codes % 8
    gaussian_sample = (8 + mantissa).astype(jnp.float32) * jnp.exp2(
        (exponent - 10).astype(jnp.float32)
    )
    subnormal = mantissa.astype(jnp.float32) * 2.0 ** (-9)
    magnitude = jnp.where(exponent > 0, gaussian_sample, subnormal)
    return magnitude * (1.0 - 2.0 * sign_bit.astype(jnp.float32))


def adaptive_update(param, moment, second, grad):
    moment_next = first_decay * moment + (1.0 - first_decay) * grad
    second_next = second_decay * second + (1.0 - second_decay) * grad * grad
    param_next = param - server_rate * moment_next / (jnp.sqrt(second_next) + adam_floor)
    return (param_next, moment_next, second_next)


def local(
    fixed_matrix_encodings,
    line_restore_multiplier,
    central_up_matrix,
    central_down_matrix,
    running_mean_up,
    squared_average_up,
    running_mean_down,
    squared_average_down,
    participant_change_up,
    participant_change_down,
    client_tallies,
):
    rows_count = lax.axis_size("row")
    cols_count = lax.axis_size("col")
    everyone = client_tallies.shape[0] * rows_count * cols_count
    weights = client_tallies.astype(jnp.float32) / (count_scale * everyone)
    summed_b = jnp.sum(
        weights[:, 0, None, None] * participant_change_up.astype(jnp.float32), axis=0
    )
    summed_a = jnp.sum(
        weights[:, 1, None, None] * participant_change_down.astype(jnp.float32), axis=0
    )
    depth_all, rank_all = summed_b.shape
    width_all = summed_a.shape[1]
    depth_dev = depth_all // rows_count
    rank_dev = rank_all // cols_count
    ranks_held = rank_all // rows_count
    width_dev = width_all // cols_count
    shaped_b = summed_b.reshape(rows_count, depth_dev, cols_count, rank_dev).transpose(0, 2, 1, 3)
    flat_b = shaped_b.reshape(rows_count, cols_count * depth_dev * rank_dev)
    part_b, part_a = sent_together(
        (flat_b.astype(jnp.bfloat16), summed_a.astype(jnp.bfloat16)), "row", 0, 1
    )
    part_b = part_b.reshape(cols_count, depth_dev * rank_dev)
    part_a = part_a.reshape(ranks_held, cols_count, width_dev).transpose(1, 0, 2)
    gradient_b, gradient_a = sent_together_2(
        (part_b.astype(jnp.bfloat16), part_a.astype(jnp.bfloat16)), "col", 0, 1
    )
    gradient_b = gradient_b.reshape(depth_dev, rank_dev)
    gradient_a = gradient_a[0]
    updated_factor_b, updated_moment_b, updated_variance_b = adaptive_update(
        central_up_matrix, running_mean_up, squared_average_up, gradient_b
    )
    updated_factor_a, updated_moment_a, updated_variance_a = adaptive_update(
        central_down_matrix, running_mean_down, squared_average_down, gradient_a
    )
    thin_up_matrix = gathered_copies(updated_factor_b.astype(jnp.bfloat16), "col", 1)
    lowrank_a = gathered_copies(updated_factor_a.astype(jnp.bfloat16), "row", 0)
    decode_weight = decode(fixed_matrix_encodings) * line_restore_multiplier[:, None]
    merged_weight = decode_weight + adapter_scale * jnp.dot(
        thin_up_matrix, lowrank_a, preferred_element_type=jnp.float32
    )
    local_peak = jnp.max(jnp.abs(merged_weight), axis=1)
    peak = over_copies(local_peak, "col") + peak_eps
    combined_normalized_entries = (merged_weight / peak[:, None]).astype(jnp.bfloat16)
    return (
        combined_normalized_entries,
        peak / fp8_top,
        updated_factor_b,
        updated_factor_a,
        updated_moment_b,
        updated_variance_b,
        updated_moment_a,
        updated_variance_a,
    )


def solution(mesh):
    return jax.shard_map(
        local,
        mesh=mesh,
        in_specs=(
            P("row", "col"),
            P("row"),
            P("row", "col"),
            P("row", "col"),
            P("row", "col"),
            P("row", "col"),
            P("row", "col"),
            P("row", "col"),
            P(("row", "col"), None, None),
            P(("row", "col"), None, None),
            P(("row", "col"), None),
        ),
        out_specs=(
            P("row", "col"),
            P("row"),
            P("row", "col"),
            P("row", "col"),
            P("row", "col"),
            P("row", "col"),
            P("row", "col"),
            P("row", "col"),
        ),
        check_vma=False,
    )
```

profile of v0, /device:TPU:0, one launch (start us, length us, event | category | flops | bytes accessed | tf_op | source)
XLA Modules:
  0.0 159.2 jit_solution(12222872169656259089)
XLA Ops:
  0.6 0.7 convert_multiply_fusion
  1.3 0.6 fusion.20
  1.9 1.6 %multiply_convert_fusion.1 = bf16[1,8192,16]{1,2,0:T(8,128)(2,1)S(1)} fusion(bf16[1,8192,16]{1,2,0:T(8,128)(2,1)} %param.19, f32[]{:T(128)} %bitcast), kind=kLoop, calls=%fused_computation.29 | loop fusion | flops 393216 | bytes 524292 | tf_op jit(solution)/shard_map/convert_element_type | solution.py:122
  3.6 1.4 copy.86
  5.0 0.8 copy.87
  5.8 2.4 %fusion.12 = bf16[16,53248]{1,0:T(8,128)(2,1)S(1)} fusion(bf16[1,16,53248]{2,1,0:T(8,128)(2,1)} %param.20, f32[]{:T(128)} %bitcast.3), kind=kLoop, calls=%fused_computation.28 | loop fusion | flops 2555904 | bytes 3407876 | tf_op jit(solution)/shard_map/convert_element_type | solution.py:122
  8.4 0.5 broadcast.72
  8.9 2.8 %reduce.14 = bf16[16,61440]{1,0:T(8,128)(2,1)} reduce(bf16[16,1,61440]{2,0,1:T(8,128)(2,1)S(1)} %maximum_bitcast_fusion, bf16[]{:T(256)} %broadcast.72), dimensions={1}, to_apply=%copy.88.reduce_sub_computation | reduce | bytes 3932162 | tf_op jit(solution)/shard_map/reshape | solution.py:20
  11.7 2.9 %reshape.85 = bf16[16,2,30720]{2,1,0:T(2,128)(2,1)S(1)} reshape(bf16[16,61440]{1,0:T(8,128)(2,1)} %reduce.14) | data formatting | bytes 3932160
  14.6 32.0 %all_to_all.26 = bf16[16,2,30720]{2,1,0:T(2,128)(2,1)} all-to-all(bf16[16,2,30720]{2,1,0:T(2,128)(2,1)S(1)} %reshape.85), channel_id=1, replica_groups=mesh['row'=16,'col'=8] {'row'}, dimensions={0} | all-to-all | bytes 3932160 | tf_op jit(solution)/shard_map/all_to_all | solution.py:26
  46.6 10.3 %reshape.86 = bf16[16,1,61440]{2,1,0:T(2,128)(2,1)} reshape(bf16[16,2,30720]{2,1,0:T(2,128)(2,1)} %all_to_all.26) | data formatting | bytes 3932160
  56.9 5.7 %reduce.3 = bf16[61440]{0:T(1024)(128)(2,1)S(1)} reduce(bf16[16,1,61440]{2,1,0:T(2,128)(2,1)} %reshape.86, bf16[]{:T(256)} %constant.98), dimensions={0,1}, to_apply=%region_0.0.clone | reduce | flops 921600 | bytes 2088962 | tf_op jit(solution)/shard_map/reduce_sum | solution.py:27
  62.8 0.6 slice_reduce_fusion
  63.6 0.7 reduce.15
  64.3 15.0 %all_to_all.27 = bf16[8,2,3840]{2,1,0:T(2,128)(2,1)S(1)} all-to-all(bf16[8,2,3840]{2,1,0:T(2,128)(2,1)S(1)} %reshape.87), channel_id=1, replica_groups=mesh['row'=16,'col'=8] {'col'}, dimensions={0} | all-to-all | bytes 245760 | tf_op jit(solution)/shard_map/all_to_all | solution.py:26
  79.4 0.3 convert_reduce_fusion
  79.7 0.2 reshape.71
  80.0 0.6 fusion.18
  80.7 0.6 broadcast_in_dim.8
  81.3 3.3 %all-to-all-start.2 = ((bf16[8,512,2]{1,2,0:T(2,128)(2,1)}), bf16[8,512,2]{1,2,0:T(2,128)(2,1)S(1)}, u32[]{:S(2)}, u32[]{:S(2)}) async-start(bf16[8,512,2]{1,2,0:T(2,128)(2,1)} %broadcast_in_dim.8), calls=%async_computation.2 | async-start | bytes 32768 | tf_op jit(solution)/shard_map/all_to_all | solution.py:57
  84.6 0.8 convert_reduce_fusion.1
  85.4 0.2 broadcast_in_dim.10
  85.7 1.9 %reduce.16 = bf16[16,6656]{1,0:T(8,128)(2,1)S(1)} reduce(bf16[16,1,6656]{2,1,0:T(2,128)(2,1)S(1)} %broadcast_in_dim.10, bf16[]{:T(256)} %broadcast.72), dimensions={1}, to_apply=%broadcast_in_dim.10.reduce_sub_computation | reduce | bytes 425986 | tf_op jit(solution)/shard_map/broadcast_in_dim | solution.py:58
  87.5 0.7 reshape.89
  88.3 4.0 %all-to-all-done.2 = bf16[8,512,2]{1,2,0:T(2,128)(2,1)S(1)} async-done(((bf16[8,512,2]{1,2,0:T(2,128)(2,1)}), bf16[8,512,2]{1,2,0:T(2,128)(2,1)S(1)}, u32[]{:S(2)}, u32[]{:S(2)}) %all-to-all-start.2) | async-done | bytes 16416 | tf_op jit(solution)/shard_map/all_to_all | solution.py:57
  92.2 3.7 %all-to-all-start.3 = ((bf16[16,2,3328]{2,1,0:T(2,128)(2,1)}), bf16[16,2,3328]{2,1,0:T(2,128)(2,1)S(1)}, u32[]{:S(2)}, u32[]{:S(2)}) async-start(bf16[16,2,3328]{2,1,0:T(2,128)(2,1)} %reshape.89), calls=%async_computation.3 | async-start | bytes 425984 | tf_op jit(solution)/shard_map/all_to_all | solution.py:57
  96.0 7.1 %all-to-all-done.3 = bf16[16,2,3328]{2,1,0:T(2,128)(2,1)S(1)} async-done(((bf16[16,2,3328]{2,1,0:T(2,128)(2,1)}), bf16[16,2,3328]{2,1,0:T(2,128)(2,1)S(1)}, u32[]{:S(2)}, u32[]{:S(2)}) %all-to-all-start.3) | async-done | bytes 213024 | tf_op jit(solution)/shard_map/all_to_all | solution.py:57
  103.1 0.2 reshape.90
  103.3 35.0 %abs_reduce_fusion = (f32[512]{0:T(512)S(1)}, f32[512,6656]{1,0:T(8,128)}) fusion(bf16[512,16]{0,1:T(8,128)(2,1)S(1)} %reshape.72, bf16[16,1,6656]{2,1,0:T(2,128)(2,1)S(1)} %reshape.90, f32[512]{0:T(512)S(1)} %copy-done.6, s32[512,6656]{1,0:T(8,128)} %param.11), kind=kOutput, calls=%fused_computation.20 | convolution fusion | flops 310115840 | bytes 27496448 | tf_op jit(solution)/shard_map/dot_general | solution.py:140
  138.3 10.6 %all_to_all.28 = f32[8,1,512]{2,1,0:T(1,128)S(1)} all-to-all(f32[8,1,512]{2,1,0:T(1,128)S(1)} %broadcast_in_dim.11), channel_id=1, replica_groups=mesh['row'=16,'col'=8] {'col'}, dimensions={0} | all-to-all | bytes 32768 | tf_op jit(solution)/shard_map/all_to_all | solution.py:57
  149.0 0.6 broadcast_multiply_fusion
  149.6 9.6 %divide_convert_fusion = bf16[512,6656]{1,0:T(8,128)(2,1)} fusion(f32[512,6656]{1,0:T(8,128)} %get-tuple-element.61, f32[512]{0:T(512)S(1)} %get-tuple-element.57), kind=kLoop, calls=%fused_computation.19 | loop fusion | flops 6815744 | bytes 20449280 | tf_op jit(solution)/shard_map/convert_element_type | solution.py:145
  (29 shorter events, 1.0 us)
Async XLA Ops:
  8.2 71.8 %copy-start.3 = (f32[512,2]{0,1:T(2,128)S(1)}, f32[512,2]{0,1:T(2,128)}, u32[]{:S(2)}) copy-start(f32[512,2]{0,1:T(2,128)} %param.13) | copy-start | bytes 12292
  8.2 71.8 %copy-start.4 = (f32[512,2]{0,1:T(2,128)S(1)}, f32[512,2]{0,1:T(2,128)}, u32[]{:S(2)}) copy-start(f32[512,2]{0,1:T(2,128)} %param.15) | copy-start | bytes 12292
  8.2 71.8 %copy-start.5 = (f32[512,2]{0,1:T(2,128)S(1)}, f32[512,2]{0,1:T(2,128)}, u32[]{:S(2)}) copy-start(f32[512,2]{0,1:T(2,128)} %param.16) | copy-start | bytes 12292
  8.2 76.4 %copy-start = (f32[1,6656]{1,0:T(1,128)S(1)}, f32[1,6656]{1,0:T(1,128)}, u32[]{:S(2)}) copy-start(f32[1,6656]{1,0:T(1,128)} %param.14) | copy-start | bytes 79876
  8.3 76.4 %copy-start.1 = (f32[1,6656]{1,0:T(1,128)S(1)}, f32[1,6656]{1,0:T(1,128)}, u32[]{:S(2)}) copy-start(f32[1,6656]{1,0:T(1,128)} %param.17) | copy-start | bytes 79876
  8.3 76.4 %copy-start.2 = (f32[1,6656]{1,0:T(1,128)S(1)}, f32[1,6656]{1,0:T(1,128)}, u32[]{:S(2)}) copy-start(f32[1,6656]{1,0:T(1,128)} %param.18) | copy-start | bytes 79876
  8.9 94.4 %copy-start.6 = (f32[512]{0:T(512)S(1)}, f32[512]{0:T(512)}, u32[]{:S(2)}) copy-start(f32[512]{0:T(512)} %param.12) | copy-start | bytes 6148
  81.3 11.0 %all-to-all-start.2 = ((bf16[8,512,2]{1,2,0:T(2,128)(2,1)}), bf16[8,512,2]{1,2,0:T(2,128)(2,1)S(1)}, u32[]{:S(2)}, u32[]{:S(2)}) async-start(bf16[8,512,2]{1,2,0:T(2,128)(2,1)} %broadcast_in_dim.8), calls=%async_computation.2 | async-start | bytes 32768 | tf_op jit(solution)/shard_map/all_to_all | solution.py:57
  92.2 10.9 %all-to-all-start.3 = ((bf16[16,2,3328]{2,1,0:T(2,128)(2,1)}), bf16[16,2,3328]{2,1,0:T(2,128)(2,1)S(1)}, u32[]{:S(2)}, u32[]{:S(2)}) async-start(bf16[16,2,3328]{2,1,0:T(2,128)(2,1)} %reshape.89), calls=%async_computation.3 | async-start | bytes 425984 | tf_op jit(solution)/shard_map/all_to_all | solution.py:57
where the time goes:
time: 160 us; the launch traced here: 159 us
  blocking collectives  57.6 us (36%)
  matrix products  35 us (22%)
  other arithmetic  27.7 us (17%)
  local copies, waits for them, and re-layouts  19.8 us (12%)
  waiting for transfers between devices  11.1 us (7%)
  starting transfers between devices  7.04 us (4%)
    all_to_all x2, blocking collectives, sent_and_summed(): lax.all_to_all(cut_along(shard, dim, length), axis, 0, 0, tiled=True)  47 us
    dot_general x1, matrix products, local(): jnp.dot(thin_up_matrix, lowrank_a, preferred_element_type=jnp.float32)  35 us
    unnamed x21, local copies, waits for them, and re-layouts  14.3 us
    all_to_all x2, waiting for transfers between devices, sent_to_all(): lax.all_to_all(jnp.broadcast_to(shard[None], (length, *shard.shape)), axi...  11.1 us
    all_to_all x1, blocking collectives, sent_to_all(): lax.all_to_all(jnp.broadcast_to(shard[None], (length, *shard.shape)), axi...  10.6 us
    convert_element_type x1, other arithmetic, local(): (merged_weight / peak[:, None]).astype(jnp.bfloat16)  9.61 us
    all_to_all x2, starting transfers between devices, sent_to_all(): lax.all_to_all(jnp.broadcast_to(shard[None], (length, *shard.shape)), axi...  7.04 us
    reduce_sum x2, other arithmetic, sent_and_summed(): return jnp.sum(tiles.astype(jnp.float32), axis=0)  5.93 us
  transfers between devices with their start and end apart: 2, of which 2 were waited for; matrix products, arithmetic and copies ran while one was open for 2% of the time, Pallas kernels for 0%

commit v1 on v0

v1 whole, which is shorter than its diff:
```python
import functools

import jax
import jax.numpy as jnp
from jax import lax
from jax.experimental import pallas as pl
from jax.experimental.pallas import tpu as pltpu
from jax.sharding import Mesh, PartitionSpec as P

first_decay = 0.9
second_decay = 0.99
server_rate = 0.1
adam_floor = 0.001
adapter_scale = 2.0
count_scale = 64.0
fp8_top = 448.0
peak_eps = 1e-06

f32, bf16, i32 = jnp.float32, jnp.bfloat16, jnp.int32
SDS = jax.ShapeDtypeStruct

ROW, COL = ("zl", "y", "c"), ("x", "zh")
CHIPS, COLS = 8, 8
RANKS = 16
DEPTH, WIDTH = 512, 6656
HALF = WIDTH // 2
FULL_B, FULL_A = DEPTH * 16, WIDTH * 8
LANES = HALF + DEPTH
PIECE = 512
PIECES = WIDTH // PIECE


def adaptive_update(param, moment, second, grad):
    moment_next = first_decay * moment + (1.0 - first_decay) * grad
    second_next = second_decay * second + (1.0 - second_decay) * grad * grad
    param_next = param - server_rate * moment_next / (jnp.sqrt(second_next) + adam_floor)
    return (param_next, moment_next, second_next)


def params_for(mib):
    return pltpu.CompilerParams(vmem_limit_bytes=mib << 20)


def in_hbm():
    return pl.BlockSpec(memory_space=pltpu.HBM)


def stay(x):
    return pltpu.with_memory_space_constraint(x, pltpu.HBM)


def near(x):
    return pltpu.with_memory_space_constraint(x, pltpu.VMEM)


def in_any():
    return pl.BlockSpec(memory_space=pl.ANY)


def in_vmem():
    return pl.BlockSpec(memory_space=pltpu.VMEM)


def in_smem():
    return pl.BlockSpec(memory_space=pltpu.SMEM)


DEC_ROWS = 32
SLOTS = 3


def decode_kernel(*refs):
    codes, state = refs[0], refs[1:7]
    out, kept = refs[7], refs[8:14]
    buf, done, sems, out_sems, state_sems = refs[14:]
    steps = DEPTH // DEC_ROWS

    def rows(step):
        return pl.ds(pl.multiple_of(step * DEC_ROWS, DEC_ROWS), DEC_ROWS)

    def fetch(step, slot):
        return pltpu.make_async_copy(codes.at[rows(step), :], buf.at[slot], sems.at[slot])

    def store(step, slot):
        return pltpu.make_async_copy(done.at[slot], out.at[rows(step), :], out_sems.at[slot])

    for s in range(SLOTS - 1):
        fetch(s, s).start()
    moves = [pltpu.make_async_copy(a, b, state_sems.at[q]) for q, (a, b) in enumerate(zip(state, kept))]
    for move in moves:
        move.start()

    def step(s, carry):
        slot = lax.rem(s, SLOTS)
        fetch(s, slot).wait()

        @pl.when(s + SLOTS - 1 < steps)
        def _():
            fetch(s + SLOTS - 1, lax.rem(s + SLOTS - 1, SLOTS)).start()

        @pl.when(s >= SLOTS)
        def _():
            store(s - SLOTS, slot).wait()

        def group(g, carry):
            at = pl.ds(pl.multiple_of(g * 16, 16), 16)
            for t in range(PIECES):
                here = pl.ds(t * PIECE, PIECE)
                code = buf[slot, at, here]
                exponent = jnp.bitwise_and(lax.shift_right_logical(code, 3), 15)
                mantissa = jnp.bitwise_and(code, 7)
                whole = jnp.where(exponent > 0, mantissa + 8, mantissa)
                value = lax.shift_left(whole, jnp.maximum(exponent, 1))
                value = jnp.where(code >= 128, -value, value)
                done[slot, at, here] = value.astype(f32).astype(bf16)
            return carry

        lax.fori_loop(0, DEC_ROWS // 16, group, 0)
        store(s, slot).start()
        return carry

    lax.fori_loop(0, steps, step, 0)
    for s in range(steps - SLOTS, steps):
        store(s, s % SLOTS).wait()
    for move in moves:
        move.wait()


def decode(codes, state):
    return pl.pallas_call(
        decode_kernel,
        out_shape=(pltpu.HBM((DEPTH, WIDTH), bf16),) + tuple(pltpu.VMEM(x.shape, f32) for x in state),
        in_specs=[in_hbm()] * 7,
        out_specs=(in_hbm(),) + (in_vmem(),) * 6,
        scratch_shapes=[
            pltpu.VMEM((SLOTS, DEC_ROWS, WIDTH), i32),
            pltpu.VMEM((SLOTS, DEC_ROWS, WIDTH), bf16),
            pltpu.SemaphoreType.DMA((SLOTS,)),
            pltpu.SemaphoreType.DMA((SLOTS,)),
            pltpu.SemaphoreType.DMA((6,)),
        ],
        compiler_params=params_for(8),
        cost_estimate=pl.CostEstimate(flops=40_000_000, transcendentals=0, bytes_accessed=24_000_000),
        name="decode",
    )(stay(codes), *[stay(x) for x in state])


def pair_kernel(own_w, mate_w, own_a, mate_a, own_b, mate_b, out, xa, xb, sem_a, sem_b):
    core = lax.axis_index("c")
    part = HALF // 2
    copies = {}
    for t in range(2):
        for src, ref in enumerate((own_a, mate_a)):
            for c in range(COLS):
                start = pl.multiple_of(c * WIDTH + core * HALF + t * part, 128)
                copies[t, src, c] = pltpu.make_async_copy(
                    ref.at[:, pl.ds(start, part)],
                    xa.at[pl.ds(src * 128 + c * 16, 16), pl.ds(t * part, part)],
                    sem_a.at[t, src, c],
                )
                copies[t, src, c].start()
        if t == 0:
            b_copies = []
            for src, ref in enumerate((own_b, mate_b)):
                b_copies.append(
                    pltpu.make_async_copy(
                        ref.at[pl.ds(pl.multiple_of(core * 8, 8), 8), :], xb.at[src], sem_b.at[src]
                    )
                )
                b_copies[-1].start()
    o = lax.broadcasted_iota(i32, (128, 256), 0)
    k = lax.broadcasted_iota(i32, (128, 256), 1)
    same_block = jnp.bitwise_and(lax.shift_right_logical(o, 1), 7) == jnp.bitwise_and(
        lax.shift_right_logical(k, 4), 7
    )
    rank = lax.shift_right_logical(o, 4) * 2 + jnp.bitwise_and(o, 1)
    same_rank = rank == jnp.bitwise_and(k, 15)
    weight = jnp.where(k < 128, own_w[0, 1], mate_w[0, 1])
    pick = jnp.where(jnp.logical_and(same_block, same_rank), weight, 0.0).astype(bf16)
    for b in b_copies:
        b.wait()
    for j in range(CHIPS):
        halves = []
        for p in range(2):
            at = pl.ds((2 * j + p) * DEPTH, DEPTH)
            halves.append(
                own_w[0, 0] * xb[0, :, at].astype(f32) + mate_w[0, 0] * xb[1, :, at].astype(f32)
            )
        out[pl.ds(j * 16, 16), pl.ds(HALF, DEPTH)] = jnp.concatenate(halves, axis=0).astype(bf16)
    for t in range(2):
        for src in range(2):
            for c in range(COLS):
                copies[t, src, c].wait()
        at = pl.ds(t * part, part)
        out[:, at] = jnp.dot(pick, xa[:, at], preferred_element_type=f32).astype(bf16)


def pair_sum(own_w, mate_w, own_a, mate_a, own_b, mate_b):
    return pl.pallas_call(
        pair_kernel,
        out_shape=SDS((CHIPS * 16, LANES), bf16),
        in_specs=[in_smem(), in_smem(), in_hbm(), in_any(), in_hbm(), in_any()],
        out_specs=in_vmem(),
        scratch_shapes=[
            pltpu.VMEM((256, HALF), bf16),
            pltpu.VMEM((2, 8, FULL_B), bf16),
            pltpu.SemaphoreType.DMA((2, 2, COLS)),
            pltpu.SemaphoreType.DMA((2,)),
        ],
        compiler_params=params_for(16),
        name="pair_sum",
    )(own_w, mate_w, stay(own_a), mate_a, stay(own_b), mate_b)


def row_kernel(got, out, scr):
    total = got[0].astype(f32)
    for j in range(1, CHIPS):
        total = total + got[j].astype(f32)
    scr[...] = jnp.zeros_like(scr)
    for d in range(16):
        core, col = divmod(d, COLS)
        a = 2 * col + core
        for i in range(7):
            w = min(PIECE, HALF - i * PIECE)
            scr[d, pl.ds(i, 1), pl.ds(0, w)] = total[a : a + 1, i * PIECE : i * PIECE + w]
        scr[d, pl.ds(8, 8), :] = total[core * 8 : core * 8 + 8, HALF:LANES]
    out[...] = scr[...].astype(bf16)


def row_sum(got):
    return pl.pallas_call(
        row_kernel,
        out_shape=SDS((16, 16, PIECE), bf16),
        in_specs=[in_vmem()],
        out_specs=in_vmem(),
        scratch_shapes=[pltpu.VMEM((16, 16, PIECE), f32)],
        compiler_params=params_for(16),
        name="row_sum",
    )(got)


APART = (0, 1, 4, 5, 2, 3, 6, 7)


def col_gather(block):
    for axis, perm in (
        ("zh", [(0, 1), (1, 0)]),
        ("x", [(0, 2), (1, 3), (2, 0), (3, 1)]),
        ("x", [(0, 1), (1, 0), (2, 3), (3, 2)]),
    ):
        other = lax.ppermute(block, axis, perm)
        last, block = block, jnp.concatenate([block, other], axis=0)
    return last, other


def step_kernel(
    got, state_0, state_1, pa, ma, va, pb, mb, vb,
    pa_n, ma_n, va_n, pb_n, mb_n, vb_n, send, factor, ga, scr, rows,
):
    col = lax.axis_index("x") * 2 + lax.axis_index("zh")
    tops = []
    for h in range(2):
        acc = got[h * 8, 0:16, :].astype(f32)
        for c in range(1, COLS):
            acc = acc + got[h * 8 + c, 0:16, :].astype(f32)
        for i in range(7):
            w = min(PIECE, HALF - i * PIECE)
            ga[:, pl.ds(h * HALF + i * PIECE, w)] = acc[i : i + 1, 0:w]
        tops.append(acc[8:16, :])
    gb = jnp.concatenate(tops, axis=0)
    for n, apart in enumerate(APART):
        block = (state_0, state_1)[n // 4][pl.ds(n % 4 * 8, 8), :]
        owner = jnp.bitwise_xor(col, apart)
        for q in range(3):
            scr[q, owner] = block[2 * q : 2 * q + 2, :]
    whole = [scr[q].reshape(RANKS, DEPTH) for q in range(3)]
    full = adaptive_update(*whole, gb)[0]
    factor[...] = full.astype(bf16)
    at = lax.broadcasted_iota(i32, gb.shape, 0)
    own = [
        jnp.sum(jnp.where(at == 2 * col + q, gb, 0.0), axis=0, keepdims=True) for q in range(2)
    ]
    pb_n[...], mb_n[...], vb_n[...] = adaptive_update(
        pb[...], mb[...], vb[...], jnp.concatenate(own, axis=0)
    )
    pn, mn, vn = adaptive_update(pa[...], ma[...], va[...], ga[...])
    pa_n[...], ma_n[...], va_n[...] = pn, mn, vn
    rows[...] = jnp.zeros_like(rows)
    for i in range(PIECES):
        rows[pl.ds(i, 1), :] = pn[:, i * PIECE : (i + 1) * PIECE]
    message = rows[...].astype(bf16)
    for d in range(16):
        send[d] = message


def server_step(got, col_state, a_state, b_state):
    a_shape, b_shape = SDS((1, WIDTH), f32), SDS((2, DEPTH), f32)
    return pl.pallas_call(
        step_kernel,
        out_shape=(a_shape,) * 3
        + (b_shape,) * 3
        + (SDS((16, 16, PIECE), bf16), SDS((RANKS, DEPTH), bf16)),
        in_specs=[in_vmem()] * 9,
        out_specs=(in_vmem(),) * 8,
        scratch_shapes=[
            pltpu.VMEM((1, WIDTH), f32),
            pltpu.VMEM((3, COLS, 2, DEPTH), f32),
            pltpu.VMEM((16, PIECE), f32),
        ],
        compiler_params=params_for(16),
        name="server_step",
    )(got, *col_state, *map(near, a_state), *map(near, b_state))


def spread_kernel(factor, out):
    k = lax.broadcasted_iota(i32, (RANKS, 256), 1)
    r = lax.broadcasted_iota(i32, (RANKS, 256), 0)
    repeat = jnp.where(lax.shift_right_logical(k, 4) == r, adapter_scale, 0.0).astype(bf16)
    tall = jnp.transpose(factor[...].astype(f32)).astype(bf16)
    out[...] = jnp.dot(tall, repeat, preferred_element_type=f32).astype(bf16)


def spread(factor):
    return pl.pallas_call(
        spread_kernel,
        out_shape=SDS((DEPTH, 256), bf16),
        in_specs=[in_vmem()],
        out_specs=in_vmem(),
        compiler_params=params_for(16),
        name="spread",
    )(factor)


BLOCK = 512


def merge_kernel(dec, scale, wide, ranks, merged, peaks, buf, row_scale, tops, sems):
    fetches = []
    for i in range(PIECES):
        fetches.append(
            pltpu.make_async_copy(dec.at[:, pl.ds(i * PIECE, PIECE)], buf.at[i], sems.at[i])
        )
        fetches[-1].start()
    row_scale[...] = jnp.transpose(jnp.broadcast_to(scale[...] * 2.0**-10, (128, DEPTH)))
    lane = jnp.bitwise_and(lax.broadcasted_iota(i32, (BLOCK, 256), 1), 15)
    right = ranks[...].reshape(256, PIECE)
    tops[...] = jnp.zeros_like(tops)
    for i in range(PIECES):
        fetches[i].wait()
        for b in range(DEPTH // BLOCK):
            at = pl.ds(b * BLOCK, BLOCK)
            left = wide[at, :]
            one = jnp.where(lane == i, left, jnp.zeros_like(left))
            low = jnp.dot(one, right, preferred_element_type=f32)
            top = tops[at, :]
            for t in range(PIECE // 128):
                here = pl.ds(t * 128, 128)
                whole = buf[i, at, here].astype(f32) * row_scale[at, :] + low[:, t * 128 : t * 128 + 128]
                merged[i, at, here] = whole
                top = jnp.maximum(top, jnp.abs(whole))
            tops[at, :] = top
    peak = jnp.max(jnp.transpose(tops[...]), axis=0, keepdims=True)
    for c in range(COLS):
        peaks[c] = peak


def merge(dec, scale, wide, ranks):
    return pl.pallas_call(
        merge_kernel,
        out_shape=(pltpu.VMEM((PIECES, DEPTH, PIECE), f32), SDS((COLS, 1, DEPTH), f32)),
        in_specs=[in_hbm()] + [in_vmem()] * 3,
        out_specs=(in_vmem(), in_vmem()),
        scratch_shapes=[
            pltpu.VMEM((PIECES, DEPTH, PIECE), bf16),
            pltpu.VMEM((DEPTH, 128), f32),
            pltpu.VMEM((DEPTH, 128), f32),
            pltpu.SemaphoreType.DMA((PIECES,)),
        ],
        compiler_params=params_for(16),
        name="merge",
    )(stay(dec), scale, wide, ranks)


OUT_ROWS = 32


def normalise_kernel(merged, peaks, out, scales, inverse, buf, sems):
    peak = peaks[0]
    for c in range(1, COLS):
        peak = jnp.maximum(peak, peaks[c])
    peak = peak + peak_eps
    scales[...] = peak / fp8_top
    inverse[...] = jnp.transpose(jnp.broadcast_to(1.0 / peak, (128, DEPTH)))
    steps, slots = DEPTH // OUT_ROWS, 4

    def store(step, slot):
        return pltpu.make_async_copy(
            buf.at[slot],
            out.at[pl.ds(pl.multiple_of(step * OUT_ROWS, OUT_ROWS), OUT_ROWS), :],
            sems.at[slot],
        )

    def step(s, carry):
        slot = lax.rem(s, slots)

        @pl.when(s >= slots)
        def _():
            store(s - slots, slot).wait()

        for g in range(OUT_ROWS // 16):
            row = pl.multiple_of(s * OUT_ROWS + g * 16, 16)
            inv = inverse[pl.ds(row, 16), :]
            inv = jnp.concatenate([inv] * (PIECE // 128), axis=1)
            for t in range(PIECES):
                here = pl.ds(t * PIECE, PIECE)
                buf[slot, pl.ds(g * 16, 16), here] = (merged[t, pl.ds(row, 16), :] * inv).astype(bf16)
        store(s, slot).start()
        return carry

    lax.fori_loop(0, steps, step, 0)
    for s in range(steps - slots, steps):
        store(s, s % slots).wait()


def normalise(merged, peaks):
    return pl.pallas_call(
        normalise_kernel,
        out_shape=(SDS((DEPTH, WIDTH), bf16), SDS((1, DEPTH), f32)),
        in_specs=[in_vmem(), in_vmem()],
        out_specs=(in_hbm(), in_vmem()),
        scratch_shapes=[
            pltpu.VMEM((DEPTH, 128), f32),
            pltpu.VMEM((4, OUT_ROWS, WIDTH), bf16),
            pltpu.SemaphoreType.DMA((4,)),
        ],
        compiler_params=params_for(16),
        name="normalise",
    )(near(merged), peaks)


def local(codes, scale, pb, pa, mb, vb, ma, va, delta_b, delta_a, tallies):
    exchange = functools.partial(lax.all_to_all, split_axis=0, concat_axis=0, tiled=True)
    mate = functools.partial(lax.ppermute, axis_name="c", perm=[(0, 1), (1, 0)])
    weights = tallies.astype(f32) / (count_scale * 128)
    own_a = delta_a.reshape(RANKS, FULL_A)
    own_b = delta_b.reshape(FULL_B, RANKS).T
    mate_a, mate_b, mate_w = mate(own_a), mate(own_b), mate(weights)
    pb, mb, vb = pb.T, mb.T, vb.T
    col_state = col_gather(jnp.concatenate([pb, mb, vb, pb], axis=0))
    pairs = pair_sum(weights, mate_w, own_a, mate_a, own_b, mate_b)
    got = exchange(pairs.reshape(CHIPS, 16, LANES), ("zl", "y"))
    got, col_state = lax.optimization_barrier((got, col_state))
    message = row_sum(got)
    codes, message = lax.optimization_barrier((codes, message))
    dec, *state = decode(codes, (pa, ma, va, pb, mb, vb))
    got = exchange(message, ("c",) + COL)
    pa_n, ma_n, va_n, pb_n, mb_n, vb_n, send, factor = server_step(
        got, col_state, state[:3], state[3:]
    )
    ranks = exchange(send, ROW)
    merged, peaks = merge(dec, scale.reshape(1, DEPTH), spread(factor), ranks)
    out, scales = normalise(merged, exchange(peaks, COL))
    return (out, scales.reshape(DEPTH), pb_n.T, pa_n, mb_n.T, vb_n.T, ma_n, va_n)


def solution(mesh):
    split = Mesh(mesh.devices.reshape(2, 4, 2, 4, 2), ROW + COL)
    tile, everyone = P(ROW, COL), P(ROW + COL, None, None)
    return jax.shard_map(
        local,
        mesh=split,
        in_specs=(tile, P(ROW)) + (tile,) * 6 + (everyone, everyone, P(ROW + COL, None)),
        out_specs=(tile, P(ROW)) + (tile,) * 6,
        check_vma=False,
    )
```

time: 160 us -> 96 us (0.60)
  blocking collectives: 57.6 us -> 15.2 us
  matrix products: 35 us -> 0 us
  other arithmetic: 27.7 us -> 0.67 us
  Pallas kernels: 0 us -> 27 us
  starting transfers between devices: 7.04 us -> 31.9 us
  local copies, waits for them, and re-layouts: 19.8 us -> 0.08 us
  waiting for transfers between devices: 11.1 us -> 19.8 us
    all_to_all x3 -> x1, blocking collectives: 57.6 us -> 15.2 us  [local(): out, scales = normalise(merged, exchange(peaks, COL))]
    dot_general x1 -> x0, matrix products: 35 us -> none  [local(): jnp.dot(thin_up_matrix, lowrank_a, preferred_element_type=jnp.float32)]
    pallas_call x0 -> x7, Pallas kernels: none -> 27 us  [the longest x1 11.6 us: decode(): pl.pallas_call(decode_kernel, out_shape=(pltpu.HBM((DEPTH, WIDTH), bf16),...]
    all_to_all x2 -> x3, starting transfers between devices: 7.04 us -> 22.9 us  [the longest x1 9.31 us: local(): got = exchange(message, ('c',) + COL)]
    convert_element_type x5 -> x0, other arithmetic: 15 us -> none  [the longest x1 9.61 us: local(): (merged_weight / peak[:, None]).astype(jnp.bfloat16)]
    unnamed x21 -> x8, local copies, waits for them, and re-layouts: 14.3 us -> 0.03 us
    ppermute x0 -> x6, waiting for transfers between devices: none -> 12.2 us  [the longest x3 9.26 us: col_gather(): other = lax.ppermute(block, axis, perm)]
    ppermute x0 -> x6, starting transfers between devices: none -> 8.98 us  [the longest x3 8.31 us: col_gather(): other = lax.ppermute(block, axis, perm)]
  transfers between devices with their start and end apart: 2 -> 9, of which waited for: 2 -> 6; matrix products, arithmetic and copies ran while one was open for 2% -> 1% of each run, Pallas kernels for 0% -> 12%
where the time goes in v1:
time: 96 us; the launch traced here: 95.4 us
  starting transfers between devices  31.9 us (33%)
  Pallas kernels  27 us (28%)
  waiting for transfers between devices  19.8 us (21%)
  blocking collectives  15.2 us (16%)
    all_to_all x1, blocking collectives, local(): out, scales = normalise(merged, exchange(peaks, COL))  15.2 us
    pallas_call x1, Pallas kernels, decode(): pl.pallas_call(decode_kernel, out_shape=(pltpu.HBM((DEPTH, WIDTH), bf16),...  11.6 us
    all_to_all x1, starting transfers between devices, local(): got = exchange(message, ('c',) + COL)  9.31 us
    ppermute x3, waiting for transfers between devices, col_gather(): other = lax.ppermute(block, axis, perm)  9.26 us
    ppermute x3, starting transfers between devices, col_gather(): other = lax.ppermute(block, axis, perm)  8.31 us
    all_to_all x1, starting transfers between devices, local(): ranks = exchange(send, ROW)  7.64 us
    all_to_all x1, waiting for transfers between devices, local(): ranks = exchange(send, ROW)  7.6 us
    all_to_all x1, starting transfers between devices, local(): got = exchange(pairs.reshape(CHIPS, 16, LANES), ('zl', 'y'))  5.92 us
  transfers between devices with their start and end apart: 9, of which 6 were waited for; matrix products, arithmetic and copies ran while one was open for 1% of the time, Pallas kernels for 12%

profile of v1, /device:TPU:0, one launch (start us, length us, event | category | flops | bytes accessed | tf_op | source)
XLA Modules:
  0.0 95.4 jit_solution(825286073106246042)
XLA Ops:
  0.6 0.0 copy-start.3
  0.6 0.0 copy-start.2
  0.7 0.0 copy-start.1
  0.7 0.1 collective-permute-start.1
  0.8 0.5 collective-permute-start.2
  1.3 0.7 convert_multiply_fusion.own_w
  1.9 0.1 collective-permute-start
  2.0 2.3 %collective-permute-done.mate_w = f32[1,2]{1,0:T(1,128)S(1)} collective-permute-done((f32[1,2]{1,0:T(1,128)S(1)}, f32[1,2]{1,0:T(1,128)S(1)}, u32[]{:S(2)}, u32[]{:S(2)}) %collective-permute-start) | collective-permute-done | bytes 40 | tf_op jit(solution)/shard_map/ppermute | solution.py:447
  4.3 0.6 collective-permute-done.2.mate_b
  4.9 0.0 collective-permute-done.1.mate_a
  4.9 3.7 %pair_sum.1 = bf16[128,3840]{1,0:T(8,128)(2,1)} custom-call(f32[1,2]{1,0:T(1,128)S(1)} %convert_multiply_fusion.own_w, f32[1,2]{1,0:T(1,128)S(1)} %collective-permute-done.mate_w, bf16[16,53248]{1,0:T(8,128)(2,1)} %bitcast.15, bf16[16,53248]{1,0:T(8,128)(2,1)S(1)} %collective-permute-done.1.mate_a, bf16[16,8192]{1,0:T(8,128)(2,1)} %bitcast.17, ...), custom_call_target="tpu_custom_call" | custom-call | tf_op jit(solution)/shard_map/pair_sum/pallas_call | solution.py:199
  8.7 5.9 %all-to-all-start = ((bf16[8,16,3840]{2,1,0:T(8,128)(2,1)}), bf16[8,16,3840]{2,1,0:T(8,128)(2,1)S(1)}, u32[]{:S(2)}, u32[]{:S(2)}) async-start(bf16[8,16,3840]{2,1,0:T(8,128)(2,1)} %bitcast.4), calls=%async_computation | async-start | bytes 1966080 | tf_op jit(solution)/shard_map/all_to_all | solution.py:451
  14.6 0.0 copy-done.3
  14.7 3.7 %collective-permute-start.3 = (f32[8,512]{1,0:T(8,128)S(1)}, f32[8,512]{1,0:T(8,128)S(1)}, u32[]{:S(2)}, u32[]{:S(2)}) collective-permute-start(f32[8,512]{1,0:T(8,128)S(1)} %pad_maximum_fusion), channel_id=1, source_target_pairs={{0,1},{1,0},{2,3},{3,2},{4,5},{5,4},{6,7},{7,6},{8,9},{9,8},{10,11... | collective-permute-start | bytes 49160 | tf_op jit(solution)/shard_map/ppermute | solution.py:251
  18.3 4.1 %collective-permute-done.3 = f32[8,512]{1,0:T(8,128)S(1)} collective-permute-done((f32[8,512]{1,0:T(8,128)S(1)}, f32[8,512]{1,0:T(8,128)S(1)}, u32[]{:S(2)}, u32[]{:S(2)}) %collective-permute-start.3) | collective-permute-done | bytes 16416 | tf_op jit(solution)/shard_map/ppermute | solution.py:251
  22.4 3.1 %collective-permute-start.4 = (f32[16,512]{1,0:T(8,128)S(1)}, f32[16,512]{1,0:T(8,128)S(1)}, u32[]{:S(2)}, u32[]{:S(2)}) collective-permute-start(f32[16,512]{1,0:T(8,128)S(1)} %concatenate.12), channel_id=1, source_target_pairs={{0,4},{2,6},{4,0},{6,2},{1,5},{3,7},{5,1},{7,3},{8,12},{10,14},{12... | collective-permute-start | bytes 98312 | tf_op jit(solution)/shard_map/ppermute | solution.py:251
  25.5 2.4 %collective-permute-done.4 = f32[16,512]{1,0:T(8,128)S(1)} collective-permute-done((f32[16,512]{1,0:T(8,128)S(1)}, f32[16,512]{1,0:T(8,128)S(1)}, u32[]{:S(2)}, u32[]{:S(2)}) %collective-permute-start.4) | collective-permute-done | bytes 32800 | tf_op jit(solution)/shard_map/ppermute | solution.py:251
  27.9 1.6 %collective-permute-start.5 = (f32[32,512]{1,0:T(8,128)S(1)}, f32[32,512]{1,0:T(8,128)S(1)}, u32[]{:S(2)}, u32[]{:S(2)}) collective-permute-start(f32[32,512]{1,0:T(8,128)S(1)} %concatenate.13.state_0), channel_id=1, source_target_pairs={{0,2},{2,0},{4,6},{6,4},{1,3},{3,1},{5,7},{7,5},{8,10},{10,8},{12,... | collective-permute-start | bytes 196616 | tf_op jit(solution)/shard_map/ppermute | solution.py:251
  29.5 2.8 %collective-permute-done.5.state_1 = f32[32,512]{1,0:T(8,128)S(1)} collective-permute-done((f32[32,512]{1,0:T(8,128)S(1)}, f32[32,512]{1,0:T(8,128)S(1)}, u32[]{:S(2)}, u32[]{:S(2)}) %collective-permute-start.5) | collective-permute-done | bytes 65568 | tf_op jit(solution)/shard_map/ppermute | solution.py:251
  32.3 0.0 all-to-all-done.got
  32.3 0.9 row_sum.1
  33.2 9.3 %all-to-all-start.1 = ((bf16[16,16,512]{2,1,0:T(8,128)(2,1)}), bf16[16,16,512]{2,1,0:T(8,128)(2,1)S(1)}, u32[]{:S(2)}, u32[]{:S(2)}) async-start(bf16[16,16,512]{2,1,0:T(8,128)(2,1)} %row_sum.1), calls=%async_computation.1 | async-start | bytes 524288 | tf_op jit(solution)/shard_map/all_to_all | solution.py:456
  42.6 0.0 copy-start
  42.6 11.6 %decode.1 = (bf16[512,6656]{1,0:T(8,128)(2,1)}, f32[1,6656]{1,0:T(1,128)S(1)}, f32[1,6656]{1,0:T(1,128)S(1)}, f32[1,6656]{1,0:T(1,128)S(1)}, f32[2,512]{1,0:T(2,...) custom-call(s32[512,6656]{1,0:T(8,128)} %refs_0_, f32[1,6656]{1,0:T(1,128)} %refs_1_.1, f32[1,6656]{1,0:T(1,128)} %refs_2_.1, ...), custom_call_target="tpu_custom_call" | custom-call | flops 40000000 | bytes 24000000 | tf_op jit(solution)/shard_map/decode/pallas_call | solution.py:130
  54.2 0.0 all-to-all-done.1.got
  54.2 0.9 server_step.1
  55.0 7.6 %all-to-all-start.2 = ((bf16[16,16,512]{2,1,0:T(8,128)(2,1)}), bf16[16,16,512]{2,1,0:T(8,128)(2,1)S(1)}, u32[]{:S(2)}, u32[]{:S(2)}) async-start(bf16[16,16,512]{2,1,0:T(8,128)(2,1)} %get-tuple-element.45), calls=%async_computation.2 | async-start | bytes 524288 | tf_op jit(solution)/shard_map/all_to_all | solution.py:460
  62.7 0.3 spread.1.wide
  63.0 7.6 %all-to-all-done.2.ranks = bf16[16,16,512]{2,1,0:T(8,128)(2,1)S(1)} async-done(((bf16[16,16,512]{2,1,0:T(8,128)(2,1)}), bf16[16,16,512]{2,1,0:T(8,128)(2,1)S(1)}, u32[]{:S(2)}, u32[]{:S(2)}) %all-to-all-start.2) | async-done | bytes 262176 | tf_op jit(solution)/shard_map/all_to_all | solution.py:460
  70.6 5.2 %merge.1 = (f32[13,512,512]{2,1,0:T(8,128)S(1)}, f32[8,1,512]{2,1,0:T(1,128)S(1)}) custom-call(bf16[512,6656]{1,0:T(8,128)(2,1)} %get-tuple-element.34.dec, f32[1,512]{1,0:T(1,128)S(1)} %bitcast.13, bf16[512,256]{1,0:T(8,128)(2,1)S(1)} %spread.1.wide, bf16[16,16,512]{2,1,0:T(8,128)(2,1)S(1)} %all-to-all-done.2.ranks), custom_call_target="tpu_custom_call" | custom-call | tf_op jit(solution)/shard_map/merge/pallas_call | solution.py:368
  75.8 15.2 %all_to_all.20.peaks = f32[8,1,512]{2,1,0:T(1,128)S(1)} all-to-all(f32[8,1,512]{2,1,0:T(1,128)S(1)} %get-tuple-element.47), channel_id=1, replica_groups=mesh['zl'=2,'y'=4,'c'=2,'x'=4,'zh'=2] {'x','zh'}, dimensions={0} | all-to-all | bytes 32768 | tf_op jit(solution)/shard_map/all_to_all | solution.py:462
  91.0 4.4 %normalise.1 = (bf16[512,6656]{1,0:T(8,128)(2,1)}, f32[1,512]{1,0:T(1,128)}) custom-call(f32[13,512,512]{2,1,0:T(8,128)S(1)} %get-tuple-element.46.merged, f32[8,1,512]{2,1,0:T(1,128)S(1)} %all_to_all.20.peaks), custom_call_target="tpu_custom_call" | custom-call | tf_op jit(solution)/shard_map/normalise/pallas_call | solution.py:426
  (6 shorter events, 0.1 us)
Async XLA Ops:
  0.6 14.0 %copy-start.3 = (f32[512,2]{0,1:T(2,128)S(1)}, f32[512,2]{0,1:T(2,128)}, u32[]{:S(2)}) copy-start(f32[512,2]{0,1:T(2,128)} %param.16) | copy-start | bytes 12292
  0.6 14.0 %copy-start.2 = (f32[512,2]{0,1:T(2,128)S(1)}, f32[512,2]{0,1:T(2,128)}, u32[]{:S(2)}) copy-start(f32[512,2]{0,1:T(2,128)} %param.15) | copy-start | bytes 12292
  0.7 14.0 %copy-start.1 = (f32[512,2]{0,1:T(2,128)S(1)}, f32[512,2]{0,1:T(2,128)}, u32[]{:S(2)}) copy-start(f32[512,2]{0,1:T(2,128)} %param.13) | copy-start | bytes 12292
  0.7 4.3 %collective-permute-start.1 = (bf16[16,53248]{1,0:T(8,128)(2,1)}, bf16[16,53248]{1,0:T(8,128)(2,1)S(1)}, u32[]{:S(2)}, u32[]{:S(2)}) collective-permute-start(bf16[16,53248]{1,0:T(8,128)(2,1)} %bitcast.14), channel_id=1, source_target_pairs={{0,8},{8,0},{1,9},{9,1},{2,10},{10,2},{3,11},{11,3},{4,12},{12,4},... | collective-permute-start | bytes 5111816 | tf_op jit(solution)/shard_map/ppermute | solution.py:447
  0.8 4.2 %collective-permute-start.2 = (bf16[16,8192]{1,0:T(8,128)(2,1)}, bf16[16,8192]{1,0:T(8,128)(2,1)S(1)}, u32[]{:S(2)}, u32[]{:S(2)}) collective-permute-start(bf16[16,8192]{1,0:T(8,128)(2,1)} %bitcast.16), channel_id=1, source_target_pairs={{0,8},{8,0},{1,9},{9,1},{2,10},{10,2},{3,11},{11,3},{4,12},{12,4},... | collective-permute-start | bytes 786440 | tf_op jit(solution)/shard_map/ppermute | solution.py:447
  1.9 2.4 %collective-permute-start = (f32[1,2]{1,0:T(1,128)S(1)}, f32[1,2]{1,0:T(1,128)S(1)}, u32[]{:S(2)}, u32[]{:S(2)}) collective-permute-start(f32[1,2]{1,0:T(1,128)S(1)} %convert_multiply_fusion.own_w), channel_id=1, source_target_pairs={{0,8},{8,0},{1,9},{9,1},{2,10},{10,2},{3,11},{11,3},{4,12},{12,4},... | collective-permute-start | bytes 32 | tf_op jit(solution)/shard_map/ppermute | solution.py:447
  8.7 23.6 %all-to-all-start = ((bf16[8,16,3840]{2,1,0:T(8,128)(2,1)}), bf16[8,16,3840]{2,1,0:T(8,128)(2,1)S(1)}, u32[]{:S(2)}, u32[]{:S(2)}) async-start(bf16[8,16,3840]{2,1,0:T(8,128)(2,1)} %bitcast.4), calls=%async_computation | async-start | bytes 1966080 | tf_op jit(solution)/shard_map/all_to_all | solution.py:451
  14.7 7.7 %collective-permute-start.3 = (f32[8,512]{1,0:T(8,128)S(1)}, f32[8,512]{1,0:T(8,128)S(1)}, u32[]{:S(2)}, u32[]{:S(2)}) collective-permute-start(f32[8,512]{1,0:T(8,128)S(1)} %pad_maximum_fusion), channel_id=1, source_target_pairs={{0,1},{1,0},{2,3},{3,2},{4,5},{5,4},{6,7},{7,6},{8,9},{9,8},{10,11... | collective-permute-start | bytes 49160 | tf_op jit(solution)/shard_map/ppermute | solution.py:251
  22.4 5.5 %collective-permute-start.4 = (f32[16,512]{1,0:T(8,128)S(1)}, f32[16,512]{1,0:T(8,128)S(1)}, u32[]{:S(2)}, u32[]{:S(2)}) collective-permute-start(f32[16,512]{1,0:T(8,128)S(1)} %concatenate.12), channel_id=1, source_target_pairs={{0,4},{2,6},{4,0},{6,2},{1,5},{3,7},{5,1},{7,3},{8,12},{10,14},{12... | collective-permute-start | bytes 98312 | tf_op jit(solution)/shard_map/ppermute | solution.py:251
  27.9 4.3 %collective-permute-start.5 = (f32[32,512]{1,0:T(8,128)S(1)}, f32[32,512]{1,0:T(8,128)S(1)}, u32[]{:S(2)}, u32[]{:S(2)}) collective-permute-start(f32[32,512]{1,0:T(8,128)S(1)} %concatenate.13.state_0), channel_id=1, source_target_pairs={{0,2},{2,0},{4,6},{6,4},{1,3},{3,1},{5,7},{7,5},{8,10},{10,8},{12,... | collective-permute-start | bytes 196616 | tf_op jit(solution)/shard_map/ppermute | solution.py:251
  33.2 20.9 %all-to-all-start.1 = ((bf16[16,16,512]{2,1,0:T(8,128)(2,1)}), bf16[16,16,512]{2,1,0:T(8,128)(2,1)S(1)}, u32[]{:S(2)}, u32[]{:S(2)}) async-start(bf16[16,16,512]{2,1,0:T(8,128)(2,1)} %row_sum.1), calls=%async_computation.1 | async-start | bytes 524288 | tf_op jit(solution)/shard_map/all_to_all | solution.py:456
  42.6 28.0 %copy-start = (f32[512]{0:T(512)S(1)}, f32[512]{0:T(512)}, u32[]{:S(2)}) copy-start(f32[512]{0:T(512)} %param.12) | copy-start | bytes 6148
  55.0 15.5 %all-to-all-start.2 = ((bf16[16,16,512]{2,1,0:T(8,128)(2,1)}), bf16[16,16,512]{2,1,0:T(8,128)(2,1)S(1)}, u32[]{:S(2)}, u32[]{:S(2)}) async-start(bf16[16,16,512]{2,1,0:T(8,128)(2,1)} %get-tuple-element.45), calls=%async_computation.2 | async-start | bytes 524288 | tf_op jit(solution)/shard_map/all_to_all | solution.py:460

commit v2 on v1

--- a/solution.py
+++ b/solution.py
@@ -67,19 +67,22 @@
 
 DEC_ROWS = 32
 SLOTS = 3
-
-
-def decode_kernel(*refs):
-    codes, state = refs[0], refs[1:7]
-    out, kept = refs[7], refs[8:14]
-    buf, done, sems, out_sems, state_sems = refs[14:]
-    steps = DEPTH // DEC_ROWS
+PART = DEPTH // 2
+
+
+def decode_kernel(first, count, *refs):
+    codes, state = refs[0], refs[1 : 1 + count]
+    out, kept = refs[1 + count], refs[2 + count : 2 + 2 * count]
+    buf, done, sems, out_sems, state_sems = refs[2 + 2 * count :]
+    steps = PART // DEC_ROWS
 
     def rows(step):
         return pl.ds(pl.multiple_of(step * DEC_ROWS, DEC_ROWS), DEC_ROWS)
 
     def fetch(step, slot):
-        return pltpu.make_async_copy(codes.at[rows(step), :], buf.at[slot], sems.at[slot])
+        return pltpu.make_async_copy(
+            codes.at[rows(step + first // DEC_ROWS), :], buf.at[slot], sems.at[slot]
+        )
 
     def store(step, slot):
         return pltpu.make_async_copy(done.at[slot], out.at[rows(step), :], out_sems.at[slot])
@@ -126,12 +129,13 @@
         move.wait()
 
 
-def decode(codes, state):
-    return pl.pallas_call(
-        decode_kernel,
-        out_shape=(pltpu.HBM((DEPTH, WIDTH), bf16),) + tuple(pltpu.VMEM(x.shape, f32) for x in state),
-        in_specs=[in_hbm()] * 7,
-        out_specs=(in_hbm(),) + (in_vmem(),) * 6,
+def decode(codes, first, state=()):
+    count = len(state)
+    return pl.pallas_call(
+        functools.partial(decode_kernel, first, count),
+        out_shape=(pltpu.HBM((PART, WIDTH), bf16),) + tuple(pltpu.VMEM(x.shape, f32) for x in state),
+        in_specs=[in_hbm()] * (1 + count),
+        out_specs=(in_hbm(),) + (in_vmem(),) * count,
         scratch_shapes=[
             pltpu.VMEM((SLOTS, DEC_ROWS, WIDTH), i32),
             pltpu.VMEM((SLOTS, DEC_ROWS, WIDTH), bf16),
@@ -140,7 +144,7 @@
             pltpu.SemaphoreType.DMA((6,)),
         ],
         compiler_params=params_for(8),
-        cost_estimate=pl.CostEstimate(flops=40_000_000, transcendentals=0, bytes_accessed=24_000_000),
+        cost_estimate=pl.CostEstimate(flops=20_000_000, transcendentals=0, bytes_accessed=12_000_000),
         name="decode",
     )(stay(codes), *[stay(x) for x in state])
 
@@ -242,13 +246,9 @@
 APART = (0, 1, 4, 5, 2, 3, 6, 7)
 
 
-def col_gather(block):
-    for axis, perm in (
-        ("zh", [(0, 1), (1, 0)]),
-        ("x", [(0, 2), (1, 3), (2, 0), (3, 1)]),
-        ("x", [(0, 1), (1, 0), (2, 3), (3, 2)]),
-    ):
-        other = lax.ppermute(block, axis, perm)
+def x_gather(block):
+    for perm in ([(0, 2), (1, 3), (2, 0), (3, 1)], [(0, 1), (1, 0), (2, 3), (3, 2)]):
+        other = lax.ppermute(block, "x", perm)
         last, block = block, jnp.concatenate([block, other], axis=0)
     return last, other
 
@@ -334,19 +334,25 @@
 BLOCK = 512
 
 
-def merge_kernel(dec, scale, wide, ranks, merged, peaks, buf, row_scale, tops, sems):
+def merge_kernel(dec_top, dec_low, scale, wide, ranks, merged, peaks, buf, row_scale, tops, sems):
     fetches = []
     for i in range(PIECES):
+        here = pl.ds(i * PIECE, PIECE)
         fetches.append(
-            pltpu.make_async_copy(dec.at[:, pl.ds(i * PIECE, PIECE)], buf.at[i], sems.at[i])
+            [
+                pltpu.make_async_copy(dec.at[:, here], buf.at[i, pl.ds(q * PART, PART), :], sems.at[i, q])
+                for q, dec in enumerate((dec_top, dec_low))
+            ]
         )
-        fetches[-1].start()
+        for fetch in fetches[-1]:
+            fetch.start()
     row_scale[...] = jnp.transpose(jnp.broadcast_to(scale[...] * 2.0**-10, (128, DEPTH)))
     lane = jnp.bitwise_and(lax.broadcasted_iota(i32, (BLOCK, 256), 1), 15)
     right = ranks[...].reshape(256, PIECE)
     tops[...] = jnp.zeros_like(tops)
     for i in range(PIECES):
-        fetches[i].wait()
+        for fetch in fetches[i]:
+            fetch.wait()
         for b in range(DEPTH // BLOCK):
             at = pl.ds(b * BLOCK, BLOCK)
             left = wide[at, :]
@@ -364,21 +370,21 @@
         peaks[c] = peak
 
 
-def merge(dec, scale, wide, ranks):
+def merge(decs, scale, wide, ranks):
     return pl.pallas_call(
         merge_kernel,
         out_shape=(pltpu.VMEM((PIECES, DEPTH, PIECE), f32), SDS((COLS, 1, DEPTH), f32)),
-        in_specs=[in_hbm()] + [in_vmem()] * 3,
+        in_specs=[in_hbm()] * 2 + [in_vmem()] * 3,
         out_specs=(in_vmem(), in_vmem()),
         scratch_shapes=[
             pltpu.VMEM((PIECES, DEPTH, PIECE), bf16),
             pltpu.VMEM((DEPTH, 128), f32),
             pltpu.VMEM((DEPTH, 128), f32),
-            pltpu.SemaphoreType.DMA((PIECES,)),
+            pltpu.SemaphoreType.DMA((PIECES, 2)),
         ],
         compiler_params=params_for(16),
         name="merge",
-    )(stay(dec), scale, wide, ranks)
+    )(*map(stay, decs), scale, wide, ranks)
 
 
 OUT_ROWS = 32
@@ -446,19 +452,24 @@
     own_b = delta_b.reshape(FULL_B, RANKS).T
     mate_a, mate_b, mate_w = mate(own_a), mate(own_b), mate(weights)
     pb, mb, vb = pb.T, mb.T, vb.T
-    col_state = col_gather(jnp.concatenate([pb, mb, vb, pb], axis=0))
+    block = jnp.concatenate([pb, mb, vb, pb], axis=0)
+    other = lax.ppermute(block, "zh", [(0, 1), (1, 0)])
     pairs = pair_sum(weights, mate_w, own_a, mate_a, own_b, mate_b)
+    pairs, codes, block, other = lax.optimization_barrier((pairs, codes, block, other))
     got = exchange(pairs.reshape(CHIPS, 16, LANES), ("zl", "y"))
-    got, col_state = lax.optimization_barrier((got, col_state))
+    col_state = x_gather(jnp.concatenate([block, other], axis=0))
+    (top,) = decode(codes, 0)
+    got, col_state, top = lax.optimization_barrier((got, col_state, top))
     message = row_sum(got)
     codes, message = lax.optimization_barrier((codes, message))
-    dec, *state = decode(codes, (pa, ma, va, pb, mb, vb))
     got = exchange(message, ("c",) + COL)
+    low, *state = decode(codes, PART, (pa, ma, va, pb, mb, vb))
+    got, low, state = lax.optimization_barrier((got, low, state))
     pa_n, ma_n, va_n, pb_n, mb_n, vb_n, send, factor = server_step(
         got, col_state, state[:3], state[3:]
     )
     ranks = exchange(send, ROW)
-    merged, peaks = merge(dec, scale.reshape(1, DEPTH), spread(factor), ranks)
+    merged, peaks = merge((top, low), scale.reshape(1, DEPTH), spread(factor), ranks)
     out, scales = normalise(merged, exchange(peaks, COL))
     return (out, scales.reshape(DEPTH), pb_n.T, pa_n, mb_n.T, vb_n.T, ma_n, va_n)
 

time: 96 us -> 82.6 us (0.86)
  starting transfers between devices: 31.9 us -> 23.1 us
  waiting for transfers between devices: 19.8 us -> 15.7 us
  blocking collectives: 15.2 us -> 12 us
  Pallas kernels: 27 us -> 28.9 us
    ppermute x3, waiting for transfers between devices: 9.26 us -> 2.39 us  [the longest x2 2.39 us: x_gather(): other = lax.ppermute(block, 'x', perm)]
    all_to_all x1, starting transfers between devices: 7.64 us -> 3.53 us  [local(): ranks = exchange(send, ROW)]
    all_to_all x1, starting transfers between devices: 9.31 us -> 5.4 us  [local(): got = exchange(message, ('c',) + COL)]
    all_to_all x1, blocking collectives: 15.2 us -> 12 us  [local(): out, scales = normalise(merged, exchange(peaks, COL))]
    all_to_all x1, waiting for transfers between devices: 0.01 us -> 2.93 us  [local(): got = exchange(message, ('c',) + COL)]
    ppermute x3, waiting for transfers between devices: 2.92 us -> 1.12 us  [local(): mate_a, mate_b, mate_w = (mate(own_a), mate(own_b), mate(weights))]
    pallas_call x1 -> x2, Pallas kernels: 11.6 us -> 13.3 us  [decode(): pl.pallas_call(functools.partial(decode_kernel, first, count), out_shape=...]
    all_to_all x1, waiting for transfers between devices: 0.01 us -> 1.72 us  [local(): got = exchange(pairs.reshape(CHIPS, 16, LANES), ('zl', 'y'))]
  transfers between devices with their start and end apart: 9 -> 9, of which waited for: 6 -> 5; matrix products, arithmetic and copies ran while one was open for 1% -> 2% of each run, Pallas kernels for 12% -> 21%
where the time goes in v2:
time: 82.6 us; the launch traced here: 81.9 us
  Pallas kernels  28.9 us (35%)
  starting transfers between devices  23.1 us (28%)
  waiting for transfers between devices  15.7 us (19%)
  blocking collectives  12 us (15%)
  other arithmetic  1.44 us (2%)
    pallas_call x2, Pallas kernels, decode(): pl.pallas_call(functools.partial(decode_kernel, first, count), out_shape=...  13.3 us
    all_to_all x1, blocking collectives, local(): out, scales = normalise(merged, exchange(peaks, COL))  12 us
    all_to_all x1, waiting for transfers between devices, local(): ranks = exchange(send, ROW)  7.56 us
    all_to_all x1, starting transfers between devices, local(): got = exchange(message, ('c',) + COL)  5.4 us
    pallas_call x1, Pallas kernels, merge(): pl.pallas_call(merge_kernel, out_shape=(pltpu.VMEM((PIECES, DEPTH, PIECE)...  5.38 us
    all_to_all x1, starting transfers between devices, local(): got = exchange(pairs.reshape(CHIPS, 16, LANES), ('zl', 'y'))  4.93 us
    ppermute x2, starting transfers between devices, x_gather(): other = lax.ppermute(block, 'x', perm)  4.6 us
    pallas_call x1, Pallas kernels, normalise(): pl.pallas_call(normalise_kernel, out_shape=(SDS((DEPTH, WIDTH), bf16), SD...  4.39 us
  transfers between devices with their start and end apart: 9, of which 5 were waited for; matrix products, arithmetic and copies ran while one was open for 2% of the time, Pallas kernels for 21%

profile of v2, /device:TPU:0, one launch (start us, length us, event | category | flops | bytes accessed | tf_op | source)
XLA Modules:
  0.0 81.9 jit_solution(4461343810941553004)
XLA Ops:
  0.6 0.1 collective-permute-start.1
  0.7 0.5 collective-permute-start.2
  1.2 0.8 pad_maximum_fusion.1
  2.0 4.0 %collective-permute-start.3 = (f32[8,512]{1,0:T(8,128)S(1)}, f32[8,512]{1,0:T(8,128)S(1)}, u32[]{:S(2)}, u32[]{:S(2)}) collective-permute-start(f32[8,512]{1,0:T(8,128)S(1)} %pad_maximum_fusion.1), channel_id=1, source_target_pairs={{0,1},{1,0},{2,3},{3,2},{4,5},{5,4},{6,7},{7,6},{8,9},{9,8},{10,11... | collective-permute-start | bytes 49160 | tf_op jit(solution)/shard_map/ppermute | solution.py:456
  6.0 0.7 convert_multiply_fusion.own_w
  6.7 0.0 collective-permute-start
  6.7 1.1 %collective-permute-done.mate_w = f32[1,2]{1,0:T(1,128)S(1)} collective-permute-done((f32[1,2]{1,0:T(1,128)S(1)}, f32[1,2]{1,0:T(1,128)S(1)}, u32[]{:S(2)}, u32[]{:S(2)}) %collective-permute-start) | collective-permute-done | bytes 40 | tf_op jit(solution)/shard_map/ppermute | solution.py:453
  7.8 0.0 collective-permute-done.2.mate_b
  7.8 0.0 collective-permute-done.1.mate_a
  7.8 3.8 %pair_sum.1 = bf16[128,3840]{1,0:T(8,128)(2,1)} custom-call(f32[1,2]{1,0:T(1,128)S(1)} %convert_multiply_fusion.own_w, f32[1,2]{1,0:T(1,128)S(1)} %collective-permute-done.mate_w, bf16[16,53248]{1,0:T(8,128)(2,1)} %bitcast.15, bf16[16,53248]{1,0:T(8,128)(2,1)S(1)} %collective-permute-done.1.mate_a, bf16[16,8192]{1,0:T(8,128)(2,1)} %bitcast.17, ...), custom_call_target="tpu_custom_call" | custom-call | tf_op jit(solution)/shard_map/pair_sum/pallas_call | solution.py:203
  11.6 0.0 collective-permute-done.3
  11.6 4.9 %all-to-all-start = ((bf16[8,16,3840]{2,1,0:T(8,128)(2,1)}), bf16[8,16,3840]{2,1,0:T(8,128)(2,1)S(1)}, u32[]{:S(2)}, u32[]{:S(2)}) async-start(bf16[8,16,3840]{2,1,0:T(8,128)(2,1)} %bitcast.7), calls=%async_computation | async-start | bytes 1966080 | tf_op jit(solution)/shard_map/all_to_all | solution.py:459
  16.5 3.1 %collective-permute-start.4 = (f32[16,512]{1,0:T(8,128)S(1)}, f32[16,512]{1,0:T(8,128)S(1)}, u32[]{:S(2)}, u32[]{:S(2)}) collective-permute-start(f32[16,512]{1,0:T(8,128)S(1)} %pad_maximum_fusion), channel_id=1, source_target_pairs={{0,4},{2,6},{4,0},{6,2},{1,5},{3,7},{5,1},{7,3},{8,12},{10,14},{12... | collective-permute-start | bytes 98312 | tf_op jit(solution)/shard_map/ppermute | solution.py:251
  19.7 2.4 %collective-permute-done.4 = f32[16,512]{1,0:T(8,128)S(1)} collective-permute-done((f32[16,512]{1,0:T(8,128)S(1)}, f32[16,512]{1,0:T(8,128)S(1)}, u32[]{:S(2)}, u32[]{:S(2)}) %collective-permute-start.4) | collective-permute-done | bytes 32800 | tf_op jit(solution)/shard_map/ppermute | solution.py:251
  22.1 1.5 %collective-permute-start.5 = (f32[32,512]{1,0:T(8,128)S(1)}, f32[32,512]{1,0:T(8,128)S(1)}, u32[]{:S(2)}, u32[]{:S(2)}) collective-permute-start(f32[32,512]{1,0:T(8,128)S(1)} %constant_dynamic-update-slice_fusion.state_0), channel_id=1, source_target_pairs={{0,2},{2,0},{4,6},{6,4},{1,3},{3,1},{5,7},{7,5},{8,10},{10,8},{12,... | collective-permute-start | bytes 196616 | tf_op jit(solution)/shard_map/ppermute | solution.py:251
  23.5 6.6 %decode.2.dec_top = bf16[256,6656]{1,0:T(8,128)(2,1)} custom-call(s32[512,6656]{1,0:T(8,128)} %refs_0_.1), custom_call_target="tpu_custom_call" | custom-call | flops 20000000 | bytes 12000000 | tf_op jit(solution)/shard_map/decode/pallas_call | solution.py:134
  30.2 0.0 collective-permute-done.5.state_1
  30.2 1.7 %all-to-all-done.got = bf16[8,16,3840]{2,1,0:T(8,128)(2,1)S(1)} async-done(((bf16[8,16,3840]{2,1,0:T(8,128)(2,1)}), bf16[8,16,3840]{2,1,0:T(8,128)(2,1)S(1)}, u32[]{:S(2)}, u32[]{:S(2)}) %all-to-all-start) | async-done | bytes 983072 | tf_op jit(solution)/shard_map/all_to_all | solution.py:459
  31.9 0.9 %row_sum.1 = bf16[16,16,512]{2,1,0:T(8,128)(2,1)} custom-call(bf16[8,16,3840]{2,1,0:T(8,128)(2,1)S(1)} %all-to-all-done.got), custom_call_target="tpu_custom_call" | custom-call | tf_op jit(solution)/shard_map/row_sum/pallas_call | solution.py:235
  32.9 5.4 %all-to-all-start.1 = ((bf16[16,16,512]{2,1,0:T(8,128)(2,1)}), bf16[16,16,512]{2,1,0:T(8,128)(2,1)S(1)}, u32[]{:S(2)}, u32[]{:S(2)}) async-start(bf16[16,16,512]{2,1,0:T(8,128)(2,1)} %row_sum.1), calls=%async_computation.1 | async-start | bytes 524288 | tf_op jit(solution)/shard_map/all_to_all | solution.py:465
  38.3 0.0 copy-start
  38.3 6.7 %decode.3 = (bf16[256,6656]{1,0:T(8,128)(2,1)}, f32[1,6656]{1,0:T(1,128)S(1)}, f32[1,6656]{1,0:T(1,128)S(1)}, f32[1,6656]{1,0:T(1,128)S(1)}, f32[2,512]{1,0:T(2,...) custom-call(s32[512,6656]{1,0:T(8,128)} %refs_0_.1, f32[1,6656]{1,0:T(1,128)} %refs_1_.1, f32[1,6656]{1,0:T(1,128)} %refs_2_.1, ...), custom_call_target="tpu_custom_call" | custom-call | flops 20000000 | bytes 12000000 | tf_op jit(solution)/shard_map/decode/pallas_call | solution.py:134
  45.0 2.9 %all-to-all-done.1.got = bf16[16,16,512]{2,1,0:T(8,128)(2,1)S(1)} async-done(((bf16[16,16,512]{2,1,0:T(8,128)(2,1)}), bf16[16,16,512]{2,1,0:T(8,128)(2,1)S(1)}, u32[]{:S(2)}, u32[]{:S(2)}) %all-to-all-start.1) | async-done | bytes 262176 | tf_op jit(solution)/shard_map/all_to_all | solution.py:465
  47.9 0.8 %server_step.1 = (f32[1,6656]{1,0:T(1,128)}, f32[1,6656]{1,0:T(1,128)}, f32[1,6656]{1,0:T(1,128)}, f32[2,512]{1,0:T(2,128)}, f32[2,512]{1,0:T(2,128)}, /*index=5...) custom-call(bf16[16,16,512]{2,1,0:T(8,128)(2,1)S(1)} %all-to-all-done.1.got, ...), custom_call_target="tpu_custom_call" | custom-call | tf_op jit(solution)/shard_map/server_step/pallas_call | solution.py:298
  48.8 3.5 %all-to-all-start.2 = ((bf16[16,16,512]{2,1,0:T(8,128)(2,1)}), bf16[16,16,512]{2,1,0:T(8,128)(2,1)S(1)}, u32[]{:S(2)}, u32[]{:S(2)}) async-start(bf16[16,16,512]{2,1,0:T(8,128)(2,1)} %get-tuple-element.71), calls=%async_computation.2 | async-start | bytes 524288 | tf_op jit(solution)/shard_map/all_to_all | solution.py:471
  52.3 0.3 spread.1.wide
  52.6 7.6 %all-to-all-done.2.ranks = bf16[16,16,512]{2,1,0:T(8,128)(2,1)S(1)} async-done(((bf16[16,16,512]{2,1,0:T(8,128)(2,1)}), bf16[16,16,512]{2,1,0:T(8,128)(2,1)S(1)}, u32[]{:S(2)}, u32[]{:S(2)}) %all-to-all-start.2) | async-done | bytes 262176 | tf_op jit(solution)/shard_map/all_to_all | solution.py:471
  60.2 0.0 copy-done
  60.2 5.4 %merge.1 = (f32[13,512,512]{2,1,0:T(8,128)S(1)}, f32[8,1,512]{2,1,0:T(1,128)S(1)}) custom-call(bf16[256,6656]{1,0:T(8,128)(2,1)} %decode.2.dec_top, bf16[256,6656]{1,0:T(8,128)(2,1)} %get-tuple-element.60.dec_low, f32[1,512]{1,0:T(1,128)S(1)} %bitcast.13, bf16[512,256]{1,0:T(8,128)(2,1)S(1)} %spread.1.wide, bf16[16,16,512]{2,1,0:T(8,128)(2,1)S(1)} %all-to-all-done.2.ranks), custom_call_target="tpu_custom_call" | custom-call | tf_op jit(solution)/shard_map/merge/pallas_call | solution.py:374
  65.6 12.0 %all_to_all.20.peaks = f32[8,1,512]{2,1,0:T(1,128)S(1)} all-to-all(f32[8,1,512]{2,1,0:T(1,128)S(1)} %get-tuple-element.73), channel_id=1, replica_groups=mesh['zl'=2,'y'=4,'c'=2,'x'=4,'zh'=2] {'x','zh'}, dimensions={0} | all-to-all | bytes 32768 | tf_op jit(solution)/shard_map/all_to_all | solution.py:473
  77.5 4.4 %normalise.1 = (bf16[512,6656]{1,0:T(8,128)(2,1)}, f32[1,512]{1,0:T(1,128)}) custom-call(f32[13,512,512]{2,1,0:T(8,128)S(1)} %get-tuple-element.72.merged, f32[8,1,512]{2,1,0:T(1,128)S(1)} %all_to_all.20.peaks), custom_call_target="tpu_custom_call" | custom-call | tf_op jit(solution)/shard_map/normalise/pallas_call | solution.py:432
  (4 shorter events, 0.0 us)
Async XLA Ops:
  0.6 7.2 %collective-permute-start.1 = (bf16[16,53248]{1,0:T(8,128)(2,1)}, bf16[16,53248]{1,0:T(8,128)(2,1)S(1)}, u32[]{:S(2)}, u32[]{:S(2)}) collective-permute-start(bf16[16,53248]{1,0:T(8,128)(2,1)} %bitcast.14), channel_id=1, source_target_pairs={{0,8},{8,0},{1,9},{9,1},{2,10},{10,2},{3,11},{11,3},{4,12},{12,4},... | collective-permute-start | bytes 5111816 | tf_op jit(solution)/shard_map/ppermute | solution.py:453
  0.7 7.1 %collective-permute-start.2 = (bf16[16,8192]{1,0:T(8,128)(2,1)}, bf16[16,8192]{1,0:T(8,128)(2,1)S(1)}, u32[]{:S(2)}, u32[]{:S(2)}) collective-permute-start(bf16[16,8192]{1,0:T(8,128)(2,1)} %bitcast.16), channel_id=1, source_target_pairs={{0,8},{8,0},{1,9},{9,1},{2,10},{10,2},{3,11},{11,3},{4,12},{12,4},... | collective-permute-start | bytes 786440 | tf_op jit(solution)/shard_map/ppermute | solution.py:453
  2.0 9.6 %collective-permute-start.3 = (f32[8,512]{1,0:T(8,128)S(1)}, f32[8,512]{1,0:T(8,128)S(1)}, u32[]{:S(2)}, u32[]{:S(2)}) collective-permute-start(f32[8,512]{1,0:T(8,128)S(1)} %pad_maximum_fusion.1), channel_id=1, source_target_pairs={{0,1},{1,0},{2,3},{3,2},{4,5},{5,4},{6,7},{7,6},{8,9},{9,8},{10,11... | collective-permute-start | bytes 49160 | tf_op jit(solution)/shard_map/ppermute | solution.py:456
  6.7 1.1 %collective-permute-start = (f32[1,2]{1,0:T(1,128)S(1)}, f32[1,2]{1,0:T(1,128)S(1)}, u32[]{:S(2)}, u32[]{:S(2)}) collective-permute-start(f32[1,2]{1,0:T(1,128)S(1)} %convert_multiply_fusion.own_w), channel_id=1, source_target_pairs={{0,8},{8,0},{1,9},{9,1},{2,10},{10,2},{3,11},{11,3},{4,12},{12,4},... | collective-permute-start | bytes 32 | tf_op jit(solution)/shard_map/ppermute | solution.py:453
  11.6 20.3 %all-to-all-start = ((bf16[8,16,3840]{2,1,0:T(8,128)(2,1)}), bf16[8,16,3840]{2,1,0:T(8,128)(2,1)S(1)}, u32[]{:S(2)}, u32[]{:S(2)}) async-start(bf16[8,16,3840]{2,1,0:T(8,128)(2,1)} %bitcast.7), calls=%async_computation | async-start | bytes 1966080 | tf_op jit(solution)/shard_map/all_to_all | solution.py:459
  16.5 5.5 %collective-permute-start.4 = (f32[16,512]{1,0:T(8,128)S(1)}, f32[16,512]{1,0:T(8,128)S(1)}, u32[]{:S(2)}, u32[]{:S(2)}) collective-permute-start(f32[16,512]{1,0:T(8,128)S(1)} %pad_maximum_fusion), channel_id=1, source_target_pairs={{0,4},{2,6},{4,0},{6,2},{1,5},{3,7},{5,1},{7,3},{8,12},{10,14},{12... | collective-permute-start | bytes 98312 | tf_op jit(solution)/shard_map/ppermute | solution.py:251
  22.1 8.1 %collective-permute-start.5 = (f32[32,512]{1,0:T(8,128)S(1)}, f32[32,512]{1,0:T(8,128)S(1)}, u32[]{:S(2)}, u32[]{:S(2)}) collective-permute-start(f32[32,512]{1,0:T(8,128)S(1)} %constant_dynamic-update-slice_fusion.state_0), channel_id=1, source_target_pairs={{0,2},{2,0},{4,6},{6,4},{1,3},{3,1},{5,7},{7,5},{8,10},{10,8},{12,... | collective-permute-start | bytes 196616 | tf_op jit(solution)/shard_map/ppermute | solution.py:251
  32.9 15.1 %all-to-all-start.1 = ((bf16[16,16,512]{2,1,0:T(8,128)(2,1)}), bf16[16,16,512]{2,1,0:T(8,128)(2,1)S(1)}, u32[]{:S(2)}, u32[]{:S(2)}) async-start(bf16[16,16,512]{2,1,0:T(8,128)(2,1)} %row_sum.1), calls=%async_computation.1 | async-start | bytes 524288 | tf_op jit(solution)/shard_map/all_to_all | solution.py:465
  38.3 21.9 %copy-start = (f32[512]{0:T(512)S(1)}, f32[512]{0:T(512)}, u32[]{:S(2)}) copy-start(f32[512]{0:T(512)} %param.12) | copy-start | bytes 6148
  48.8 11.4 %all-to-all-start.2 = ((bf16[16,16,512]{2,1,0:T(8,128)(2,1)}), bf16[16,16,512]{2,1,0:T(8,128)(2,1)S(1)}, u32[]{:S(2)}, u32[]{:S(2)}) async-start(bf16[16,16,512]{2,1,0:T(8,128)(2,1)} %get-tuple-element.71), calls=%async_computation.2 | async-start | bytes 524288 | tf_op jit(solution)/shard_map/all_to_all | solution.py:471

commit v3 on v2

v3 whole, which is shorter than its diff:
```python
import functools

import jax
import jax.numpy as jnp
from jax import lax
from jax.experimental import pallas as pl
from jax.experimental.pallas import tpu as pltpu
from jax.sharding import Mesh, PartitionSpec as P

first_decay = 0.9
second_decay = 0.99
server_rate = 0.1
adam_floor = 0.001
adapter_scale = 2.0
count_scale = 64.0
fp8_top = 448.0
peak_eps = 1e-06

f32, bf16, i32 = jnp.float32, jnp.bfloat16, jnp.int32
SDS = jax.ShapeDtypeStruct

ROW, COL = ("zl", "y", "c"), ("x", "zh")
CHIPS, COLS = 8, 8
RANKS = 16
DEPTH, WIDTH = 512, 6656
HALF = WIDTH // 2
FULL_B, FULL_A = DEPTH * 16, WIDTH * 8
LANES = HALF + DEPTH
PIECE = 512
PIECES = WIDTH // PIECE


def adaptive_update(param, moment, second, grad):
    moment_next = first_decay * moment + (1.0 - first_decay) * grad
    second_next = second_decay * second + (1.0 - second_decay) * grad * grad
    param_next = param - server_rate * moment_next / (jnp.sqrt(second_next) + adam_floor)
    return (param_next, moment_next, second_next)


def params_for(mib):
    return pltpu.CompilerParams(vmem_limit_bytes=mib << 20)


def in_hbm():
    return pl.BlockSpec(memory_space=pltpu.HBM)


def stay(x):
    return pltpu.with_memory_space_constraint(x, pltpu.HBM)


def near(x):
    return pltpu.with_memory_space_constraint(x, pltpu.VMEM)


def in_any():
    return pl.BlockSpec(memory_space=pl.ANY)


def kept(shape, kind=f32):
    return pltpu.VMEM(shape, kind)


def in_vmem():
    return pl.BlockSpec(memory_space=pltpu.VMEM)


def in_smem():
    return pl.BlockSpec(memory_space=pltpu.SMEM)


DEC_ROWS = 32
SLOTS = 6
TOP = 352


def decode_kernel(first, steps, count, *refs):
    codes, state = refs[0], refs[1 : 1 + count]
    out, held = refs[1 + count], refs[2 + count : 2 + 2 * count]
    buf, done, sems, out_sems, state_sems = refs[2 + 2 * count :]

    def rows(step):
        return pl.ds(pl.multiple_of(step * DEC_ROWS, DEC_ROWS), DEC_ROWS)

    def fetch(step, slot):
        return pltpu.make_async_copy(
            codes.at[rows(step + first // DEC_ROWS), :], buf.at[slot], sems.at[slot]
        )

    def store(step, slot):
        return pltpu.make_async_copy(done.at[slot], out.at[rows(step), :], out_sems.at[slot])

    for s in range(min(SLOTS - 1, steps)):
        fetch(s, s).start()
    moves = [pltpu.make_async_copy(a, b, state_sems.at[q]) for q, (a, b) in enumerate(zip(state, held))]
    for move in moves:
        move.start()

    def step(s, carry):
        slot = lax.rem(s, SLOTS)
        fetch(s, slot).wait()

        @pl.when(s + SLOTS - 1 < steps)
        def _():
            fetch(s + SLOTS - 1, lax.rem(s + SLOTS - 1, SLOTS)).start()

        @pl.when(s >= SLOTS)
        def _():
            store(s - SLOTS, slot).wait()

        def group(g, carry):
            at = pl.ds(pl.multiple_of(g * 16, 16), 16)
            for t in range(PIECES):
                here = pl.ds(t * PIECE, PIECE)
                code = buf[slot, at, here]
                eights = jnp.maximum(jnp.bitwise_and(code, 120), 8)
                value = lax.shift_left(
                    jnp.bitwise_and(code, 127) - eights + 8, lax.shift_right_logical(eights, 3)
                )
                value = jnp.where(code >= 128, -value, value)
                done[slot, at, here] = value.astype(f32).astype(bf16)
            return carry

        lax.fori_loop(0, DEC_ROWS // 16, group, 0)
        store(s, slot).start()
        return carry

    lax.fori_loop(0, steps, step, 0)
    for s in range(max(steps - SLOTS, 0), steps):
        store(s, s % SLOTS).wait()
    for move in moves:
        move.wait()


def decode(codes, first, rows, state=()):
    count = len(state)
    return pl.pallas_call(
        functools.partial(decode_kernel, first, rows // DEC_ROWS, count),
        out_shape=(pltpu.HBM((rows, WIDTH), bf16),) + tuple(kept(x.shape) for x in state),
        in_specs=[in_hbm()] * (1 + count),
        out_specs=(in_hbm(),) + (in_vmem(),) * count,
        scratch_shapes=[
            pltpu.VMEM((SLOTS, DEC_ROWS, WIDTH), i32),
            pltpu.VMEM((SLOTS, DEC_ROWS, WIDTH), bf16),
            pltpu.SemaphoreType.DMA((SLOTS,)),
            pltpu.SemaphoreType.DMA((SLOTS,)),
            pltpu.SemaphoreType.DMA((6,)),
        ],
        compiler_params=params_for(12),
        cost_estimate=pl.CostEstimate(flops=20_000_000, transcendentals=0, bytes_accessed=12_000_000),
        name="decode",
    )(stay(codes), *[stay(x) for x in state])


def own_kernel(a, b, xa, xb, sem_a, sem_b):
    core = lax.axis_index("c")
    moves = [
        pltpu.make_async_copy(b.at[pl.ds(pl.multiple_of(core * 8, 8), 8), :], xb, sem_b)
    ] + [
        pltpu.make_async_copy(
            a.at[:, pl.ds(pl.multiple_of(c * WIDTH + core * HALF, 128), HALF)],
            xa.at[pl.ds(c * 16, 16), :],
            sem_a.at[c],
        )
        for c in range(COLS)
    ]
    for move in moves:
        move.start()
    for move in moves:
        move.wait()


def own_half(a, b):
    return pl.pallas_call(
        own_kernel,
        out_shape=(kept((128, HALF), bf16), kept((8, FULL_B), bf16)),
        in_specs=[in_hbm()] * 2,
        out_specs=(in_vmem(),) * 2,
        scratch_shapes=[pltpu.SemaphoreType.DMA((COLS,)), pltpu.SemaphoreType.DMA],
        compiler_params=params_for(8),
        name="own_half",
    )(stay(a), stay(b))


CHUNKS = (768, 768, 768, 1024)


def pair_kernel(own_w, mate_w, own_a, mate_a, own_b, mate_b, out, buf, sems):
    core = lax.axis_index("c")

    def store(n, start, width):
        here = pl.ds(start, width)
        return pltpu.make_async_copy(buf.at[:, here], out.at[:, here], sems.at[n])

    o = lax.broadcasted_iota(i32, (128, 256), 0)
    k = lax.broadcasted_iota(i32, (128, 256), 1)
    same_block = jnp.bitwise_and(lax.shift_right_logical(o, 1), 7) == jnp.bitwise_and(
        lax.shift_right_logical(k, 4), 7
    )
    rank = lax.shift_right_logical(o, 4) * 2 + jnp.bitwise_and(o, 1)
    same_rank = rank == jnp.bitwise_and(k, 15)
    weight = jnp.where(k < 128, own_w[0, 1], mate_w[0, 1])
    pick = jnp.where(jnp.logical_and(same_block, same_rank), weight, 0.0).astype(bf16)
    start = 0
    for n, width in enumerate(CHUNKS):
        theirs = [
            mate_a[:, pl.ds(pl.multiple_of(c * WIDTH + core * HALF + start, 128), width)]
            for c in range(COLS)
        ]
        both = jnp.concatenate([own_a[:, pl.ds(start, width)]] + theirs, axis=0)
        buf[:, pl.ds(start, width)] = jnp.dot(pick, both, preferred_element_type=f32).astype(bf16)
        store(n, start, width).start()
        start += width
    for j in range(CHIPS):
        halves = []
        for p in range(2):
            at = pl.ds((2 * j + p) * DEPTH, DEPTH)
            theirs = mate_b[pl.ds(pl.multiple_of(core * 8, 8), 8), at]
            halves.append(own_w[0, 0] * own_b[:, at].astype(f32) + mate_w[0, 0] * theirs.astype(f32))
        buf[pl.ds(j * 16, 16), pl.ds(HALF, DEPTH)] = jnp.concatenate(halves, axis=0).astype(bf16)
    store(len(CHUNKS), HALF, DEPTH).start()
    start = 0
    for n, width in enumerate(CHUNKS + (DEPTH,)):
        store(n, start, width).wait()
        start += width


def pair_sum(own_w, mate_w, own_a, mate_a, own_b, mate_b):
    return pl.pallas_call(
        pair_kernel,
        out_shape=pltpu.HBM((CHIPS * 16, LANES), bf16),
        in_specs=[in_smem()] * 2 + [in_vmem()] * 4,
        out_specs=in_hbm(),
        scratch_shapes=[
            pltpu.VMEM((CHIPS * 16, LANES), bf16),
            pltpu.SemaphoreType.DMA((len(CHUNKS) + 1,)),
        ],
        compiler_params=params_for(16),
        name="pair_sum",
    )(own_w, mate_w, *map(near, (own_a, mate_a, own_b, mate_b)))


def row_kernel(got, out, scr):
    total = got[0].astype(f32)
    for j in range(1, CHIPS):
        total = total + got[j].astype(f32)
    scr[:, 0:8, :] = jnp.zeros_like(scr[:, 0:8, :])
    for d in range(16):
        core, col = divmod(d, COLS)
        a = 2 * col + core
        for i in range(7):
            w = min(PIECE, HALF - i * PIECE)
            scr[d, pl.ds(i, 1), pl.ds(0, w)] = total[a : a + 1, i * PIECE : i * PIECE + w]
        scr[d, pl.ds(8, 8), :] = total[core * 8 : core * 8 + 8, HALF:LANES]
    out[...] = scr[...].astype(bf16)


def row_sum(got):
    return pl.pallas_call(
        row_kernel,
        out_shape=SDS((16, 16, PIECE), bf16),
        in_specs=[in_vmem()],
        out_specs=in_vmem(),
        scratch_shapes=[pltpu.VMEM((16, 16, PIECE), f32)],
        compiler_params=params_for(16),
        name="row_sum",
    )(near(got))


def step_kernel(got, pa, ma, va, send, ga, gb, rows):
    for h in range(2):
        acc = jnp.zeros((16, PIECE), f32)
        for c in range(COLS):
            acc = acc + got[h * COLS + c].astype(f32)
        for i in range(7):
            w = min(PIECE, HALF - i * PIECE)
            ga[:, pl.ds(h * HALF + i * PIECE, w)] = acc[i : i + 1, 0:w]
        gb[pl.ds(h * 8, 8), :] = acc[8:16, :]
    pn = adaptive_update(pa[...], ma[...], va[...], ga[...])[0]
    rows[...] = jnp.zeros_like(rows)
    for i in range(PIECES):
        rows[pl.ds(i, 1), :] = pn[:, i * PIECE : (i + 1) * PIECE]
    message = rows[...].astype(bf16)
    for d in range(16):
        send[d] = message


def server_step(got, pa, ma, va):
    return pl.pallas_call(
        step_kernel,
        out_shape=(SDS((16, 16, PIECE), bf16), kept((1, WIDTH)), kept((RANKS, DEPTH))),
        in_specs=[in_vmem()] * 4,
        out_specs=(in_vmem(),) * 3,
        scratch_shapes=[pltpu.VMEM((16, PIECE), f32)],
        compiler_params=params_for(16),
        name="server_step",
    )(*map(near, (got, pa, ma, va)))


APART = (0, 4, 2, 6, 1, 5, 3, 7)


def state_kernel(
    ga, gb, pa, ma, va, pb, mb, vb, col_0, col_1, pa_n, ma_n, va_n, pb_n, mb_n, vb_n, wide, scr
):
    col = lax.axis_index("x") * 2 + lax.axis_index("zh")
    for n, apart in enumerate(APART):
        block = (col_0, col_1)[n // 4][pl.ds(n % 4 * 8, 8), :]
        owner = jnp.bitwise_xor(col, apart)
        for q in range(3):
            scr[q, owner] = block[2 * q : 2 * q + 2, :]
    grad = gb[...]
    whole = [scr[q].reshape(RANKS, DEPTH) for q in range(3)]
    full = adaptive_update(*whole, grad)[0]
    k = lax.broadcasted_iota(i32, (RANKS, 256), 1)
    r = lax.broadcasted_iota(i32, (RANKS, 256), 0)
    repeat = jnp.where(lax.shift_right_logical(k, 4) == r, adapter_scale, 0.0).astype(bf16)
    tall = jnp.transpose(full).astype(bf16)
    wide[...] = jnp.dot(tall, repeat, preferred_element_type=f32).astype(bf16)
    own = [
        jnp.sum(jnp.where(r[:, 0:1] == 2 * col + q, grad, 0.0), axis=0, keepdims=True)
        for q in range(2)
    ]
    pb_n[...], mb_n[...], vb_n[...] = adaptive_update(
        pb[...], mb[...], vb[...], jnp.concatenate(own, axis=0)
    )
    pa_n[...], ma_n[...], va_n[...] = adaptive_update(pa[...], ma[...], va[...], ga[...])


def server_state(ga, gb, a_state, b_state, col_state):
    a_shape, b_shape = SDS((1, WIDTH), f32), SDS((2, DEPTH), f32)
    return pl.pallas_call(
        state_kernel,
        out_shape=(a_shape,) * 3 + (b_shape,) * 3 + (kept((DEPTH, 256), bf16),),
        in_specs=[in_vmem()] * 10,
        out_specs=(in_vmem(),) * 7,
        scratch_shapes=[pltpu.VMEM((3, COLS, 2, DEPTH), f32)],
        compiler_params=params_for(16),
        name="server_state",
    )(*map(near, (ga, gb, *a_state, *b_state)), *col_state)


BLOCK = 512


def merge_kernel(dec_top, dec_low, scale, wide, ranks, merged, peaks, buf, row_scale, tops, sems):
    fetches = []
    for i in range(PIECES):
        here = pl.ds(i * PIECE, PIECE)
        fetches.append(
            [
                pltpu.make_async_copy(dec.at[:, here], buf.at[i, pl.ds(q * TOP, (TOP, DEPTH - TOP)[q]), :], sems.at[i, q])
                for q, dec in enumerate((dec_top, dec_low))
            ]
        )
        for fetch in fetches[-1]:
            fetch.start()
    row_scale[...] = jnp.transpose(jnp.broadcast_to(scale[...] * 2.0**-10, (128, DEPTH)))
    lane = jnp.bitwise_and(lax.broadcasted_iota(i32, (BLOCK, 256), 1), 15)
    right = ranks[...].reshape(256, PIECE)
    tops[...] = jnp.zeros_like(tops)
    for i in range(PIECES):
        for fetch in fetches[i]:
            fetch.wait()
        for b in range(DEPTH // BLOCK):
            at = pl.ds(b * BLOCK, BLOCK)
            left = wide[at, :]
            one = jnp.where(lane == i, left, jnp.zeros_like(left))
            low = jnp.dot(one, right, preferred_element_type=f32)
            top = tops[at, :]
            for t in range(PIECE // 128):
                here = pl.ds(t * 128, 128)
                whole = buf[i, at, here].astype(f32) * row_scale[at, :] + low[:, t * 128 : t * 128 + 128]
                merged[i, at, here] = whole
                top = jnp.maximum(top, jnp.abs(whole))
            tops[at, :] = top
    peak = jnp.max(jnp.transpose(tops[...]), axis=0, keepdims=True)
    for c in range(COLS):
        peaks[c] = peak


def merge(decs, scale, wide, ranks):
    return pl.pallas_call(
        merge_kernel,
        out_shape=(pltpu.VMEM((PIECES, DEPTH, PIECE), f32), SDS((COLS, 1, DEPTH), f32)),
        in_specs=[in_hbm()] * 2 + [in_vmem()] * 3,
        out_specs=(in_vmem(), in_vmem()),
        scratch_shapes=[
            pltpu.VMEM((PIECES, DEPTH, PIECE), bf16),
            pltpu.VMEM((DEPTH, 128), f32),
            pltpu.VMEM((DEPTH, 128), f32),
            pltpu.SemaphoreType.DMA((PIECES, 2)),
        ],
        compiler_params=params_for(16),
        name="merge",
    )(*map(stay, decs), scale, near(wide), near(ranks))


OUT_ROWS = 32


def normalise_kernel(merged, peaks, out, scales, inverse, buf, sems):
    peak = peaks[0]
    for c in range(1, COLS):
        peak = jnp.maximum(peak, peaks[c])
    peak = peak + peak_eps
    scales[...] = peak / fp8_top
    inverse[...] = jnp.transpose(jnp.broadcast_to(1.0 / peak, (128, DEPTH)))
    steps, slots = DEPTH // OUT_ROWS, 8

    def store(step, slot):
        return pltpu.make_async_copy(
            buf.at[slot],
            out.at[pl.ds(pl.multiple_of(step * OUT_ROWS, OUT_ROWS), OUT_ROWS), :],
            sems.at[slot],
        )

    def step(s, carry):
        slot = lax.rem(s, slots)

        @pl.when(s >= slots)
        def _():
            store(s - slots, slot).wait()

        for g in range(OUT_ROWS // 16):
            row = pl.multiple_of(s * OUT_ROWS + g * 16, 16)
            inv = inverse[pl.ds(row, 16), :]
            inv = jnp.concatenate([inv] * (PIECE // 128), axis=1)
            for t in range(PIECES):
                here = pl.ds(t * PIECE, PIECE)
                buf[slot, pl.ds(g * 16, 16), here] = (merged[t, pl.ds(row, 16), :] * inv).astype(bf16)
        store(s, slot).start()
        return carry

    lax.fori_loop(0, steps, step, 0)
    for s in range(steps - slots, steps):
        store(s, s % slots).wait()


def normalise(merged, peaks):
    return pl.pallas_call(
        normalise_kernel,
        out_shape=(SDS((DEPTH, WIDTH), bf16), SDS((1, DEPTH), f32)),
        in_specs=[in_vmem(), in_vmem()],
        out_specs=(in_hbm(), in_vmem()),
        scratch_shapes=[
            pltpu.VMEM((DEPTH, 128), f32),
            pltpu.VMEM((8, OUT_ROWS, WIDTH), bf16),
            pltpu.SemaphoreType.DMA((8,)),
        ],
        compiler_params=params_for(16),
        name="normalise",
    )(near(merged), peaks)


def local(codes, scale, pb, pa, mb, vb, ma, va, delta_b, delta_a, tallies):
    exchange = functools.partial(lax.all_to_all, split_axis=0, concat_axis=0, tiled=True)
    swap = functools.partial(lax.ppermute, perm=[(0, 1), (1, 0)])
    weights = tallies.astype(f32) / (count_scale * 128)
    own_a = delta_a.reshape(RANKS, FULL_A)
    own_b = delta_b.reshape(FULL_B, RANKS).T
    mate_a, mate_b, mate_w = swap(own_a, "c"), swap(own_b, "c"), swap(weights, "c")
    pb, mb, vb = pb.T, mb.T, vb.T
    near_a, near_b = own_half(own_a, own_b)
    pairs = pair_sum(weights, mate_w, near_a, mate_a, near_b, mate_b)
    pairs, codes, pb, mb, vb = lax.optimization_barrier((pairs, codes, pb, mb, vb))
    got = exchange(pairs.reshape(CHIPS, 16, LANES), ("zl", "y"))
    block = jnp.concatenate([pb, mb, vb, pb], axis=0)
    for apart in (2, 1):
        other = lax.ppermute(block, "x", [(k, k ^ apart) for k in range(4)])
        block = jnp.concatenate([block, other], axis=0)
    (top,) = decode(codes, 0, TOP)
    got, top, block = lax.optimization_barrier((got, top, block))
    message = row_sum(got)
    codes, message, block = lax.optimization_barrier((codes, message, block))
    got = exchange(message, ("c",) + COL)
    other = swap(block, "zh")
    low, *state = decode(codes, TOP, DEPTH - TOP, (pa, ma, va, pb, mb, vb))
    got, low, state, other = lax.optimization_barrier((got, low, state, other))
    send, ga, gb = server_step(got, *state[:3])
    ranks = exchange(send, ROW)
    pa_n, ma_n, va_n, pb_n, mb_n, vb_n, wide = server_state(
        ga, gb, state[:3], state[3:], (block, other)
    )
    merged, peaks = merge((top, low), scale.reshape(1, DEPTH), wide, ranks)
    out, scales = normalise(merged, exchange(peaks, COL))
    return (out, scales.reshape(DEPTH), pb_n.T, pa_n, mb_n.T, vb_n.T, ma_n, va_n)


def solution(mesh):
    split = Mesh(mesh.devices.reshape(2, 4, 2, 4, 2), ROW + COL)
    tile, everyone = P(ROW, COL), P(ROW + COL, None, None)
    return jax.shard_map(
        local,
        mesh=split,
        in_specs=(tile, P(ROW)) + (tile,) * 6 + (everyone, everyone, P(ROW + COL, None)),
        out_specs=(tile, P(ROW)) + (tile,) * 6,
        check_vma=False,
    )
```

time: 82.6 us -> 78.9 us (0.955)
  Pallas kernels: 28.9 us -> 25.1 us
  starting transfers between devices: 23.1 us -> 25.7 us
    pallas_call x5 -> x6, Pallas kernels: 18.2 us -> 15.1 us  [the longest x2 10.3 us: decode(): pl.pallas_call(functools.partial(decode_kernel, first, rows // DEC_ROWS,...]
    all_to_all x1, starting transfers between devices: 5.4 us -> 7.42 us  [local(): got = exchange(message, ('c',) + COL)]
    all_to_all x1, starting transfers between devices: 4.93 us -> 5.92 us  [local(): got = exchange(pairs.reshape(CHIPS, 16, LANES), ('zl', 'y'))]
  transfers between devices with their start and end apart: 9 -> 9, of which waited for: 5 -> 6; matrix products, arithmetic and copies ran while one was open for 2% -> 1% of each run, Pallas kernels for 21% -> 16%
where the time goes in v3:
time: 78.9 us; the launch traced here: 78.5 us
  starting transfers between devices  25.7 us (33%)
  Pallas kernels  25.1 us (32%)
  waiting for transfers between devices  14.9 us (19%)
  blocking collectives  11.2 us (14%)
    all_to_all x1, blocking collectives, local(): out, scales = normalise(merged, exchange(peaks, COL))  11.2 us
    pallas_call x2, Pallas kernels, decode(): pl.pallas_call(functools.partial(decode_kernel, first, rows // DEC_ROWS,...  10.3 us
    all_to_all x1, starting transfers between devices, local(): got = exchange(message, ('c',) + COL)  7.42 us
    all_to_all x1, waiting for transfers between devices, local(): ranks = exchange(send, ROW)  6.96 us
    all_to_all x1, starting transfers between devices, local(): got = exchange(pairs.reshape(CHIPS, 16, LANES), ('zl', 'y'))  5.92 us
    pallas_call x1, Pallas kernels, merge(): pl.pallas_call(merge_kernel, out_shape=(pltpu.VMEM((PIECES, DEPTH, PIECE)...  5.38 us
    ppermute x2, starting transfers between devices, local(): other = lax.ppermute(block, 'x', [(k, k ^ apart) for k in range(4)])  4.66 us
    pallas_call x1, Pallas kernels, normalise(): pl.pallas_call(normalise_kernel, out_shape=(SDS((DEPTH, WIDTH), bf16), SD...  3.64 us
  transfers between devices with their start and end apart: 9, of which 6 were waited for; matrix products, arithmetic and copies ran while one was open for 1% of the time, Pallas kernels for 16%

profile of v3, /device:TPU:0, one launch (start us, length us, event | category | flops | bytes accessed | tf_op | source)
XLA Modules:
  0.0 78.5 jit_solution(3032076095582364123)
XLA Ops:
  0.6 0.0 copy-start.3
  0.6 0.0 copy-start.2
  0.7 0.0 copy-start.1
  0.7 0.1 collective-permute-start.1
  0.8 0.5 collective-permute-start.2
  1.3 0.7 convert_multiply_fusion.own_w
  1.9 0.1 collective-permute-start
  2.0 1.3 %own_half.1 = (bf16[128,3328]{1,0:T(8,128)(2,1)S(1)}, bf16[8,8192]{1,0:T(8,128)(2,1)S(1)}) custom-call(bf16[16,53248]{1,0:T(8,128)(2,1)} %bitcast.16, bf16[16,8192]{1,0:T(8,128)(2,1)} %bitcast.18), custom_call_target="tpu_custom_call" | custom-call | tf_op jit(solution)/shard_map/own_half/pallas_call | solution.py:174
  3.4 1.0 %collective-permute-done.mate_w = f32[1,2]{1,0:T(1,128)S(1)} collective-permute-done((f32[1,2]{1,0:T(1,128)S(1)}, f32[1,2]{1,0:T(1,128)S(1)}, u32[]{:S(2)}, u32[]{:S(2)}) %collective-permute-start) | collective-permute-done | bytes 40 | tf_op jit(solution)/shard_map/ppermute | solution.py:462
  4.3 0.6 collective-permute-done.2.mate_b
  4.9 0.0 collective-permute-done.1.mate_a
  4.9 1.8 %pair_sum.1 = bf16[128,3840]{1,0:T(8,128)(2,1)} custom-call(f32[1,2]{1,0:T(1,128)S(1)} %convert_multiply_fusion.own_w, f32[1,2]{1,0:T(1,128)S(1)} %collective-permute-done.mate_w, bf16[128,3328]{1,0:T(8,128)(2,1)S(1)} %get-tuple-element.51.own_a, bf16[16,53248]{1,0:T(8,128)(2,1)S(1)} %collective-permute-done.1.mate_a, ...), custom_call_target="tpu_custom_call" | custom-call | tf_op jit(solution)/shard_map/pair_sum/pallas_call | solution.py:229
  6.8 5.9 %all-to-all-start = ((bf16[8,16,3840]{2,1,0:T(8,128)(2,1)}), bf16[8,16,3840]{2,1,0:T(8,128)(2,1)S(1)}, u32[]{:S(2)}, u32[]{:S(2)}) async-start(bf16[8,16,3840]{2,1,0:T(8,128)(2,1)} %bitcast.14), calls=%async_computation | async-start | bytes 1966080 | tf_op jit(solution)/shard_map/all_to_all | solution.py:467
  12.7 3.1 %collective-permute-start.3 = (f32[8,512]{1,0:T(8,128)S(1)}, f32[8,512]{1,0:T(8,128)S(1)}, u32[]{:S(2)}, u32[]{:S(2)}) collective-permute-start(f32[8,512]{1,0:T(8,128)S(1)} %pad_maximum_fusion), channel_id=1, source_target_pairs={{0,4},{2,6},{4,0},{6,2},{1,5},{3,7},{5,1},{7,3},{8,12},{10,14},{12... | collective-permute-start | bytes 49160 | tf_op jit(solution)/shard_map/ppermute | solution.py:470
  15.8 2.2 %collective-permute-done.3 = f32[8,512]{1,0:T(8,128)S(1)} collective-permute-done((f32[8,512]{1,0:T(8,128)S(1)}, f32[8,512]{1,0:T(8,128)S(1)}, u32[]{:S(2)}, u32[]{:S(2)}) %collective-permute-start.3) | collective-permute-done | bytes 16416 | tf_op jit(solution)/shard_map/ppermute | solution.py:470
  18.1 1.6 %collective-permute-start.4 = (f32[16,512]{1,0:T(8,128)S(1)}, f32[16,512]{1,0:T(8,128)S(1)}, u32[]{:S(2)}, u32[]{:S(2)}) collective-permute-start(f32[16,512]{1,0:T(8,128)S(1)} %concatenate.12), channel_id=1, source_target_pairs={{0,2},{2,0},{4,6},{6,4},{1,3},{3,1},{5,7},{7,5},{8,10},{10,8},{12,... | collective-permute-start | bytes 98312 | tf_op jit(solution)/shard_map/ppermute | solution.py:470
  19.6 6.3 %decode.2.dec_top = bf16[352,6656]{1,0:T(8,128)(2,1)} custom-call(s32[512,6656]{1,0:T(8,128)} %refs_0_.1), custom_call_target="tpu_custom_call" | custom-call | flops 20000000 | bytes 12000000 | tf_op jit(solution)/shard_map/decode/pallas_call | solution.py:137
  25.9 0.0 collective-permute-done.4
  26.0 2.0 %all-to-all-done.got = bf16[8,16,3840]{2,1,0:T(8,128)(2,1)S(1)} async-done(((bf16[8,16,3840]{2,1,0:T(8,128)(2,1)}), bf16[8,16,3840]{2,1,0:T(8,128)(2,1)S(1)}, u32[]{:S(2)}, u32[]{:S(2)}) %all-to-all-start) | async-done | bytes 983072 | tf_op jit(solution)/shard_map/all_to_all | solution.py:467
  28.0 1.0 %row_sum.1 = bf16[16,16,512]{2,1,0:T(8,128)(2,1)} custom-call(bf16[8,16,3840]{2,1,0:T(8,128)(2,1)S(1)} %all-to-all-done.got), custom_call_target="tpu_custom_call" | custom-call | tf_op jit(solution)/shard_map/row_sum/pallas_call | solution.py:259
  28.9 7.4 %all-to-all-start.1 = ((bf16[16,16,512]{2,1,0:T(8,128)(2,1)}), bf16[16,16,512]{2,1,0:T(8,128)(2,1)S(1)}, u32[]{:S(2)}, u32[]{:S(2)}) async-start(bf16[16,16,512]{2,1,0:T(8,128)(2,1)} %row_sum.1), calls=%async_computation.1 | async-start | bytes 524288 | tf_op jit(solution)/shard_map/all_to_all | solution.py:476
  36.4 0.0 copy-start
  36.4 3.5 %collective-permute-start.5 = (f32[32,512]{1,0:T(8,128)S(1)}, f32[32,512]{1,0:T(8,128)S(1)}, u32[]{:S(2)}, u32[]{:S(2)}) collective-permute-start(f32[32,512]{1,0:T(8,128)S(1)} %concatenate.13.col_0), channel_id=1, source_target_pairs={{0,1},{1,0},{2,3},{3,2},{4,5},{5,4},{6,7},{7,6},{8,9},{9,8},{10,11... | collective-permute-start | bytes 196616 | tf_op jit(solution)/shard_map/ppermute | solution.py:477
  39.9 4.0 %decode.3 = (bf16[160,6656]{1,0:T(8,128)(2,1)}, f32[1,6656]{1,0:T(1,128)S(1)}, f32[1,6656]{1,0:T(1,128)S(1)}, f32[1,6656]{1,0:T(1,128)S(1)}, f32[2,512]{1,0:T(2,...) custom-call(s32[512,6656]{1,0:T(8,128)} %refs_0_.1, f32[1,6656]{1,0:T(1,128)} %refs_1_.1, f32[1,6656]{1,0:T(1,128)} %refs_2_.1, ...), custom_call_target="tpu_custom_call" | custom-call | flops 20000000 | bytes 12000000 | tf_op jit(solution)/shard_map/decode/pallas_call | solution.py:137
  43.9 2.1 %all-to-all-done.1.got = bf16[16,16,512]{2,1,0:T(8,128)(2,1)S(1)} async-done(((bf16[16,16,512]{2,1,0:T(8,128)(2,1)}), bf16[16,16,512]{2,1,0:T(8,128)(2,1)S(1)}, u32[]{:S(2)}, u32[]{:S(2)}) %all-to-all-start.1) | async-done | bytes 262176 | tf_op jit(solution)/shard_map/all_to_all | solution.py:476
  46.0 0.8 %server_step.1 = (bf16[16,16,512]{2,1,0:T(8,128)(2,1)}, f32[1,6656]{1,0:T(1,128)S(1)}, f32[16,512]{1,0:T(8,128)S(1)}) custom-call(bf16[16,16,512]{2,1,0:T(8,128)(2,1)S(1)} %all-to-all-done.1.got, f32[1,6656]{1,0:T(1,128)S(1)} %get-tuple-element.73.pa, f32[1,6656]{1,0:T(1,128)S(1)} %get-tuple-element.74.ma, f32[1,6656]{1,0:T(1,128)S(1)} %get-tuple-element.75.va), custom_call_target="tpu_custom_call" | custom-call | tf_op jit(solution)/shard_map/server_step/pallas_call | solution.py:289
  46.8 3.5 %all-to-all-start.2 = ((bf16[16,16,512]{2,1,0:T(8,128)(2,1)}), bf16[16,16,512]{2,1,0:T(8,128)(2,1)S(1)}, u32[]{:S(2)}, u32[]{:S(2)}) async-start(bf16[16,16,512]{2,1,0:T(8,128)(2,1)} %get-tuple-element.83), calls=%async_computation.2 | async-start | bytes 524288 | tf_op jit(solution)/shard_map/all_to_all | solution.py:481
  50.4 0.9 %server_state.1 = (f32[1,6656]{1,0:T(1,128)}, f32[1,6656]{1,0:T(1,128)}, f32[1,6656]{1,0:T(1,128)}, f32[2,512]{1,0:T(2,128)}, f32[2,512]{1,0:T(2,128)}, /*index=5*/f32[2,512]{1,0:T(2,128)}, bf16[512,256]{1,0:T(8,128)(2,1)S(1)}) custom-call(f32[1,6656]{1,0:T(1,128)S(1)} %get-tuple-element.76.ga, f32[16,512]{1,0:T(8,128)S(1)} %get-tuple-element.77.gb, ...), custom_call_target="tpu_custom_call" | custom-call | tf_op jit(solution)/shard_map/server_state/pallas_call | solution.py:332
  51.3 7.0 %all-to-all-done.2.ranks = bf16[16,16,512]{2,1,0:T(8,128)(2,1)S(1)} async-done(((bf16[16,16,512]{2,1,0:T(8,128)(2,1)}), bf16[16,16,512]{2,1,0:T(8,128)(2,1)S(1)}, u32[]{:S(2)}, u32[]{:S(2)}) %all-to-all-start.2) | async-done | bytes 262176 | tf_op jit(solution)/shard_map/all_to_all | solution.py:481
  58.2 5.4 %merge.1 = (f32[13,512,512]{2,1,0:T(8,128)S(1)}, f32[8,1,512]{2,1,0:T(1,128)S(1)}) custom-call(bf16[352,6656]{1,0:T(8,128)(2,1)} %decode.2.dec_top, bf16[160,6656]{1,0:T(8,128)(2,1)} %get-tuple-element.71.dec_low, f32[1,512]{1,0:T(1,128)S(1)} %bitcast.13, bf16[512,256]{1,0:T(8,128)(2,1)S(1)} %get-tuple-element.82.wide, ...), custom_call_target="tpu_custom_call" | custom-call | tf_op jit(solution)/shard_map/merge/pallas_call | solution.py:383
  63.6 11.2 %all_to_all.20.peaks = f32[8,1,512]{2,1,0:T(1,128)S(1)} all-to-all(f32[8,1,512]{2,1,0:T(1,128)S(1)} %get-tuple-element.85), channel_id=1, replica_groups=mesh['zl'=2,'y'=4,'c'=2,'x'=4,'zh'=2] {'x','zh'}, dimensions={0} | all-to-all | bytes 32768 | tf_op jit(solution)/shard_map/all_to_all | solution.py:486
  74.8 3.6 %normalise.1 = (bf16[512,6656]{1,0:T(8,128)(2,1)}, f32[1,512]{1,0:T(1,128)}) custom-call(f32[13,512,512]{2,1,0:T(8,128)S(1)} %get-tuple-element.84.merged, f32[8,1,512]{2,1,0:T(1,128)S(1)} %all_to_all.20.peaks), custom_call_target="tpu_custom_call" | custom-call | tf_op jit(solution)/shard_map/normalise/pallas_call | solution.py:441
  (8 shorter events, 0.1 us)
Async XLA Ops:
  0.6 12.0 %copy-start.3 = (f32[512,2]{0,1:T(2,128)S(1)}, f32[512,2]{0,1:T(2,128)}, u32[]{:S(2)}) copy-start(f32[512,2]{0,1:T(2,128)} %param.16) | copy-start | bytes 12292
  0.6 12.0 %copy-start.2 = (f32[512,2]{0,1:T(2,128)S(1)}, f32[512,2]{0,1:T(2,128)}, u32[]{:S(2)}) copy-start(f32[512,2]{0,1:T(2,128)} %param.15) | copy-start | bytes 12292
  0.7 12.0 %copy-start.1 = (f32[512,2]{0,1:T(2,128)S(1)}, f32[512,2]{0,1:T(2,128)}, u32[]{:S(2)}) copy-start(f32[512,2]{0,1:T(2,128)} %param.13) | copy-start | bytes 12292
  0.7 4.3 %collective-permute-start.1 = (bf16[16,53248]{1,0:T(8,128)(2,1)}, bf16[16,53248]{1,0:T(8,128)(2,1)S(1)}, u32[]{:S(2)}, u32[]{:S(2)}) collective-permute-start(bf16[16,53248]{1,0:T(8,128)(2,1)} %bitcast.15), channel_id=1, source_target_pairs={{0,8},{8,0},{1,9},{9,1},{2,10},{10,2},{3,11},{11,3},{4,12},{12,4},... | collective-permute-start | bytes 5111816 | tf_op jit(solution)/shard_map/ppermute | solution.py:462
  0.8 4.2 %collective-permute-start.2 = (bf16[16,8192]{1,0:T(8,128)(2,1)}, bf16[16,8192]{1,0:T(8,128)(2,1)S(1)}, u32[]{:S(2)}, u32[]{:S(2)}) collective-permute-start(bf16[16,8192]{1,0:T(8,128)(2,1)} %bitcast.17), channel_id=1, source_target_pairs={{0,8},{8,0},{1,9},{9,1},{2,10},{10,2},{3,11},{11,3},{4,12},{12,4},... | collective-permute-start | bytes 786440 | tf_op jit(solution)/shard_map/ppermute | solution.py:462
  1.9 2.4 %collective-permute-start = (f32[1,2]{1,0:T(1,128)S(1)}, f32[1,2]{1,0:T(1,128)S(1)}, u32[]{:S(2)}, u32[]{:S(2)}) collective-permute-start(f32[1,2]{1,0:T(1,128)S(1)} %convert_multiply_fusion.own_w), channel_id=1, source_target_pairs={{0,8},{8,0},{1,9},{9,1},{2,10},{10,2},{3,11},{11,3},{4,12},{12,4},... | collective-permute-start | bytes 32 | tf_op jit(solution)/shard_map/ppermute | solution.py:462
  6.8 21.2 %all-to-all-start = ((bf16[8,16,3840]{2,1,0:T(8,128)(2,1)}), bf16[8,16,3840]{2,1,0:T(8,128)(2,1)S(1)}, u32[]{:S(2)}, u32[]{:S(2)}) async-start(bf16[8,16,3840]{2,1,0:T(8,128)(2,1)} %bitcast.14), calls=%async_computation | async-start | bytes 1966080 | tf_op jit(solution)/shard_map/all_to_all | solution.py:467
  12.7 5.3 %collective-permute-start.3 = (f32[8,512]{1,0:T(8,128)S(1)}, f32[8,512]{1,0:T(8,128)S(1)}, u32[]{:S(2)}, u32[]{:S(2)}) collective-permute-start(f32[8,512]{1,0:T(8,128)S(1)} %pad_maximum_fusion), channel_id=1, source_target_pairs={{0,4},{2,6},{4,0},{6,2},{1,5},{3,7},{5,1},{7,3},{8,12},{10,14},{12... | collective-permute-start | bytes 49160 | tf_op jit(solution)/shard_map/ppermute | solution.py:470
  18.1 7.8 %collective-permute-start.4 = (f32[16,512]{1,0:T(8,128)S(1)}, f32[16,512]{1,0:T(8,128)S(1)}, u32[]{:S(2)}, u32[]{:S(2)}) collective-permute-start(f32[16,512]{1,0:T(8,128)S(1)} %concatenate.12), channel_id=1, source_target_pairs={{0,2},{2,0},{4,6},{6,4},{1,3},{3,1},{5,7},{7,5},{8,10},{10,8},{12,... | collective-permute-start | bytes 98312 | tf_op jit(solution)/shard_map/ppermute | solution.py:470
  28.9 17.1 %all-to-all-start.1 = ((bf16[16,16,512]{2,1,0:T(8,128)(2,1)}), bf16[16,16,512]{2,1,0:T(8,128)(2,1)S(1)}, u32[]{:S(2)}, u32[]{:S(2)}) async-start(bf16[16,16,512]{2,1,0:T(8,128)(2,1)} %row_sum.1), calls=%async_computation.1 | async-start | bytes 524288 | tf_op jit(solution)/shard_map/all_to_all | solution.py:476
  36.4 21.9 %copy-start = (f32[512]{0:T(512)S(1)}, f32[512]{0:T(512)}, u32[]{:S(2)}) copy-start(f32[512]{0:T(512)} %param.12) | copy-start | bytes 6148
  36.4 7.5 %collective-permute-start.5 = (f32[32,512]{1,0:T(8,128)S(1)}, f32[32,512]{1,0:T(8,128)S(1)}, u32[]{:S(2)}, u32[]{:S(2)}) collective-permute-start(f32[32,512]{1,0:T(8,128)S(1)} %concatenate.13.col_0), channel_id=1, source_target_pairs={{0,1},{1,0},{2,3},{3,2},{4,5},{5,4},{6,7},{7,6},{8,9},{9,8},{10,11... | collective-permute-start | bytes 196616 | tf_op jit(solution)/shard_map/ppermute | solution.py:477
  46.8 11.4 %all-to-all-start.2 = ((bf16[16,16,512]{2,1,0:T(8,128)(2,1)}), bf16[16,16,512]{2,1,0:T(8,128)(2,1)S(1)}, u32[]{:S(2)}, u32[]{:S(2)}) async-start(bf16[16,16,512]{2,1,0:T(8,128)(2,1)} %get-tuple-element.83), calls=%async_computation.2 | async-start | bytes 524288 | tf_op jit(solution)/shard_map/all_to_all | solution.py:481

commit v4 on v3

--- a/solution.py
+++ b/solution.py
@@ -23,9 +23,8 @@
 CHIPS, COLS = 8, 8
 RANKS = 16
 DEPTH, WIDTH = 512, 6656
-HALF = WIDTH // 2
 FULL_B, FULL_A = DEPTH * 16, WIDTH * 8
-LANES = HALF + DEPTH
+LANES = WIDTH + 2 * DEPTH
 PIECE = 512
 PIECES = WIDTH // PIECE
 
@@ -71,7 +70,7 @@
 
 DEC_ROWS = 32
 SLOTS = 6
-TOP = 352
+ROW_PARTS = (352, 160)
 
 
 def decode_kernel(first, steps, count, *refs):
@@ -92,7 +91,14 @@
 
     for s in range(min(SLOTS - 1, steps)):
         fetch(s, s).start()
-    moves = [pltpu.make_async_copy(a, b, state_sems.at[q]) for q, (a, b) in enumerate(zip(state, held))]
+    pairs = []
+    for a, b in zip(state, held):
+        if a.shape == b.shape:
+            pairs.append((a, b))
+        else:
+            for i in range(PIECES):
+                pairs.append((a.at[:, pl.ds(i * PIECE, PIECE)], b.at[pl.ds(i, 1), :]))
+    moves = [pltpu.make_async_copy(a, b, state_sems.at[q]) for q, (a, b) in enumerate(pairs)]
     for move in moves:
         move.start()
 
@@ -136,7 +142,7 @@
     count = len(state)
     return pl.pallas_call(
         functools.partial(decode_kernel, first, rows // DEC_ROWS, count),
-        out_shape=(pltpu.HBM((rows, WIDTH), bf16),) + tuple(kept(x.shape) for x in state),
+        out_shape=(pltpu.HBM((rows, WIDTH), bf16),) + tuple(kept(x.shape if x.shape[0] > 1 else (16, PIECE)) for x in state),
         in_specs=[in_hbm()] * (1 + count),
         out_specs=(in_hbm(),) + (in_vmem(),) * count,
         scratch_shapes=[
@@ -144,7 +150,7 @@
             pltpu.VMEM((SLOTS, DEC_ROWS, WIDTH), bf16),
             pltpu.SemaphoreType.DMA((SLOTS,)),
             pltpu.SemaphoreType.DMA((SLOTS,)),
-            pltpu.SemaphoreType.DMA((6,)),
+            pltpu.SemaphoreType.DMA((3 * PIECES + 3,)),
         ],
         compiler_params=params_for(12),
         cost_estimate=pl.CostEstimate(flops=20_000_000, transcendentals=0, bytes_accessed=12_000_000),
@@ -153,14 +159,9 @@
 
 
 def own_kernel(a, b, xa, xb, sem_a, sem_b):
-    core = lax.axis_index("c")
-    moves = [
-        pltpu.make_async_copy(b.at[pl.ds(pl.multiple_of(core * 8, 8), 8), :], xb, sem_b)
-    ] + [
+    moves = [pltpu.make_async_copy(b, xb, sem_b)] + [
         pltpu.make_async_copy(
-            a.at[:, pl.ds(pl.multiple_of(c * WIDTH + core * HALF, 128), HALF)],
-            xa.at[pl.ds(c * 16, 16), :],
-            sem_a.at[c],
+            a.at[:, pl.ds(c * WIDTH, WIDTH)], xa.at[pl.ds(c * RANKS, RANKS), :], sem_a.at[c]
         )
         for c in range(COLS)
     ]
@@ -170,19 +171,19 @@
         move.wait()
 
 
-def own_half(a, b):
+def own_deltas(a, b):
     return pl.pallas_call(
         own_kernel,
-        out_shape=(kept((128, HALF), bf16), kept((8, FULL_B), bf16)),
+        out_shape=(kept((128, WIDTH), bf16), kept((RANKS, FULL_B), bf16)),
         in_specs=[in_hbm()] * 2,
         out_specs=(in_vmem(),) * 2,
         scratch_shapes=[pltpu.SemaphoreType.DMA((COLS,)), pltpu.SemaphoreType.DMA],
         compiler_params=params_for(8),
-        name="own_half",
+        name="own_deltas",
     )(stay(a), stay(b))
 
 
-CHUNKS = (768, 768, 768, 1024)
+CHUNKS = (1536, 1536, 1536, 2048)
 
 
 def pair_kernel(own_w, mate_w, own_a, mate_a, own_b, mate_b, out, buf, sems):
@@ -192,35 +193,27 @@
         here = pl.ds(start, width)
         return pltpu.make_async_copy(buf.at[:, here], out.at[:, here], sems.at[n])
 
-    o = lax.broadcasted_iota(i32, (128, 256), 0)
-    k = lax.broadcasted_iota(i32, (128, 256), 1)
-    same_block = jnp.bitwise_and(lax.shift_right_logical(o, 1), 7) == jnp.bitwise_and(
-        lax.shift_right_logical(k, 4), 7
-    )
-    rank = lax.shift_right_logical(o, 4) * 2 + jnp.bitwise_and(o, 1)
-    same_rank = rank == jnp.bitwise_and(k, 15)
+    o = lax.broadcasted_iota(i32, (64, 256), 0)
+    k = lax.broadcasted_iota(i32, (64, 256), 1)
+    same_block = jnp.bitwise_and(o, 7) == jnp.bitwise_and(lax.shift_right_logical(k, 4), 7)
+    same_rank = lax.shift_right_logical(o, 3) * 2 + core == jnp.bitwise_and(k, 15)
     weight = jnp.where(k < 128, own_w[0, 1], mate_w[0, 1])
     pick = jnp.where(jnp.logical_and(same_block, same_rank), weight, 0.0).astype(bf16)
     start = 0
     for n, width in enumerate(CHUNKS):
-        theirs = [
-            mate_a[:, pl.ds(pl.multiple_of(c * WIDTH + core * HALF + start, 128), width)]
-            for c in range(COLS)
-        ]
+        theirs = [mate_a[:, pl.ds(c * WIDTH + start, width)] for c in range(COLS)]
         both = jnp.concatenate([own_a[:, pl.ds(start, width)]] + theirs, axis=0)
         buf[:, pl.ds(start, width)] = jnp.dot(pick, both, preferred_element_type=f32).astype(bf16)
         store(n, start, width).start()
         start += width
     for j in range(CHIPS):
-        halves = []
-        for p in range(2):
-            at = pl.ds((2 * j + p) * DEPTH, DEPTH)
-            theirs = mate_b[pl.ds(pl.multiple_of(core * 8, 8), 8), at]
-            halves.append(own_w[0, 0] * own_b[:, at].astype(f32) + mate_w[0, 0] * theirs.astype(f32))
-        buf[pl.ds(j * 16, 16), pl.ds(HALF, DEPTH)] = jnp.concatenate(halves, axis=0).astype(bf16)
-    store(len(CHUNKS), HALF, DEPTH).start()
+        at = pl.ds(pl.multiple_of((2 * j + core) * DEPTH, DEPTH), DEPTH)
+        both = own_w[0, 0] * own_b[:, at].astype(f32) + mate_w[0, 0] * mate_b[:, at].astype(f32)
+        both = jnp.concatenate([both[0:8, :], both[8:16, :]], axis=1)
+        buf[pl.ds(j * 8, 8), pl.ds(WIDTH, 2 * DEPTH)] = both.astype(bf16)
+    store(len(CHUNKS), WIDTH, 2 * DEPTH).start()
     start = 0
-    for n, width in enumerate(CHUNKS + (DEPTH,)):
+    for n, width in enumerate(CHUNKS + (2 * DEPTH,)):
         store(n, start, width).wait()
         start += width
 
@@ -228,11 +221,11 @@
 def pair_sum(own_w, mate_w, own_a, mate_a, own_b, mate_b):
     return pl.pallas_call(
         pair_kernel,
-        out_shape=pltpu.HBM((CHIPS * 16, LANES), bf16),
+        out_shape=pltpu.HBM((CHIPS * 8, LANES), bf16),
         in_specs=[in_smem()] * 2 + [in_vmem()] * 4,
         out_specs=in_hbm(),
         scratch_shapes=[
-            pltpu.VMEM((CHIPS * 16, LANES), bf16),
+            pltpu.VMEM((CHIPS * 8, LANES), bf16),
             pltpu.SemaphoreType.DMA((len(CHUNKS) + 1,)),
         ],
         compiler_params=params_for(16),
@@ -244,43 +237,35 @@
     total = got[0].astype(f32)
     for j in range(1, CHIPS):
         total = total + got[j].astype(f32)
-    scr[:, 0:8, :] = jnp.zeros_like(scr[:, 0:8, :])
-    for d in range(16):
-        core, col = divmod(d, COLS)
-        a = 2 * col + core
-        for i in range(7):
-            w = min(PIECE, HALF - i * PIECE)
-            scr[d, pl.ds(i, 1), pl.ds(0, w)] = total[a : a + 1, i * PIECE : i * PIECE + w]
-        scr[d, pl.ds(8, 8), :] = total[core * 8 : core * 8 + 8, HALF:LANES]
+    scr[:, 8:16, :] = jnp.zeros_like(scr[:, 8:16, :])
+    for c in range(COLS):
+        for i in range(PIECES):
+            scr[c, pl.ds(i, 1), :] = total[c : c + 1, i * PIECE : (i + 1) * PIECE]
+        scr[c, pl.ds(16, 8), :] = total[:, WIDTH : WIDTH + DEPTH]
+        scr[c, pl.ds(24, 8), :] = total[:, WIDTH + DEPTH : LANES]
     out[...] = scr[...].astype(bf16)
 
 
 def row_sum(got):
     return pl.pallas_call(
         row_kernel,
-        out_shape=SDS((16, 16, PIECE), bf16),
+        out_shape=SDS((COLS, 32, PIECE), bf16),
         in_specs=[in_vmem()],
         out_specs=in_vmem(),
-        scratch_shapes=[pltpu.VMEM((16, 16, PIECE), f32)],
+        scratch_shapes=[pltpu.VMEM((COLS, 32, PIECE), f32)],
         compiler_params=params_for(16),
         name="row_sum",
     )(near(got))
 
 
-def step_kernel(got, pa, ma, va, send, ga, gb, rows):
-    for h in range(2):
-        acc = jnp.zeros((16, PIECE), f32)
-        for c in range(COLS):
-            acc = acc + got[h * COLS + c].astype(f32)
-        for i in range(7):
-            w = min(PIECE, HALF - i * PIECE)
-            ga[:, pl.ds(h * HALF + i * PIECE, w)] = acc[i : i + 1, 0:w]
-        gb[pl.ds(h * 8, 8), :] = acc[8:16, :]
-    pn = adaptive_update(pa[...], ma[...], va[...], ga[...])[0]
-    rows[...] = jnp.zeros_like(rows)
-    for i in range(PIECES):
-        rows[pl.ds(i, 1), :] = pn[:, i * PIECE : (i + 1) * PIECE]
-    message = rows[...].astype(bf16)
+def step_kernel(got, pa, ma, va, send, grad):
+    total = got[0].astype(f32)
+    for c in range(1, COLS):
+        total = total + got[c].astype(f32)
+    grad[...] = total
+    pn = adaptive_update(pa[...], ma[...], va[...], total[0:16, :])[0]
+    row = lax.broadcasted_iota(i32, pn.shape, 0)
+    message = jnp.where(row < PIECES, pn, 0.0).astype(bf16)
     for d in range(16):
         send[d] = message
 
@@ -288,20 +273,19 @@
 def server_step(got, pa, ma, va):
     return pl.pallas_call(
         step_kernel,
-        out_shape=(SDS((16, 16, PIECE), bf16), kept((1, WIDTH)), kept((RANKS, DEPTH))),
+        out_shape=(SDS((16, 16, PIECE), bf16), kept((32, PIECE))),
         in_specs=[in_vmem()] * 4,
-        out_specs=(in_vmem(),) * 3,
-        scratch_shapes=[pltpu.VMEM((16, PIECE), f32)],
+        out_specs=(in_vmem(),) * 2,
         compiler_params=params_for(16),
         name="server_step",
     )(*map(near, (got, pa, ma, va)))
 
 
-APART = (0, 4, 2, 6, 1, 5, 3, 7)
+APART = (0, 1, 4, 5, 2, 3, 6, 7)
 
 
 def state_kernel(
-    ga, gb, pa, ma, va, pb, mb, vb, col_0, col_1, pa_n, ma_n, va_n, pb_n, mb_n, vb_n, wide, scr
+    sums, pa, ma, va, pb, mb, vb, col_0, col_1, pa_n, ma_n, va_n, pb_n, mb_n, vb_n, wide, scr
 ):
     col = lax.axis_index("x") * 2 + lax.axis_index("zh")
     for n, apart in enumerate(APART):
@@ -309,7 +293,7 @@
         owner = jnp.bitwise_xor(col, apart)
         for q in range(3):
             scr[q, owner] = block[2 * q : 2 * q + 2, :]
-    grad = gb[...]
+    grad = sums[16:32, :]
     whole = [scr[q].reshape(RANKS, DEPTH) for q in range(3)]
     full = adaptive_update(*whole, grad)[0]
     k = lax.broadcasted_iota(i32, (RANKS, 256), 1)
@@ -324,56 +308,60 @@
     pb_n[...], mb_n[...], vb_n[...] = adaptive_update(
         pb[...], mb[...], vb[...], jnp.concatenate(own, axis=0)
     )
-    pa_n[...], ma_n[...], va_n[...] = adaptive_update(pa[...], ma[...], va[...], ga[...])
-
-
-def server_state(ga, gb, a_state, b_state, col_state):
+    news = adaptive_update(pa[...], ma[...], va[...], sums[0:16, :])
+    for ref, new in zip((pa_n, ma_n, va_n), news):
+        for i in range(PIECES):
+            ref[:, pl.ds(i * PIECE, PIECE)] = new[i : i + 1, :]
+
+
+def server_state(sums, a_state, b_state, col_state):
     a_shape, b_shape = SDS((1, WIDTH), f32), SDS((2, DEPTH), f32)
     return pl.pallas_call(
         state_kernel,
         out_shape=(a_shape,) * 3 + (b_shape,) * 3 + (kept((DEPTH, 256), bf16),),
-        in_specs=[in_vmem()] * 10,
+        in_specs=[in_vmem()] * 9,
         out_specs=(in_vmem(),) * 7,
         scratch_shapes=[pltpu.VMEM((3, COLS, 2, DEPTH), f32)],
         compiler_params=params_for(16),
         name="server_state",
-    )(*map(near, (ga, gb, *a_state, *b_state)), *col_state)
-
-
-BLOCK = 512
-
-
-def merge_kernel(dec_top, dec_low, scale, wide, ranks, merged, peaks, buf, row_scale, tops, sems):
-    fetches = []
-    for i in range(PIECES):
-        here = pl.ds(i * PIECE, PIECE)
-        fetches.append(
-            [
-                pltpu.make_async_copy(dec.at[:, here], buf.at[i, pl.ds(q * TOP, (TOP, DEPTH - TOP)[q]), :], sems.at[i, q])
-                for q, dec in enumerate((dec_top, dec_low))
-            ]
-        )
-        for fetch in fetches[-1]:
-            fetch.start()
+    )(*map(near, (sums, *a_state, *b_state)), *col_state)
+
+
+GROUPS = (1, 2, 4, 6)
+
+
+def merge_kernel(dec_0, dec_1, scale, wide, ranks, merged, peaks, buf, row_scale, tops, sems):
+    fetches, piece = [], 0
+    for n, count in enumerate(GROUPS):
+        here = pl.ds(piece * PIECE, count * PIECE)
+        fetches.append([])
+        row = 0
+        for q, dec in enumerate((dec_0, dec_1)):
+            to = buf.at[pl.ds(row, ROW_PARTS[q]), here]
+            fetches[-1].append(pltpu.make_async_copy(dec.at[:, here], to, sems.at[n, q]))
+            fetches[-1][-1].start()
+            row += ROW_PARTS[q]
+        piece += count
     row_scale[...] = jnp.transpose(jnp.broadcast_to(scale[...] * 2.0**-10, (128, DEPTH)))
-    lane = jnp.bitwise_and(lax.broadcasted_iota(i32, (BLOCK, 256), 1), 15)
+    lane = jnp.bitwise_and(lax.broadcasted_iota(i32, (DEPTH, 256), 1), 15)
     right = ranks[...].reshape(256, PIECE)
     tops[...] = jnp.zeros_like(tops)
-    for i in range(PIECES):
-        for fetch in fetches[i]:
+    piece = 0
+    for n, count in enumerate(GROUPS):
+        for fetch in fetches[n]:
             fetch.wait()
-        for b in range(DEPTH // BLOCK):
-            at = pl.ds(b * BLOCK, BLOCK)
-            left = wide[at, :]
-            one = jnp.where(lane == i, left, jnp.zeros_like(left))
+        for i in range(piece, piece + count):
+            one = jnp.where(lane == i, wide[...], jnp.zeros((DEPTH, 256), bf16))
             low = jnp.dot(one, right, preferred_element_type=f32)
-            top = tops[at, :]
+            top = tops[...]
             for t in range(PIECE // 128):
-                here = pl.ds(t * 128, 128)
-                whole = buf[i, at, here].astype(f32) * row_scale[at, :] + low[:, t * 128 : t * 128 + 128]
-                merged[i, at, here] = whole
+                at = t * 128
+                code = buf[:, pl.ds(i * PIECE + at, 128)].astype(f32)
+                whole = code * row_scale[...] + low[:, at : at + 128]
+                merged[i, :, pl.ds(at, 128)] = whole
                 top = jnp.maximum(top, jnp.abs(whole))
-            tops[at, :] = top
+            tops[...] = top
+        piece += count
     peak = jnp.max(jnp.transpose(tops[...]), axis=0, keepdims=True)
     for c in range(COLS):
         peaks[c] = peak
@@ -386,12 +374,12 @@
         in_specs=[in_hbm()] * 2 + [in_vmem()] * 3,
         out_specs=(in_vmem(), in_vmem()),
         scratch_shapes=[
-            pltpu.VMEM((PIECES, DEPTH, PIECE), bf16),
+            pltpu.VMEM((DEPTH, WIDTH), bf16),
             pltpu.VMEM((DEPTH, 128), f32),
             pltpu.VMEM((DEPTH, 128), f32),
-            pltpu.SemaphoreType.DMA((PIECES, 2)),
+            pltpu.SemaphoreType.DMA((len(GROUPS), 2)),
         ],
-        compiler_params=params_for(16),
+        compiler_params=params_for(20),
         name="merge",
     )(*map(stay, decs), scale, near(wide), near(ranks))
 
@@ -461,28 +449,28 @@
     own_b = delta_b.reshape(FULL_B, RANKS).T
     mate_a, mate_b, mate_w = swap(own_a, "c"), swap(own_b, "c"), swap(weights, "c")
     pb, mb, vb = pb.T, mb.T, vb.T
-    near_a, near_b = own_half(own_a, own_b)
+    block = jnp.concatenate([pb, mb, vb, pb], axis=0)
+    other = swap(block, "zh")
+    near_a, near_b = own_deltas(own_a, own_b)
     pairs = pair_sum(weights, mate_w, near_a, mate_a, near_b, mate_b)
-    pairs, codes, pb, mb, vb = lax.optimization_barrier((pairs, codes, pb, mb, vb))
-    got = exchange(pairs.reshape(CHIPS, 16, LANES), ("zl", "y"))
-    block = jnp.concatenate([pb, mb, vb, pb], axis=0)
+    pairs, codes, block, other = lax.optimization_barrier((pairs, codes, block, other))
+    got = exchange(pairs.reshape(CHIPS, 8, LANES), ("zl", "y"))
     for apart in (2, 1):
+        block = jnp.concatenate([block, other], axis=0)
         other = lax.ppermute(block, "x", [(k, k ^ apart) for k in range(4)])
-        block = jnp.concatenate([block, other], axis=0)
-    (top,) = decode(codes, 0, TOP)
-    got, top, block = lax.optimization_barrier((got, top, block))
+    dec_0, *state = decode(codes, 0, ROW_PARTS[0], (pa, ma, va, pb, mb, vb))
+    got, dec_0, block, other, state = lax.optimization_barrier((got, dec_0, block, other, state))
     message = row_sum(got)
-    codes, message, block = lax.optimization_barrier((codes, message, block))
-    got = exchange(message, ("c",) + COL)
-    other = swap(block, "zh")
-    low, *state = decode(codes, TOP, DEPTH - TOP, (pa, ma, va, pb, mb, vb))
-    got, low, state, other = lax.optimization_barrier((got, low, state, other))
-    send, ga, gb = server_step(got, *state[:3])
+    codes, message = lax.optimization_barrier((codes, message))
+    got = exchange(message, COL)
+    (dec_1,) = decode(codes, *ROW_PARTS)
+    got, dec_1 = lax.optimization_barrier((got, dec_1))
+    send, sums = server_step(got, *state[:3])
     ranks = exchange(send, ROW)
     pa_n, ma_n, va_n, pb_n, mb_n, vb_n, wide = server_state(
-        ga, gb, state[:3], state[3:], (block, other)
+        sums, state[:3], state[3:], (block, other)
     )
-    merged, peaks = merge((top, low), scale.reshape(1, DEPTH), wide, ranks)
+    merged, peaks = merge((dec_0, dec_1), scale.reshape(1, DEPTH), wide, ranks)
     out, scales = normalise(merged, exchange(peaks, COL))
     return (out, scales.reshape(DEPTH), pb_n.T, pa_n, mb_n.T, vb_n.T, ma_n, va_n)
 

time: 78.9 us -> 77.1 us (0.977)
  starting transfers between devices: 25.7 us -> 22.6 us
    all_to_all x2, starting transfers between devices: 13.3 us -> 9.83 us  [the longest x1 4.94 us: local(): got = exchange(pairs.reshape(CHIPS, 8, LANES), ('zl', 'y'))]
    all_to_all x2, waiting for transfers between devices: 4.13 us -> 6 us  [the longest x1 4.26 us: local(): got = exchange(message, COL)]
    pallas_call x2, Pallas kernels: 10.3 us -> 11.2 us  [decode(): pl.pallas_call(functools.partial(decode_kernel, first, rows // DEC_ROWS,...]
    ppermute x1, waiting for transfers between devices: 0.95 us -> 0.01 us  [local(): swap(weights, 'c')]
    pallas_call x1, Pallas kernels: 5.38 us -> 4.44 us  [merge(): pl.pallas_call(merge_kernel, out_shape=(pltpu.VMEM((PIECES, DEPTH, PIECE)...]
  transfers between devices with their start and end apart: 9 -> 9, of which waited for: 6 -> 4; matrix products, arithmetic and copies ran while one was open for 1% -> 2% of each run, Pallas kernels for 16% -> 21%
where the time goes in v4:
time: 77.1 us; the launch traced here: 76.7 us
  Pallas kernels  25.7 us (33%)
  starting transfers between devices  22.6 us (29%)
  waiting for transfers between devices  15.4 us (20%)
  blocking collectives  10.9 us (14%)
  other arithmetic  1.44 us (2%)
    pallas_call x2, Pallas kernels, decode(): pl.pallas_call(functools.partial(decode_kernel, first, rows // DEC_ROWS,...  11.2 us
    all_to_all x1, blocking collectives, local(): out, scales = normalise(merged, exchange(peaks, COL))  10.9 us
    all_to_all x1, waiting for transfers between devices, local(): ranks = exchange(send, ROW)  6.95 us
    all_to_all x1, starting transfers between devices, local(): got = exchange(pairs.reshape(CHIPS, 8, LANES), ('zl', 'y'))  4.94 us
    all_to_all x1, starting transfers between devices, local(): got = exchange(message, COL)  4.89 us
    ppermute x2, starting transfers between devices, local(): other = lax.ppermute(block, 'x', [(k, k ^ apart) for k in range(4)])  4.6 us
    pallas_call x1, Pallas kernels, merge(): pl.pallas_call(merge_kernel, out_shape=(pltpu.VMEM((PIECES, DEPTH, PIECE)...  4.44 us
    all_to_all x1, waiting for transfers between devices, local(): got = exchange(message, COL)  4.26 us
  transfers between devices with their start and end apart: 9, of which 4 were waited for; matrix products, arithmetic and copies ran while one was open for 2% of the time, Pallas kernels for 21%

profile of v4, /device:TPU:0, one launch (start us, length us, event | category | flops | bytes accessed | tf_op | source)
XLA Modules:
  0.0 76.7 jit_solution(3684245183299005043)
XLA Ops:
  0.6 0.1 collective-permute-start.1
  0.7 0.5 collective-permute-start.2
  1.2 0.8 %pad_maximum_fusion.1 = f32[8,512]{1,0:T(8,128)S(1)} fusion(f32[2,512]{1,0:T(2,128)} %bitcast.19, f32[2,512]{1,0:T(2,128)} %bitcast.23, f32[2,512]{1,0:T(2,128)} %bitcast.21), kind=kLoop, calls=%fused_computation.1 | loop fusion | flops 12288 | bytes 28672 | tf_op jit(solution)/shard_map/concatenate | solution.py:452
  2.0 4.0 %collective-permute-start.3 = (f32[8,512]{1,0:T(8,128)S(1)}, f32[8,512]{1,0:T(8,128)S(1)}, u32[]{:S(2)}, u32[]{:S(2)}) collective-permute-start(f32[8,512]{1,0:T(8,128)S(1)} %pad_maximum_fusion.1), channel_id=1, source_target_pairs={{0,1},{1,0},{2,3},{3,2},{4,5},{5,4},{6,7},{7,6},{8,9},{9,8},{10,11... | collective-permute-start | bytes 49160 | tf_op jit(solution)/shard_map/ppermute | solution.py:453
  6.0 0.7 convert_multiply_fusion.own_w
  6.7 0.0 collective-permute-start
  6.7 1.7 %own_deltas.1 = (bf16[128,6656]{1,0:T(8,128)(2,1)S(1)}, bf16[16,8192]{1,0:T(8,128)(2,1)S(1)}) custom-call(bf16[16,53248]{1,0:T(8,128)(2,1)} %bitcast.16, bf16[16,8192]{1,0:T(8,128)(2,1)} %bitcast.18), custom_call_target="tpu_custom_call" | custom-call | tf_op jit(solution)/shard_map/own_deltas/pallas_call | solution.py:175
  8.4 0.0 collective-permute-done.mate_w
  8.4 0.0 collective-permute-done.2.mate_b
  8.4 0.0 collective-permute-done.1.mate_a
  8.4 2.1 %pair_sum.1 = bf16[64,7680]{1,0:T(8,128)(2,1)} custom-call(f32[1,2]{1,0:T(1,128)S(1)} %convert_multiply_fusion.own_w, f32[1,2]{1,0:T(1,128)S(1)} %collective-permute-done.mate_w, bf16[128,6656]{1,0:T(8,128)(2,1)S(1)} %get-tuple-element.48.own_a, bf16[16,53248]{1,0:T(8,128)(2,1)S(1)} %collective-permute-done.1.mate_a, ...), custom_call_target="tpu_custom_call" | custom-call | tf_op jit(solution)/shard_map/pair_sum/pallas_call | solution.py:222
  10.5 0.0 collective-permute-done.3
  10.5 4.9 %all-to-all-start = ((bf16[8,8,7680]{2,1,0:T(8,128)(2,1)}), bf16[8,8,7680]{2,1,0:T(8,128)(2,1)S(1)}, u32[]{:S(2)}, u32[]{:S(2)}) async-start(bf16[8,8,7680]{2,1,0:T(8,128)(2,1)} %bitcast.14), calls=%async_computation | async-start | bytes 1966080 | tf_op jit(solution)/shard_map/all_to_all | solution.py:457
  15.4 3.1 %collective-permute-start.4 = (f32[16,512]{1,0:T(8,128)S(1)}, f32[16,512]{1,0:T(8,128)S(1)}, u32[]{:S(2)}, u32[]{:S(2)}) collective-permute-start(f32[16,512]{1,0:T(8,128)S(1)} %pad_maximum_fusion), channel_id=1, source_target_pairs={{0,4},{2,6},{4,0},{6,2},{1,5},{3,7},{5,1},{7,3},{8,12},{10,14},{12... | collective-permute-start | bytes 98312 | tf_op jit(solution)/shard_map/ppermute | solution.py:460
  18.6 2.4 %collective-permute-done.4 = f32[16,512]{1,0:T(8,128)S(1)} collective-permute-done((f32[16,512]{1,0:T(8,128)S(1)}, f32[16,512]{1,0:T(8,128)S(1)}, u32[]{:S(2)}, u32[]{:S(2)}) %collective-permute-start.4) | collective-permute-done | bytes 32800 | tf_op jit(solution)/shard_map/ppermute | solution.py:460
  21.0 1.5 %collective-permute-start.5 = (f32[32,512]{1,0:T(8,128)S(1)}, f32[32,512]{1,0:T(8,128)S(1)}, u32[]{:S(2)}, u32[]{:S(2)}) collective-permute-start(f32[32,512]{1,0:T(8,128)S(1)} %constant_dynamic-update-slice_fusion.col_0), channel_id=1, source_target_pairs={{0,2},{2,0},{4,6},{6,4},{1,3},{3,1},{5,7},{7,5},{8,10},{10,8},{12,... | collective-permute-start | bytes 196616 | tf_op jit(solution)/shard_map/ppermute | solution.py:460
  22.4 6.9 %decode.2 = (bf16[352,6656]{1,0:T(8,128)(2,1)}, f32[16,512]{1,0:T(8,128)S(1)}, f32[16,512]{1,0:T(8,128)S(1)}, f32[16,512]{1,0:T(8,128)S(1)}, f32[2,512]{1,0:T(2,...) custom-call(s32[512,6656]{1,0:T(8,128)} %refs_0_.1, f32[1,6656]{1,0:T(1,128)} %refs_1_.1, f32[1,6656]{1,0:T(1,128)} %refs_2_.1, ...), custom_call_target="tpu_custom_call" | custom-call | flops 20000000 | bytes 12000000 | tf_op jit(solution)/shard_map/decode/pallas_call | solution.py:143
  29.4 0.0 collective-permute-done.5.col_1
  29.4 1.7 %all-to-all-done.got = bf16[8,8,7680]{2,1,0:T(8,128)(2,1)S(1)} async-done(((bf16[8,8,7680]{2,1,0:T(8,128)(2,1)}), bf16[8,8,7680]{2,1,0:T(8,128)(2,1)S(1)}, u32[]{:S(2)}, u32[]{:S(2)}) %all-to-all-start) | async-done | bytes 983072 | tf_op jit(solution)/shard_map/all_to_all | solution.py:457
  31.1 0.9 %row_sum.1 = bf16[8,32,512]{2,1,0:T(8,128)(2,1)} custom-call(bf16[8,8,7680]{2,1,0:T(8,128)(2,1)S(1)} %all-to-all-done.got), custom_call_target="tpu_custom_call" | custom-call | tf_op jit(solution)/shard_map/row_sum/pallas_call | solution.py:250
  32.1 4.9 %all-to-all-start.1 = ((bf16[8,32,512]{2,1,0:T(8,128)(2,1)}), bf16[8,32,512]{2,1,0:T(8,128)(2,1)S(1)}, u32[]{:S(2)}, u32[]{:S(2)}) async-start(bf16[8,32,512]{2,1,0:T(8,128)(2,1)} %row_sum.1), calls=%async_computation.1 | async-start | bytes 524288 | tf_op jit(solution)/shard_map/all_to_all | solution.py:465
  37.0 0.0 copy-start
  37.0 4.3 %decode.3.dec_1 = bf16[160,6656]{1,0:T(8,128)(2,1)} custom-call(s32[512,6656]{1,0:T(8,128)} %refs_0_.1), custom_call_target="tpu_custom_call" | custom-call | flops 20000000 | bytes 12000000 | tf_op jit(solution)/shard_map/decode/pallas_call | solution.py:143
  41.3 4.3 %all-to-all-done.1.got = bf16[8,32,512]{2,1,0:T(8,128)(2,1)S(1)} async-done(((bf16[8,32,512]{2,1,0:T(8,128)(2,1)}), bf16[8,32,512]{2,1,0:T(8,128)(2,1)S(1)}, u32[]{:S(2)}, u32[]{:S(2)}) %all-to-all-start.1) | async-done | bytes 262176 | tf_op jit(solution)/shard_map/all_to_all | solution.py:465
  45.6 0.8 server_step.1
  46.3 3.5 %all-to-all-start.2 = ((bf16[16,16,512]{2,1,0:T(8,128)(2,1)}), bf16[16,16,512]{2,1,0:T(8,128)(2,1)S(1)}, u32[]{:S(2)}, u32[]{:S(2)}) async-start(bf16[16,16,512]{2,1,0:T(8,128)(2,1)} %get-tuple-element.77), calls=%async_computation.2 | async-start | bytes 524288 | tf_op jit(solution)/shard_map/all_to_all | solution.py:469
  49.9 0.9 %server_state.1 = (f32[1,6656]{1,0:T(1,128)}, f32[1,6656]{1,0:T(1,128)}, f32[1,6656]{1,0:T(1,128)}, f32[2,512]{1,0:T(2,128)}, f32[2,512]{1,0:T(2,128)}, /*index=5*/f32[2,512]{1,0:T(2,128)}, bf16[512,256]{1,0:T(8,128)(2,1)S(1)}) custom-call(f32[32,512]{1,0:T(8,128)S(1)} %get-tuple-element.70.sums, f32[16,512]{1,0:T(8,128)S(1)} %get-tuple-element.67.pa, ...), custom_call_target="tpu_custom_call" | custom-call | tf_op jit(solution)/shard_map/server_state/pallas_call | solution.py:319
  50.7 7.0 %all-to-all-done.2.ranks = bf16[16,16,512]{2,1,0:T(8,128)(2,1)S(1)} async-done(((bf16[16,16,512]{2,1,0:T(8,128)(2,1)}), bf16[16,16,512]{2,1,0:T(8,128)(2,1)S(1)}, u32[]{:S(2)}, u32[]{:S(2)}) %all-to-all-start.2) | async-done | bytes 262176 | tf_op jit(solution)/shard_map/all_to_all | solution.py:469
  57.7 0.0 copy-done
  57.7 4.4 %merge.1 = (f32[13,512,512]{2,1,0:T(8,128)S(1)}, f32[8,1,512]{2,1,0:T(1,128)S(1)}) custom-call(bf16[352,6656]{1,0:T(8,128)(2,1)} %get-tuple-element.61.dec_0, bf16[160,6656]{1,0:T(8,128)(2,1)} %decode.3.dec_1, f32[1,512]{1,0:T(1,128)S(1)} %bitcast.13, bf16[512,256]{1,0:T(8,128)(2,1)S(1)} %get-tuple-element.76.wide, bf16[16,16,512]{2,1,0:T(8,128)(2,1)S(1)} %all-to-all-done.2.ranks), custom_call_target="tpu_custom_call" | custom-call | tf_op jit(solution)/shard_map/merge/pallas_call | solution.py:371
  62.2 10.9 %all_to_all.20.peaks = f32[8,1,512]{2,1,0:T(1,128)S(1)} all-to-all(f32[8,1,512]{2,1,0:T(1,128)S(1)} %get-tuple-element.79), channel_id=1, replica_groups=mesh['zl'=2,'y'=4,'c'=2,'x'=4,'zh'=2] {'x','zh'}, dimensions={0} | all-to-all | bytes 32768 | tf_op jit(solution)/shard_map/all_to_all | solution.py:474
  73.0 3.6 %normalise.1 = (bf16[512,6656]{1,0:T(8,128)(2,1)}, f32[1,512]{1,0:T(1,128)}) custom-call(f32[13,512,512]{2,1,0:T(8,128)S(1)} %get-tuple-element.78.merged, f32[8,1,512]{2,1,0:T(1,128)S(1)} %all_to_all.20.peaks), custom_call_target="tpu_custom_call" | custom-call | tf_op jit(solution)/shard_map/normalise/pallas_call | solution.py:429
  (4 shorter events, 0.0 us)
Async XLA Ops:
  0.6 7.8 %collective-permute-start.1 = (bf16[16,53248]{1,0:T(8,128)(2,1)}, bf16[16,53248]{1,0:T(8,128)(2,1)S(1)}, u32[]{:S(2)}, u32[]{:S(2)}) collective-permute-start(bf16[16,53248]{1,0:T(8,128)(2,1)} %bitcast.15), channel_id=1, source_target_pairs={{0,8},{8,0},{1,9},{9,1},{2,10},{10,2},{3,11},{11,3},{4,12},{12,4},... | collective-permute-start | bytes 5111816 | tf_op jit(solution)/shard_map/ppermute | solution.py:450
  0.7 7.7 %collective-permute-start.2 = (bf16[16,8192]{1,0:T(8,128)(2,1)}, bf16[16,8192]{1,0:T(8,128)(2,1)S(1)}, u32[]{:S(2)}, u32[]{:S(2)}) collective-permute-start(bf16[16,8192]{1,0:T(8,128)(2,1)} %bitcast.17), channel_id=1, source_target_pairs={{0,8},{8,0},{1,9},{9,1},{2,10},{10,2},{3,11},{11,3},{4,12},{12,4},... | collective-permute-start | bytes 786440 | tf_op jit(solution)/shard_map/ppermute | solution.py:450
  2.0 8.5 %collective-permute-start.3 = (f32[8,512]{1,0:T(8,128)S(1)}, f32[8,512]{1,0:T(8,128)S(1)}, u32[]{:S(2)}, u32[]{:S(2)}) collective-permute-start(f32[8,512]{1,0:T(8,128)S(1)} %pad_maximum_fusion.1), channel_id=1, source_target_pairs={{0,1},{1,0},{2,3},{3,2},{4,5},{5,4},{6,7},{7,6},{8,9},{9,8},{10,11... | collective-permute-start | bytes 49160 | tf_op jit(solution)/shard_map/ppermute | solution.py:453
  6.7 1.7 %collective-permute-start = (f32[1,2]{1,0:T(1,128)S(1)}, f32[1,2]{1,0:T(1,128)S(1)}, u32[]{:S(2)}, u32[]{:S(2)}) collective-permute-start(f32[1,2]{1,0:T(1,128)S(1)} %convert_multiply_fusion.own_w), channel_id=1, source_target_pairs={{0,8},{8,0},{1,9},{9,1},{2,10},{10,2},{3,11},{11,3},{4,12},{12,4},... | collective-permute-start | bytes 32 | tf_op jit(solution)/shard_map/ppermute | solution.py:450
  10.5 20.6 %all-to-all-start = ((bf16[8,8,7680]{2,1,0:T(8,128)(2,1)}), bf16[8,8,7680]{2,1,0:T(8,128)(2,1)S(1)}, u32[]{:S(2)}, u32[]{:S(2)}) async-start(bf16[8,8,7680]{2,1,0:T(8,128)(2,1)} %bitcast.14), calls=%async_computation | async-start | bytes 1966080 | tf_op jit(solution)/shard_map/all_to_all | solution.py:457
  15.4 5.5 %collective-permute-start.4 = (f32[16,512]{1,0:T(8,128)S(1)}, f32[16,512]{1,0:T(8,128)S(1)}, u32[]{:S(2)}, u32[]{:S(2)}) collective-permute-start(f32[16,512]{1,0:T(8,128)S(1)} %pad_maximum_fusion), channel_id=1, source_target_pairs={{0,4},{2,6},{4,0},{6,2},{1,5},{3,7},{5,1},{7,3},{8,12},{10,14},{12... | collective-permute-start | bytes 98312 | tf_op jit(solution)/shard_map/ppermute | solution.py:460
  21.0 8.4 %collective-permute-start.5 = (f32[32,512]{1,0:T(8,128)S(1)}, f32[32,512]{1,0:T(8,128)S(1)}, u32[]{:S(2)}, u32[]{:S(2)}) collective-permute-start(f32[32,512]{1,0:T(8,128)S(1)} %constant_dynamic-update-slice_fusion.col_0), channel_id=1, source_target_pairs={{0,2},{2,0},{4,6},{6,4},{1,3},{3,1},{5,7},{7,5},{8,10},{10,8},{12,... | collective-permute-start | bytes 196616 | tf_op jit(solution)/shard_map/ppermute | solution.py:460
  32.1 13.5 %all-to-all-start.1 = ((bf16[8,32,512]{2,1,0:T(8,128)(2,1)}), bf16[8,32,512]{2,1,0:T(8,128)(2,1)S(1)}, u32[]{:S(2)}, u32[]{:S(2)}) async-start(bf16[8,32,512]{2,1,0:T(8,128)(2,1)} %row_sum.1), calls=%async_computation.1 | async-start | bytes 524288 | tf_op jit(solution)/shard_map/all_to_all | solution.py:465
  37.0 20.8 %copy-start = (f32[512]{0:T(512)S(1)}, f32[512]{0:T(512)}, u32[]{:S(2)}) copy-start(f32[512]{0:T(512)} %param.12) | copy-start | bytes 6148
  46.3 11.4 %all-to-all-start.2 = ((bf16[16,16,512]{2,1,0:T(8,128)(2,1)}), bf16[16,16,512]{2,1,0:T(8,128)(2,1)S(1)}, u32[]{:S(2)}, u32[]{:S(2)}) async-start(bf16[16,16,512]{2,1,0:T(8,128)(2,1)} %get-tuple-element.77), calls=%async_computation.2 | async-start | bytes 524288 | tf_op jit(solution)/shard_map/all_to_all | solution.py:469

commit v5 on v4

--- a/solution.py
+++ b/solution.py
@@ -20,6 +20,7 @@
 SDS = jax.ShapeDtypeStruct
 
 ROW, COL = ("zl", "y", "c"), ("x", "zh")
+CLIENTS = 128
 CHIPS, COLS = 8, 8
 RANKS = 16
 DEPTH, WIDTH = 512, 6656
@@ -64,13 +65,9 @@
     return pl.BlockSpec(memory_space=pltpu.VMEM)
 
 
-def in_smem():
-    return pl.BlockSpec(memory_space=pltpu.SMEM)
-
-
 DEC_ROWS = 32
 SLOTS = 6
-ROW_PARTS = (352, 160)
+ROW_PARTS = (320, 192)
 
 
 def decode_kernel(first, steps, count, *refs):
@@ -158,8 +155,8 @@
     )(stay(codes), *[stay(x) for x in state])
 
 
-def own_kernel(a, b, xa, xb, sem_a, sem_b):
-    moves = [pltpu.make_async_copy(b, xb, sem_b)] + [
+def own_kernel(n, a, b, xn, xa, xb, sem_a, sem_b, sem_n):
+    moves = [pltpu.make_async_copy(b, xb, sem_b), pltpu.make_async_copy(n, xn, sem_n)] + [
         pltpu.make_async_copy(
             a.at[:, pl.ds(c * WIDTH, WIDTH)], xa.at[pl.ds(c * RANKS, RANKS), :], sem_a.at[c]
         )
@@ -171,33 +168,35 @@
         move.wait()
 
 
-def own_deltas(a, b):
+def own_deltas(n, a, b):
     return pl.pallas_call(
         own_kernel,
-        out_shape=(kept((128, WIDTH), bf16), kept((RANKS, FULL_B), bf16)),
-        in_specs=[in_hbm()] * 2,
-        out_specs=(in_vmem(),) * 2,
-        scratch_shapes=[pltpu.SemaphoreType.DMA((COLS,)), pltpu.SemaphoreType.DMA],
+        out_shape=(kept((1, 2), i32), kept((128, WIDTH), bf16), kept((RANKS, FULL_B), bf16)),
+        in_specs=[in_hbm()] * 3,
+        out_specs=(in_vmem(),) * 3,
+        scratch_shapes=[pltpu.SemaphoreType.DMA((COLS,))] + [pltpu.SemaphoreType.DMA] * 2,
         compiler_params=params_for(8),
         name="own_deltas",
-    )(stay(a), stay(b))
+    )(stay(n), stay(a), stay(b))
 
 
 CHUNKS = (1536, 1536, 1536, 2048)
 
 
-def pair_kernel(own_w, mate_w, own_a, mate_a, own_b, mate_b, out, buf, sems):
+def pair_kernel(own_n, mate_n, own_a, mate_a, own_b, mate_b, out, buf, sems):
     core = lax.axis_index("c")
 
     def store(n, start, width):
         here = pl.ds(start, width)
         return pltpu.make_async_copy(buf.at[:, here], out.at[:, here], sems.at[n])
 
+    weights = [n[...].astype(f32) / (count_scale * CLIENTS) for n in (own_n, mate_n)]
+    own_w, mate_w = ((w[:, 0:1], w[:, 1:2]) for w in weights)
     o = lax.broadcasted_iota(i32, (64, 256), 0)
     k = lax.broadcasted_iota(i32, (64, 256), 1)
     same_block = jnp.bitwise_and(o, 7) == jnp.bitwise_and(lax.shift_right_logical(k, 4), 7)
     same_rank = lax.shift_right_logical(o, 3) * 2 + core == jnp.bitwise_and(k, 15)
-    weight = jnp.where(k < 128, own_w[0, 1], mate_w[0, 1])
+    weight = jnp.where(k < 128, own_w[1], mate_w[1])
     pick = jnp.where(jnp.logical_and(same_block, same_rank), weight, 0.0).astype(bf16)
     start = 0
     for n, width in enumerate(CHUNKS):
@@ -208,7 +207,7 @@
         start += width
     for j in range(CHIPS):
         at = pl.ds(pl.multiple_of((2 * j + core) * DEPTH, DEPTH), DEPTH)
-        both = own_w[0, 0] * own_b[:, at].astype(f32) + mate_w[0, 0] * mate_b[:, at].astype(f32)
+        both = own_w[0] * own_b[:, at].astype(f32) + mate_w[0] * mate_b[:, at].astype(f32)
         both = jnp.concatenate([both[0:8, :], both[8:16, :]], axis=1)
         buf[pl.ds(j * 8, 8), pl.ds(WIDTH, 2 * DEPTH)] = both.astype(bf16)
     store(len(CHUNKS), WIDTH, 2 * DEPTH).start()
@@ -218,11 +217,11 @@
         start += width
 
 
-def pair_sum(own_w, mate_w, own_a, mate_a, own_b, mate_b):
+def pair_sum(own_n, mate_n, own_a, mate_a, own_b, mate_b):
     return pl.pallas_call(
         pair_kernel,
         out_shape=pltpu.HBM((CHIPS * 8, LANES), bf16),
-        in_specs=[in_smem()] * 2 + [in_vmem()] * 4,
+        in_specs=[in_vmem()] * 6,
         out_specs=in_hbm(),
         scratch_shapes=[
             pltpu.VMEM((CHIPS * 8, LANES), bf16),
@@ -230,7 +229,7 @@
         ],
         compiler_params=params_for(16),
         name="pair_sum",
-    )(own_w, mate_w, *map(near, (own_a, mate_a, own_b, mate_b)))
+    )(*map(near, (own_n, mate_n, own_a, mate_a, own_b, mate_b)))
 
 
 def row_kernel(got, out, scr):
@@ -266,14 +265,14 @@
     pn = adaptive_update(pa[...], ma[...], va[...], total[0:16, :])[0]
     row = lax.broadcasted_iota(i32, pn.shape, 0)
     message = jnp.where(row < PIECES, pn, 0.0).astype(bf16)
-    for d in range(16):
+    for d in range(CHIPS):
         send[d] = message
 
 
 def server_step(got, pa, ma, va):
     return pl.pallas_call(
         step_kernel,
-        out_shape=(SDS((16, 16, PIECE), bf16), kept((32, PIECE))),
+        out_shape=(SDS((CHIPS, 16, PIECE), bf16), kept((32, PIECE))),
         in_specs=[in_vmem()] * 4,
         out_specs=(in_vmem(),) * 2,
         compiler_params=params_for(16),
@@ -298,7 +297,10 @@
     full = adaptive_update(*whole, grad)[0]
     k = lax.broadcasted_iota(i32, (RANKS, 256), 1)
     r = lax.broadcasted_iota(i32, (RANKS, 256), 0)
-    repeat = jnp.where(lax.shift_right_logical(k, 4) == r, adapter_scale, 0.0).astype(bf16)
+    core = lax.axis_index("c")
+    parity = jnp.bitwise_xor(lax.shift_right_logical(k, 7), core)
+    rank = jnp.bitwise_and(lax.shift_right_logical(k, 4), 7) * 2 + parity
+    repeat = jnp.where(rank == r, adapter_scale, 0.0).astype(bf16)
     tall = jnp.transpose(full).astype(bf16)
     wide[...] = jnp.dot(tall, repeat, preferred_element_type=f32).astype(bf16)
     own = [
@@ -330,7 +332,7 @@
 GROUPS = (1, 2, 4, 6)
 
 
-def merge_kernel(dec_0, dec_1, scale, wide, ranks, merged, peaks, buf, row_scale, tops, sems):
+def merge_kernel(dec_0, dec_1, scale, wide, ranks, mate_ranks, merged, peaks, buf, row_scale, tops, sems):
     fetches, piece = [], 0
     for n, count in enumerate(GROUPS):
         here = pl.ds(piece * PIECE, count * PIECE)
@@ -344,7 +346,7 @@
         piece += count
     row_scale[...] = jnp.transpose(jnp.broadcast_to(scale[...] * 2.0**-10, (128, DEPTH)))
     lane = jnp.bitwise_and(lax.broadcasted_iota(i32, (DEPTH, 256), 1), 15)
-    right = ranks[...].reshape(256, PIECE)
+    right = jnp.concatenate([r[...].reshape(128, PIECE) for r in (ranks, mate_ranks)], axis=0)
     tops[...] = jnp.zeros_like(tops)
     piece = 0
     for n, count in enumerate(GROUPS):
@@ -367,11 +369,11 @@
         peaks[c] = peak
 
 
-def merge(decs, scale, wide, ranks):
+def merge(decs, scale, wide, ranks, mate_ranks):
     return pl.pallas_call(
         merge_kernel,
         out_shape=(pltpu.VMEM((PIECES, DEPTH, PIECE), f32), SDS((COLS, 1, DEPTH), f32)),
-        in_specs=[in_hbm()] * 2 + [in_vmem()] * 3,
+        in_specs=[in_hbm()] * 2 + [in_vmem()] * 4,
         out_specs=(in_vmem(), in_vmem()),
         scratch_shapes=[
             pltpu.VMEM((DEPTH, WIDTH), bf16),
@@ -381,7 +383,7 @@
         ],
         compiler_params=params_for(20),
         name="merge",
-    )(*map(stay, decs), scale, near(wide), near(ranks))
+    )(*map(stay, decs), scale, near(wide), near(ranks), near(mate_ranks))
 
 
 OUT_ROWS = 32
@@ -444,15 +446,14 @@
 def local(codes, scale, pb, pa, mb, vb, ma, va, delta_b, delta_a, tallies):
     exchange = functools.partial(lax.all_to_all, split_axis=0, concat_axis=0, tiled=True)
     swap = functools.partial(lax.ppermute, perm=[(0, 1), (1, 0)])
-    weights = tallies.astype(f32) / (count_scale * 128)
     own_a = delta_a.reshape(RANKS, FULL_A)
     own_b = delta_b.reshape(FULL_B, RANKS).T
-    mate_a, mate_b, mate_w = swap(own_a, "c"), swap(own_b, "c"), swap(weights, "c")
+    mate_a, mate_b, mate_n = swap(own_a, "c"), swap(own_b, "c"), swap(tallies, "c")
     pb, mb, vb = pb.T, mb.T, vb.T
     block = jnp.concatenate([pb, mb, vb, pb], axis=0)
     other = swap(block, "zh")
-    near_a, near_b = own_deltas(own_a, own_b)
-    pairs = pair_sum(weights, mate_w, near_a, mate_a, near_b, mate_b)
+    own_n, own_a, own_b = own_deltas(tallies, own_a, own_b)
+    pairs = pair_sum(own_n, mate_n, own_a, mate_a, own_b, mate_b)
     pairs, codes, block, other = lax.optimization_barrier((pairs, codes, block, other))
     got = exchange(pairs.reshape(CHIPS, 8, LANES), ("zl", "y"))
     for apart in (2, 1):
@@ -466,11 +467,11 @@
     (dec_1,) = decode(codes, *ROW_PARTS)
     got, dec_1 = lax.optimization_barrier((got, dec_1))
     send, sums = server_step(got, *state[:3])
-    ranks = exchange(send, ROW)
+    ranks = exchange(send, ("zl", "y"))
     pa_n, ma_n, va_n, pb_n, mb_n, vb_n, wide = server_state(
         sums, state[:3], state[3:], (block, other)
     )
-    merged, peaks = merge((dec_0, dec_1), scale.reshape(1, DEPTH), wide, ranks)
+    merged, peaks = merge((dec_0, dec_1), scale.reshape(1, DEPTH), wide, ranks, swap(ranks, "c"))
     out, scales = normalise(merged, exchange(peaks, COL))
     return (out, scales.reshape(DEPTH), pb_n.T, pa_n, mb_n.T, vb_n.T, ma_n, va_n)
 

time: 77.1 us -> 76.1 us (0.987)
  blocking collectives: 10.9 us -> 21.6 us
  waiting for transfers between devices: 15.4 us -> 8.83 us
  starting transfers between devices: 22.6 us -> 19.2 us
  Pallas kernels: 25.7 us -> 24.5 us
    all_to_all x0 -> x1, blocking collectives: none -> 10.1 us  [local(): ranks = exchange(send, ('zl', 'y'))]
    all_to_all x1 -> x0, waiting for transfers between devices: 6.95 us -> none  [local(): ranks = exchange(send, ROW)]
    all_to_all x1 -> x0, starting transfers between devices: 3.53 us -> none  [local(): ranks = exchange(send, ROW)]
  transfers between devices with their start and end apart: 9 -> 9, of which waited for: 4 -> 4; matrix products, arithmetic and copies ran while one was open for 2% -> 1% of each run, Pallas kernels for 21% -> 20%
where the time goes in v5:
time: 76.1 us; the launch traced here: 75.7 us
  Pallas kernels  24.5 us (32%)
  blocking collectives  21.6 us (28%)
  starting transfers between devices  19.2 us (25%)
  waiting for transfers between devices  8.83 us (12%)
  other arithmetic  0.78 us (1%)
    all_to_all x1, blocking collectives, local(): out, scales = normalise(merged, exchange(peaks, COL))  11.6 us
    pallas_call x2, Pallas kernels, decode(): pl.pallas_call(functools.partial(decode_kernel, first, rows // DEC_ROWS,...  11.2 us
    all_to_all x1, blocking collectives, local(): ranks = exchange(send, ('zl', 'y'))  10.1 us
    all_to_all x1, starting transfers between devices, local(): got = exchange(message, COL)  5.07 us
    all_to_all x1, starting transfers between devices, local(): got = exchange(pairs.reshape(CHIPS, 8, LANES), ('zl', 'y'))  4.93 us
    ppermute x2, starting transfers between devices, local(): other = lax.ppermute(block, 'x', [(k, k ^ apart) for k in range(4)])  4.6 us
    pallas_call x1, Pallas kernels, merge(): pl.pallas_call(merge_kernel, out_shape=(pltpu.VMEM((PIECES, DEPTH, PIECE)...  4.47 us
    ppermute x1, starting transfers between devices, local(): other = swap(block, 'zh')  4.04 us
  transfers between devices with their start and end apart: 9, of which 4 were waited for; matrix products, arithmetic and copies ran while one was open for 1% of the time, Pallas kernels for 20%

profile of v5, /device:TPU:0, one launch (start us, length us, event | category | flops | bytes accessed | tf_op | source)
XLA Modules:
  0.0 75.7 jit_solution(7783075704457079846)
XLA Ops:
  0.6 0.1 collective-permute-start.1
  0.7 0.5 collective-permute-start.2
  1.2 0.8 %pad_maximum_fusion.1 = f32[8,512]{1,0:T(8,128)S(1)} fusion(f32[2,512]{1,0:T(2,128)} %bitcast.19, f32[2,512]{1,0:T(2,128)} %bitcast.23, f32[2,512]{1,0:T(2,128)} %bitcast.21), kind=kLoop, calls=%fused_computation.1 | loop fusion | flops 12288 | bytes 28672 | tf_op jit(solution)/shard_map/concatenate | solution.py:453
  2.0 4.0 %collective-permute-start.3 = (f32[8,512]{1,0:T(8,128)S(1)}, f32[8,512]{1,0:T(8,128)S(1)}, u32[]{:S(2)}, u32[]{:S(2)}) collective-permute-start(f32[8,512]{1,0:T(8,128)S(1)} %pad_maximum_fusion.1), channel_id=1, source_target_pairs={{0,1},{1,0},{2,3},{3,2},{4,5},{5,4},{6,7},{7,6},{8,9},{9,8},{10,11... | collective-permute-start | bytes 49160 | tf_op jit(solution)/shard_map/ppermute | solution.py:454
  6.0 0.0 collective-permute-start
  6.0 1.7 %own_deltas.1 = (s32[1,2]{1,0:T(1,128)S(1)}, bf16[128,6656]{1,0:T(8,128)(2,1)S(1)}, bf16[16,8192]{1,0:T(8,128)(2,1)S(1)}) custom-call(s32[1,2]{1,0:T(1,128)} %n.1, bf16[16,53248]{1,0:T(8,128)(2,1)} %bitcast.16, bf16[16,8192]{1,0:T(8,128)(2,1)} %bitcast.18), custom_call_target="tpu_custom_call" | custom-call | tf_op jit(solution)/shard_map/own_deltas/pallas_call | solution.py:172
  7.7 0.0 collective-permute-done.mate_n
  7.7 0.0 collective-permute-done.2.mate_b
  7.7 0.0 collective-permute-done.1.mate_a
  7.8 1.6 %pair_sum.1 = bf16[64,7680]{1,0:T(8,128)(2,1)} custom-call(s32[1,2]{1,0:T(1,128)S(1)} %get-tuple-element.49.own_n, s32[1,2]{1,0:T(1,128)S(1)} %collective-permute-done.mate_n, bf16[128,6656]{1,0:T(8,128)(2,1)S(1)} %get-tuple-element.50.own_a, bf16[16,53248]{1,0:T(8,128)(2,1)S(1)} %collective-permute-done.1.mate_a, ...), custom_call_target="tpu_custom_call" | custom-call | tf_op jit(solution)/shard_map/pair_sum/pallas_call | solution.py:221
  9.4 0.0 collective-permute-done.3
  9.4 4.9 %all-to-all-start = ((bf16[8,8,7680]{2,1,0:T(8,128)(2,1)}), bf16[8,8,7680]{2,1,0:T(8,128)(2,1)S(1)}, u32[]{:S(2)}, u32[]{:S(2)}) async-start(bf16[8,8,7680]{2,1,0:T(8,128)(2,1)} %bitcast.14), calls=%async_computation | async-start | bytes 1966080 | tf_op jit(solution)/shard_map/all_to_all | solution.py:458
  14.3 3.1 %collective-permute-start.4 = (f32[16,512]{1,0:T(8,128)S(1)}, f32[16,512]{1,0:T(8,128)S(1)}, u32[]{:S(2)}, u32[]{:S(2)}) collective-permute-start(f32[16,512]{1,0:T(8,128)S(1)} %pad_maximum_fusion), channel_id=1, source_target_pairs={{0,4},{2,6},{4,0},{6,2},{1,5},{3,7},{5,1},{7,3},{8,12},{10,14},{12... | collective-permute-start | bytes 98312 | tf_op jit(solution)/shard_map/ppermute | solution.py:461
  17.4 2.4 %collective-permute-done.4 = f32[16,512]{1,0:T(8,128)S(1)} collective-permute-done((f32[16,512]{1,0:T(8,128)S(1)}, f32[16,512]{1,0:T(8,128)S(1)}, u32[]{:S(2)}, u32[]{:S(2)}) %collective-permute-start.4) | collective-permute-done | bytes 32800 | tf_op jit(solution)/shard_map/ppermute | solution.py:461
  19.8 1.5 %collective-permute-start.5 = (f32[32,512]{1,0:T(8,128)S(1)}, f32[32,512]{1,0:T(8,128)S(1)}, u32[]{:S(2)}, u32[]{:S(2)}) collective-permute-start(f32[32,512]{1,0:T(8,128)S(1)} %constant_dynamic-update-slice_fusion.col_0), channel_id=1, source_target_pairs={{0,2},{2,0},{4,6},{6,4},{1,3},{3,1},{5,7},{7,5},{8,10},{10,8},{12,... | collective-permute-start | bytes 196616 | tf_op jit(solution)/shard_map/ppermute | solution.py:461
  21.3 6.5 %decode.2 = (bf16[320,6656]{1,0:T(8,128)(2,1)}, f32[16,512]{1,0:T(8,128)S(1)}, f32[16,512]{1,0:T(8,128)S(1)}, f32[16,512]{1,0:T(8,128)S(1)}, f32[2,512]{1,0:T(2,...) custom-call(s32[512,6656]{1,0:T(8,128)} %refs_0_.1, f32[1,6656]{1,0:T(1,128)} %refs_1_.1, f32[1,6656]{1,0:T(1,128)} %refs_2_.1, ...), custom_call_target="tpu_custom_call" | custom-call | flops 20000000 | bytes 12000000 | tf_op jit(solution)/shard_map/decode/pallas_call | solution.py:140
  27.8 0.0 collective-permute-done.5.col_1
  27.9 2.1 %all-to-all-done.got = bf16[8,8,7680]{2,1,0:T(8,128)(2,1)S(1)} async-done(((bf16[8,8,7680]{2,1,0:T(8,128)(2,1)}), bf16[8,8,7680]{2,1,0:T(8,128)(2,1)S(1)}, u32[]{:S(2)}, u32[]{:S(2)}) %all-to-all-start) | async-done | bytes 983072 | tf_op jit(solution)/shard_map/all_to_all | solution.py:458
  30.0 1.0 %row_sum.1 = bf16[8,32,512]{2,1,0:T(8,128)(2,1)} custom-call(bf16[8,8,7680]{2,1,0:T(8,128)(2,1)S(1)} %all-to-all-done.got), custom_call_target="tpu_custom_call" | custom-call | tf_op jit(solution)/shard_map/row_sum/pallas_call | solution.py:249
  30.9 5.1 %all-to-all-start.1 = ((bf16[8,32,512]{2,1,0:T(8,128)(2,1)}), bf16[8,32,512]{2,1,0:T(8,128)(2,1)S(1)}, u32[]{:S(2)}, u32[]{:S(2)}) async-start(bf16[8,32,512]{2,1,0:T(8,128)(2,1)} %row_sum.1), calls=%async_computation.1 | async-start | bytes 524288 | tf_op jit(solution)/shard_map/all_to_all | solution.py:466
  36.0 0.0 copy-start
  36.0 4.7 %decode.3.dec_1 = bf16[192,6656]{1,0:T(8,128)(2,1)} custom-call(s32[512,6656]{1,0:T(8,128)} %refs_0_.1), custom_call_target="tpu_custom_call" | custom-call | flops 20000000 | bytes 12000000 | tf_op jit(solution)/shard_map/decode/pallas_call | solution.py:140
  40.7 3.8 %all-to-all-done.1.got = bf16[8,32,512]{2,1,0:T(8,128)(2,1)S(1)} async-done(((bf16[8,32,512]{2,1,0:T(8,128)(2,1)}), bf16[8,32,512]{2,1,0:T(8,128)(2,1)S(1)}, u32[]{:S(2)}, u32[]{:S(2)}) %all-to-all-start.1) | async-done | bytes 262176 | tf_op jit(solution)/shard_map/all_to_all | solution.py:466
  44.5 0.1 server_step.1
  44.6 10.1 %all_to_all.20.ranks = bf16[8,16,512]{2,1,0:T(8,128)(2,1)S(1)} all-to-all(bf16[8,16,512]{2,1,0:T(8,128)(2,1)S(1)} %get-tuple-element.79), channel_id=1, replica_groups=mesh['zl'=2,'y'=4,'c'=2,'x'=4,'zh'=2] {'zl','y'}, dimensions={0} | all-to-all | bytes 262144 | tf_op jit(solution)/shard_map/all_to_all | solution.py:470
  54.7 0.0 collective-permute-start.6
  54.7 0.9 %server_state.1 = (f32[1,6656]{1,0:T(1,128)}, f32[1,6656]{1,0:T(1,128)}, f32[1,6656]{1,0:T(1,128)}, f32[2,512]{1,0:T(2,128)}, f32[2,512]{1,0:T(2,128)}, /*index=5*/f32[2,512]{1,0:T(2,128)}, bf16[512,256]{1,0:T(8,128)(2,1)S(1)}) custom-call(f32[32,512]{1,0:T(8,128)S(1)} %get-tuple-element.72.sums, f32[16,512]{1,0:T(8,128)S(1)} %get-tuple-element.69.pa, ...), custom_call_target="tpu_custom_call" | custom-call | tf_op jit(solution)/shard_map/server_state/pallas_call | solution.py:321
  55.6 0.5 collective-permute-done.6.mate_ranks
  56.0 0.0 copy-done
  56.0 4.5 %merge.1 = (f32[13,512,512]{2,1,0:T(8,128)S(1)}, f32[8,1,512]{2,1,0:T(1,128)S(1)}) custom-call(bf16[320,6656]{1,0:T(8,128)(2,1)} %get-tuple-element.63.dec_0, bf16[192,6656]{1,0:T(8,128)(2,1)} %decode.3.dec_1, f32[1,512]{1,0:T(1,128)S(1)} %bitcast.13, bf16[512,256]{1,0:T(8,128)(2,1)S(1)} %get-tuple-element.78.wide, ...), custom_call_target="tpu_custom_call" | custom-call | tf_op jit(solution)/shard_map/merge/pallas_call | solution.py:373
  60.5 11.6 %all_to_all.21.peaks = f32[8,1,512]{2,1,0:T(1,128)S(1)} all-to-all(f32[8,1,512]{2,1,0:T(1,128)S(1)} %get-tuple-element.81), channel_id=1, replica_groups=mesh['zl'=2,'y'=4,'c'=2,'x'=4,'zh'=2] {'x','zh'}, dimensions={0} | all-to-all | bytes 32768 | tf_op jit(solution)/shard_map/all_to_all | solution.py:475
  72.1 3.6 %normalise.1 = (bf16[512,6656]{1,0:T(8,128)(2,1)}, f32[1,512]{1,0:T(1,128)}) custom-call(f32[13,512,512]{2,1,0:T(8,128)S(1)} %get-tuple-element.80.merged, f32[8,1,512]{2,1,0:T(1,128)S(1)} %all_to_all.21.peaks), custom_call_target="tpu_custom_call" | custom-call | tf_op jit(solution)/shard_map/normalise/pallas_call | solution.py:431
  (4 shorter events, 0.0 us)
Async XLA Ops:
  0.6 7.1 %collective-permute-start.1 = (bf16[16,53248]{1,0:T(8,128)(2,1)}, bf16[16,53248]{1,0:T(8,128)(2,1)S(1)}, u32[]{:S(2)}, u32[]{:S(2)}) collective-permute-start(bf16[16,53248]{1,0:T(8,128)(2,1)} %bitcast.15), channel_id=1, source_target_pairs={{0,8},{8,0},{1,9},{9,1},{2,10},{10,2},{3,11},{11,3},{4,12},{12,4},... | collective-permute-start | bytes 5111816 | tf_op jit(solution)/shard_map/ppermute | solution.py:451
  0.7 7.0 %collective-permute-start.2 = (bf16[16,8192]{1,0:T(8,128)(2,1)}, bf16[16,8192]{1,0:T(8,128)(2,1)S(1)}, u32[]{:S(2)}, u32[]{:S(2)}) collective-permute-start(bf16[16,8192]{1,0:T(8,128)(2,1)} %bitcast.17), channel_id=1, source_target_pairs={{0,8},{8,0},{1,9},{9,1},{2,10},{10,2},{3,11},{11,3},{4,12},{12,4},... | collective-permute-start | bytes 786440 | tf_op jit(solution)/shard_map/ppermute | solution.py:451
  2.0 7.4 %collective-permute-start.3 = (f32[8,512]{1,0:T(8,128)S(1)}, f32[8,512]{1,0:T(8,128)S(1)}, u32[]{:S(2)}, u32[]{:S(2)}) collective-permute-start(f32[8,512]{1,0:T(8,128)S(1)} %pad_maximum_fusion.1), channel_id=1, source_target_pairs={{0,1},{1,0},{2,3},{3,2},{4,5},{5,4},{6,7},{7,6},{8,9},{9,8},{10,11... | collective-permute-start | bytes 49160 | tf_op jit(solution)/shard_map/ppermute | solution.py:454
  6.0 1.7 %collective-permute-start = (s32[1,2]{1,0:T(1,128)}, s32[1,2]{1,0:T(1,128)S(1)}, u32[]{:S(2)}, u32[]{:S(2)}) collective-permute-start(s32[1,2]{1,0:T(1,128)} %n.1), channel_id=1, source_target_pairs={{0,8},{8,0},{1,9},{9,1},{2,10},{10,2},{3,11},{11,3},{4,12},{12,4},... | collective-permute-start | bytes 32 | tf_op jit(solution)/shard_map/ppermute | solution.py:451
  9.4 20.6 %all-to-all-start = ((bf16[8,8,7680]{2,1,0:T(8,128)(2,1)}), bf16[8,8,7680]{2,1,0:T(8,128)(2,1)S(1)}, u32[]{:S(2)}, u32[]{:S(2)}) async-start(bf16[8,8,7680]{2,1,0:T(8,128)(2,1)} %bitcast.14), calls=%async_computation | async-start | bytes 1966080 | tf_op jit(solution)/shard_map/all_to_all | solution.py:458
  14.3 5.5 %collective-permute-start.4 = (f32[16,512]{1,0:T(8,128)S(1)}, f32[16,512]{1,0:T(8,128)S(1)}, u32[]{:S(2)}, u32[]{:S(2)}) collective-permute-start(f32[16,512]{1,0:T(8,128)S(1)} %pad_maximum_fusion), channel_id=1, source_target_pairs={{0,4},{2,6},{4,0},{6,2},{1,5},{3,7},{5,1},{7,3},{8,12},{10,14},{12... | collective-permute-start | bytes 98312 | tf_op jit(solution)/shard_map/ppermute | solution.py:461
  19.8 8.0 %collective-permute-start.5 = (f32[32,512]{1,0:T(8,128)S(1)}, f32[32,512]{1,0:T(8,128)S(1)}, u32[]{:S(2)}, u32[]{:S(2)}) collective-permute-start(f32[32,512]{1,0:T(8,128)S(1)} %constant_dynamic-update-slice_fusion.col_0), channel_id=1, source_target_pairs={{0,2},{2,0},{4,6},{6,4},{1,3},{3,1},{5,7},{7,5},{8,10},{10,8},{12,... | collective-permute-start | bytes 196616 | tf_op jit(solution)/shard_map/ppermute | solution.py:461
  30.9 13.6 %all-to-all-start.1 = ((bf16[8,32,512]{2,1,0:T(8,128)(2,1)}), bf16[8,32,512]{2,1,0:T(8,128)(2,1)S(1)}, u32[]{:S(2)}, u32[]{:S(2)}) async-start(bf16[8,32,512]{2,1,0:T(8,128)(2,1)} %row_sum.1), calls=%async_computation.1 | async-start | bytes 524288 | tf_op jit(solution)/shard_map/all_to_all | solution.py:466
  36.0 20.0 %copy-start = (f32[512]{0:T(512)S(1)}, f32[512]{0:T(512)}, u32[]{:S(2)}) copy-start(f32[512]{0:T(512)} %param.12) | copy-start | bytes 6148
  54.7 1.3 %collective-permute-start.6 = (bf16[8,16,512]{2,1,0:T(8,128)(2,1)S(1)}, bf16[8,16,512]{2,1,0:T(8,128)(2,1)S(1)}, u32[]{:S(2)}, u32[]{:S(2)}) collective-permute-start(bf16[8,16,512]{2,1,0:T(8,128)(2,1)S(1)} %all_to_all.20.ranks), channel_id=1, source_target_pairs={{0,8},{8,0},{1,9},{9,1},{2,10},{10,2},{3,11},{11,3},{4,12},{12,4},... | collective-permute-start | bytes 393224 | tf_op jit(solution)/shard_map/ppermute | solution.py:474

commit v6 on v5

--- a/solution.py
+++ b/solution.py
@@ -17,6 +17,7 @@
 peak_eps = 1e-06
 
 f32, bf16, i32 = jnp.float32, jnp.bfloat16, jnp.int32
+f8 = jnp.float8_e4m3fn
 SDS = jax.ShapeDtypeStruct
 
 ROW, COL = ("zl", "y", "c"), ("x", "zh")
@@ -112,7 +113,7 @@
             store(s - SLOTS, slot).wait()
 
         def group(g, carry):
-            at = pl.ds(pl.multiple_of(g * 16, 16), 16)
+            at = pl.ds(pl.multiple_of(g * 32, 32), 32)
             for t in range(PIECES):
                 here = pl.ds(t * PIECE, PIECE)
                 code = buf[slot, at, here]
@@ -121,10 +122,10 @@
                     jnp.bitwise_and(code, 127) - eights + 8, lax.shift_right_logical(eights, 3)
                 )
                 value = jnp.where(code >= 128, -value, value)
-                done[slot, at, here] = value.astype(f32).astype(bf16)
+                done[slot, at, here] = (value.astype(f32) * 2.0**-10).astype(f8)
             return carry
 
-        lax.fori_loop(0, DEC_ROWS // 16, group, 0)
+        lax.fori_loop(0, DEC_ROWS // 32, group, 0)
         store(s, slot).start()
         return carry
 
@@ -139,12 +140,12 @@
     count = len(state)
     return pl.pallas_call(
         functools.partial(decode_kernel, first, rows // DEC_ROWS, count),
-        out_shape=(pltpu.HBM((rows, WIDTH), bf16),) + tuple(kept(x.shape if x.shape[0] > 1 else (16, PIECE)) for x in state),
+        out_shape=(pltpu.HBM((rows, WIDTH), f8),) + tuple(kept(x.shape if x.shape[0] > 1 else (16, PIECE)) for x in state),
         in_specs=[in_hbm()] * (1 + count),
         out_specs=(in_hbm(),) + (in_vmem(),) * count,
         scratch_shapes=[
             pltpu.VMEM((SLOTS, DEC_ROWS, WIDTH), i32),
-            pltpu.VMEM((SLOTS, DEC_ROWS, WIDTH), bf16),
+            pltpu.VMEM((SLOTS, DEC_ROWS, WIDTH), f8),
             pltpu.SemaphoreType.DMA((SLOTS,)),
             pltpu.SemaphoreType.DMA((SLOTS,)),
             pltpu.SemaphoreType.DMA((3 * PIECES + 3,)),
@@ -329,7 +330,7 @@
     )(*map(near, (sums, *a_state, *b_state)), *col_state)
 
 
-GROUPS = (1, 2, 4, 6)
+GROUPS = (2, 5, 6)
 
 
 def merge_kernel(dec_0, dec_1, scale, wide, ranks, mate_ranks, merged, peaks, buf, row_scale, tops, sems):
@@ -344,7 +345,7 @@
             fetches[-1][-1].start()
             row += ROW_PARTS[q]
         piece += count
-    row_scale[...] = jnp.transpose(jnp.broadcast_to(scale[...] * 2.0**-10, (128, DEPTH)))
+    row_scale[...] = jnp.transpose(jnp.broadcast_to(scale[...], (128, DEPTH)))
     lane = jnp.bitwise_and(lax.broadcasted_iota(i32, (DEPTH, 256), 1), 15)
     right = jnp.concatenate([r[...].reshape(128, PIECE) for r in (ranks, mate_ranks)], axis=0)
     tops[...] = jnp.zeros_like(tops)
@@ -376,7 +377,7 @@
         in_specs=[in_hbm()] * 2 + [in_vmem()] * 4,
         out_specs=(in_vmem(), in_vmem()),
         scratch_shapes=[
-            pltpu.VMEM((DEPTH, WIDTH), bf16),
+            pltpu.VMEM((DEPTH, WIDTH), f8),
             pltpu.VMEM((DEPTH, 128), f32),
             pltpu.VMEM((DEPTH, 128), f32),
             pltpu.SemaphoreType.DMA((len(GROUPS), 2)),

time: 76.1 us -> 75.9 us (level)
  transfers between devices with their start and end apart: 9 -> 9, of which waited for: 4 -> 4; matrix products, arithmetic and copies ran while one was open for 1% -> 1% of each run, Pallas kernels for 20% -> 21%
where the time goes in v6:
time: 75.9 us; the launch traced here: 75.5 us
  Pallas kernels  24.2 us (32%)
  blocking collectives  21.8 us (29%)
  starting transfers between devices  19.2 us (25%)
  waiting for transfers between devices  8.67 us (11%)
  other arithmetic  0.78 us (1%)
    all_to_all x1, blocking collectives, local(): out, scales = normalise(merged, exchange(peaks, COL))  11.6 us
    pallas_call x2, Pallas kernels, decode(): pl.pallas_call(functools.partial(decode_kernel, first, rows // DEC_ROWS,...  11.4 us
    all_to_all x1, blocking collectives, local(): ranks = exchange(send, ('zl', 'y'))  10.2 us
    all_to_all x1, starting transfers between devices, local(): got = exchange(message, COL)  5.07 us
    all_to_all x1, starting transfers between devices, local(): got = exchange(pairs.reshape(CHIPS, 8, LANES), ('zl', 'y'))  4.93 us
    ppermute x2, starting transfers between devices, local(): other = lax.ppermute(block, 'x', [(k, k ^ apart) for k in range(4)])  4.6 us
    pallas_call x1, Pallas kernels, merge(): pl.pallas_call(merge_kernel, out_shape=(pltpu.VMEM((PIECES, DEPTH, PIECE)...  4.06 us
    ppermute x1, starting transfers between devices, local(): other = swap(block, 'zh')  4.04 us
  transfers between devices with their start and end apart: 9, of which 4 were waited for; matrix products, arithmetic and copies ran while one was open for 1% of the time, Pallas kernels for 21%

profile of v6, /device:TPU:0, one launch (start us, length us, event | category | flops | bytes accessed | tf_op | source)
XLA Modules:
  0.0 75.5 jit_solution(11380515055800442497)
XLA Ops:
  0.6 0.1 collective-permute-start.1
  0.7 0.5 collective-permute-start.2
  1.2 0.8 %pad_maximum_fusion.1 = f32[8,512]{1,0:T(8,128)S(1)} fusion(f32[2,512]{1,0:T(2,128)} %bitcast.19, f32[2,512]{1,0:T(2,128)} %bitcast.23, f32[2,512]{1,0:T(2,128)} %bitcast.21), kind=kLoop, calls=%fused_computation.1 | loop fusion | flops 12288 | bytes 28672 | tf_op jit(solution)/shard_map/concatenate | solution.py:454
  2.0 4.0 %collective-permute-start.3 = (f32[8,512]{1,0:T(8,128)S(1)}, f32[8,512]{1,0:T(8,128)S(1)}, u32[]{:S(2)}, u32[]{:S(2)}) collective-permute-start(f32[8,512]{1,0:T(8,128)S(1)} %pad_maximum_fusion.1), channel_id=1, source_target_pairs={{0,1},{1,0},{2,3},{3,2},{4,5},{5,4},{6,7},{7,6},{8,9},{9,8},{10,11... | collective-permute-start | bytes 49160 | tf_op jit(solution)/shard_map/ppermute | solution.py:455
  6.0 0.0 collective-permute-start
  6.0 1.7 %own_deltas.1 = (s32[1,2]{1,0:T(1,128)S(1)}, bf16[128,6656]{1,0:T(8,128)(2,1)S(1)}, bf16[16,8192]{1,0:T(8,128)(2,1)S(1)}) custom-call(s32[1,2]{1,0:T(1,128)} %n.1, bf16[16,53248]{1,0:T(8,128)(2,1)} %bitcast.16, bf16[16,8192]{1,0:T(8,128)(2,1)} %bitcast.18), custom_call_target="tpu_custom_call" | custom-call | tf_op jit(solution)/shard_map/own_deltas/pallas_call | solution.py:173
  7.7 0.0 collective-permute-done.mate_n
  7.7 0.0 collective-permute-done.2.mate_b
  7.7 0.0 collective-permute-done.1.mate_a
  7.8 1.6 %pair_sum.1 = bf16[64,7680]{1,0:T(8,128)(2,1)} custom-call(s32[1,2]{1,0:T(1,128)S(1)} %get-tuple-element.49.own_n, s32[1,2]{1,0:T(1,128)S(1)} %collective-permute-done.mate_n, bf16[128,6656]{1,0:T(8,128)(2,1)S(1)} %get-tuple-element.50.own_a, bf16[16,53248]{1,0:T(8,128)(2,1)S(1)} %collective-permute-done.1.mate_a, ...), custom_call_target="tpu_custom_call" | custom-call | tf_op jit(solution)/shard_map/pair_sum/pallas_call | solution.py:222
  9.4 0.0 collective-permute-done.3
  9.4 4.9 %all-to-all-start = ((bf16[8,8,7680]{2,1,0:T(8,128)(2,1)}), bf16[8,8,7680]{2,1,0:T(8,128)(2,1)S(1)}, u32[]{:S(2)}, u32[]{:S(2)}) async-start(bf16[8,8,7680]{2,1,0:T(8,128)(2,1)} %bitcast.14), calls=%async_computation | async-start | bytes 1966080 | tf_op jit(solution)/shard_map/all_to_all | solution.py:459
  14.3 3.1 %collective-permute-start.4 = (f32[16,512]{1,0:T(8,128)S(1)}, f32[16,512]{1,0:T(8,128)S(1)}, u32[]{:S(2)}, u32[]{:S(2)}) collective-permute-start(f32[16,512]{1,0:T(8,128)S(1)} %pad_maximum_fusion), channel_id=1, source_target_pairs={{0,4},{2,6},{4,0},{6,2},{1,5},{3,7},{5,1},{7,3},{8,12},{10,14},{12... | collective-permute-start | bytes 98312 | tf_op jit(solution)/shard_map/ppermute | solution.py:462
  17.4 2.4 %collective-permute-done.4 = f32[16,512]{1,0:T(8,128)S(1)} collective-permute-done((f32[16,512]{1,0:T(8,128)S(1)}, f32[16,512]{1,0:T(8,128)S(1)}, u32[]{:S(2)}, u32[]{:S(2)}) %collective-permute-start.4) | collective-permute-done | bytes 32800 | tf_op jit(solution)/shard_map/ppermute | solution.py:462
  19.8 1.5 %collective-permute-start.5 = (f32[32,512]{1,0:T(8,128)S(1)}, f32[32,512]{1,0:T(8,128)S(1)}, u32[]{:S(2)}, u32[]{:S(2)}) collective-permute-start(f32[32,512]{1,0:T(8,128)S(1)} %constant_dynamic-update-slice_fusion.col_0), channel_id=1, source_target_pairs={{0,2},{2,0},{4,6},{6,4},{1,3},{3,1},{5,7},{7,5},{8,10},{10,8},{12,... | collective-permute-start | bytes 196616 | tf_op jit(solution)/shard_map/ppermute | solution.py:462
  21.3 6.6 %decode.2 = (f8e4m3fn[320,6656]{1,0:T(32,128)(4,1)}, f32[16,512]{1,0:T(8,128)S(1)}, f32[16,512]{1,0:T(8,128)S(1)}, f32[16,512]{1,0:T(8,128)S(1)}, f32[2,512]{1,0...) custom-call(s32[512,6656]{1,0:T(8,128)} %refs_0_.1, f32[1,6656]{1,0:T(1,128)} %refs_1_.1, f32[1,6656]{1,0:T(1,128)} %refs_2_.1, ...), custom_call_target="tpu_custom_call" | custom-call | flops 20000000 | bytes 12000000 | tf_op jit(solution)/shard_map/decode/pallas_call | solution.py:141
  27.9 0.0 collective-permute-done.5.col_1
  28.0 2.0 %all-to-all-done.got = bf16[8,8,7680]{2,1,0:T(8,128)(2,1)S(1)} async-done(((bf16[8,8,7680]{2,1,0:T(8,128)(2,1)}), bf16[8,8,7680]{2,1,0:T(8,128)(2,1)S(1)}, u32[]{:S(2)}, u32[]{:S(2)}) %all-to-all-start) | async-done | bytes 983072 | tf_op jit(solution)/shard_map/all_to_all | solution.py:459
  30.0 0.9 %row_sum.1 = bf16[8,32,512]{2,1,0:T(8,128)(2,1)} custom-call(bf16[8,8,7680]{2,1,0:T(8,128)(2,1)S(1)} %all-to-all-done.got), custom_call_target="tpu_custom_call" | custom-call | tf_op jit(solution)/shard_map/row_sum/pallas_call | solution.py:250
  30.9 5.1 %all-to-all-start.1 = ((bf16[8,32,512]{2,1,0:T(8,128)(2,1)}), bf16[8,32,512]{2,1,0:T(8,128)(2,1)S(1)}, u32[]{:S(2)}, u32[]{:S(2)}) async-start(bf16[8,32,512]{2,1,0:T(8,128)(2,1)} %row_sum.1), calls=%async_computation.1 | async-start | bytes 524288 | tf_op jit(solution)/shard_map/all_to_all | solution.py:467
  36.0 0.0 copy-start
  36.0 4.7 %decode.3.dec_1 = f8e4m3fn[192,6656]{1,0:T(32,128)(4,1)} custom-call(s32[512,6656]{1,0:T(8,128)} %refs_0_.1), custom_call_target="tpu_custom_call" | custom-call | flops 20000000 | bytes 12000000 | tf_op jit(solution)/shard_map/decode/pallas_call | solution.py:141
  40.8 3.8 %all-to-all-done.1.got = bf16[8,32,512]{2,1,0:T(8,128)(2,1)S(1)} async-done(((bf16[8,32,512]{2,1,0:T(8,128)(2,1)}), bf16[8,32,512]{2,1,0:T(8,128)(2,1)S(1)}, u32[]{:S(2)}, u32[]{:S(2)}) %all-to-all-start.1) | async-done | bytes 262176 | tf_op jit(solution)/shard_map/all_to_all | solution.py:467
  44.5 0.1 server_step.1
  44.6 10.2 %all_to_all.20.ranks = bf16[8,16,512]{2,1,0:T(8,128)(2,1)S(1)} all-to-all(bf16[8,16,512]{2,1,0:T(8,128)(2,1)S(1)} %get-tuple-element.79), channel_id=1, replica_groups=mesh['zl'=2,'y'=4,'c'=2,'x'=4,'zh'=2] {'zl','y'}, dimensions={0} | all-to-all | bytes 262144 | tf_op jit(solution)/shard_map/all_to_all | solution.py:471
  54.8 0.0 collective-permute-start.6
  54.8 0.9 %server_state.1 = (f32[1,6656]{1,0:T(1,128)}, f32[1,6656]{1,0:T(1,128)}, f32[1,6656]{1,0:T(1,128)}, f32[2,512]{1,0:T(2,128)}, f32[2,512]{1,0:T(2,128)}, /*index=5*/f32[2,512]{1,0:T(2,128)}, bf16[512,256]{1,0:T(8,128)(2,1)S(1)}) custom-call(f32[32,512]{1,0:T(8,128)S(1)} %get-tuple-element.72.sums, f32[16,512]{1,0:T(8,128)S(1)} %get-tuple-element.69.pa, ...), custom_call_target="tpu_custom_call" | custom-call | tf_op jit(solution)/shard_map/server_state/pallas_call | solution.py:322
  55.7 0.5 collective-permute-done.6.mate_ranks
  56.1 0.0 copy-done
  56.1 4.1 %merge.1 = (f32[13,512,512]{2,1,0:T(8,128)S(1)}, f32[8,1,512]{2,1,0:T(1,128)S(1)}) custom-call(f8e4m3fn[320,6656]{1,0:T(32,128)(4,1)} %get-tuple-element.63.dec_0, f8e4m3fn[192,6656]{1,0:T(32,128)(4,1)} %decode.3.dec_1, f32[1,512]{1,0:T(1,128)S(1)} %bitcast.13, bf16[512,256]{1,0:T(8,128)(2,1)S(1)} %get-tuple-element.78.wide, ...), custom_call_target="tpu_custom_call" | custom-call | tf_op jit(solution)/shard_map/merge/pallas_call | solution.py:374
  60.2 11.6 %all_to_all.21.peaks = f32[8,1,512]{2,1,0:T(1,128)S(1)} all-to-all(f32[8,1,512]{2,1,0:T(1,128)S(1)} %get-tuple-element.81), channel_id=1, replica_groups=mesh['zl'=2,'y'=4,'c'=2,'x'=4,'zh'=2] {'x','zh'}, dimensions={0} | all-to-all | bytes 32768 | tf_op jit(solution)/shard_map/all_to_all | solution.py:476
  71.8 3.6 %normalise.1 = (bf16[512,6656]{1,0:T(8,128)(2,1)}, f32[1,512]{1,0:T(1,128)}) custom-call(f32[13,512,512]{2,1,0:T(8,128)S(1)} %get-tuple-element.80.merged, f32[8,1,512]{2,1,0:T(1,128)S(1)} %all_to_all.21.peaks), custom_call_target="tpu_custom_call" | custom-call | tf_op jit(solution)/shard_map/normalise/pallas_call | solution.py:432
  (4 shorter events, 0.0 us)
Async XLA Ops:
  0.6 7.1 %collective-permute-start.1 = (bf16[16,53248]{1,0:T(8,128)(2,1)}, bf16[16,53248]{1,0:T(8,128)(2,1)S(1)}, u32[]{:S(2)}, u32[]{:S(2)}) collective-permute-start(bf16[16,53248]{1,0:T(8,128)(2,1)} %bitcast.15), channel_id=1, source_target_pairs={{0,8},{8,0},{1,9},{9,1},{2,10},{10,2},{3,11},{11,3},{4,12},{12,4},... | collective-permute-start | bytes 5111816 | tf_op jit(solution)/shard_map/ppermute | solution.py:452
  0.7 7.0 %collective-permute-start.2 = (bf16[16,8192]{1,0:T(8,128)(2,1)}, bf16[16,8192]{1,0:T(8,128)(2,1)S(1)}, u32[]{:S(2)}, u32[]{:S(2)}) collective-permute-start(bf16[16,8192]{1,0:T(8,128)(2,1)} %bitcast.17), channel_id=1, source_target_pairs={{0,8},{8,0},{1,9},{9,1},{2,10},{10,2},{3,11},{11,3},{4,12},{12,4},... | collective-permute-start | bytes 786440 | tf_op jit(solution)/shard_map/ppermute | solution.py:452
  2.0 7.4 %collective-permute-start.3 = (f32[8,512]{1,0:T(8,128)S(1)}, f32[8,512]{1,0:T(8,128)S(1)}, u32[]{:S(2)}, u32[]{:S(2)}) collective-permute-start(f32[8,512]{1,0:T(8,128)S(1)} %pad_maximum_fusion.1), channel_id=1, source_target_pairs={{0,1},{1,0},{2,3},{3,2},{4,5},{5,4},{6,7},{7,6},{8,9},{9,8},{10,11... | collective-permute-start | bytes 49160 | tf_op jit(solution)/shard_map/ppermute | solution.py:455
  6.0 1.7 %collective-permute-start = (s32[1,2]{1,0:T(1,128)}, s32[1,2]{1,0:T(1,128)S(1)}, u32[]{:S(2)}, u32[]{:S(2)}) collective-permute-start(s32[1,2]{1,0:T(1,128)} %n.1), channel_id=1, source_target_pairs={{0,8},{8,0},{1,9},{9,1},{2,10},{10,2},{3,11},{11,3},{4,12},{12,4},... | collective-permute-start | bytes 32 | tf_op jit(solution)/shard_map/ppermute | solution.py:452
  9.4 20.6 %all-to-all-start = ((bf16[8,8,7680]{2,1,0:T(8,128)(2,1)}), bf16[8,8,7680]{2,1,0:T(8,128)(2,1)S(1)}, u32[]{:S(2)}, u32[]{:S(2)}) async-start(bf16[8,8,7680]{2,1,0:T(8,128)(2,1)} %bitcast.14), calls=%async_computation | async-start | bytes 1966080 | tf_op jit(solution)/shard_map/all_to_all | solution.py:459
  14.3 5.5 %collective-permute-start.4 = (f32[16,512]{1,0:T(8,128)S(1)}, f32[16,512]{1,0:T(8,128)S(1)}, u32[]{:S(2)}, u32[]{:S(2)}) collective-permute-start(f32[16,512]{1,0:T(8,128)S(1)} %pad_maximum_fusion), channel_id=1, source_target_pairs={{0,4},{2,6},{4,0},{6,2},{1,5},{3,7},{5,1},{7,3},{8,12},{10,14},{12... | collective-permute-start | bytes 98312 | tf_op jit(solution)/shard_map/ppermute | solution.py:462
  19.8 8.1 %collective-permute-start.5 = (f32[32,512]{1,0:T(8,128)S(1)}, f32[32,512]{1,0:T(8,128)S(1)}, u32[]{:S(2)}, u32[]{:S(2)}) collective-permute-start(f32[32,512]{1,0:T(8,128)S(1)} %constant_dynamic-update-slice_fusion.col_0), channel_id=1, source_target_pairs={{0,2},{2,0},{4,6},{6,4},{1,3},{3,1},{5,7},{7,5},{8,10},{10,8},{12,... | collective-permute-start | bytes 196616 | tf_op jit(solution)/shard_map/ppermute | solution.py:462
  30.9 13.6 %all-to-all-start.1 = ((bf16[8,32,512]{2,1,0:T(8,128)(2,1)}), bf16[8,32,512]{2,1,0:T(8,128)(2,1)S(1)}, u32[]{:S(2)}, u32[]{:S(2)}) async-start(bf16[8,32,512]{2,1,0:T(8,128)(2,1)} %row_sum.1), calls=%async_computation.1 | async-start | bytes 524288 | tf_op jit(solution)/shard_map/all_to_all | solution.py:467
  36.0 20.1 %copy-start = (f32[512]{0:T(512)S(1)}, f32[512]{0:T(512)}, u32[]{:S(2)}) copy-start(f32[512]{0:T(512)} %param.12) | copy-start | bytes 6148
  54.8 1.3 %collective-permute-start.6 = (bf16[8,16,512]{2,1,0:T(8,128)(2,1)S(1)}, bf16[8,16,512]{2,1,0:T(8,128)(2,1)S(1)}, u32[]{:S(2)}, u32[]{:S(2)}) collective-permute-start(bf16[8,16,512]{2,1,0:T(8,128)(2,1)S(1)} %all_to_all.20.ranks), channel_id=1, source_target_pairs={{0,8},{8,0},{1,9},{9,1},{2,10},{10,2},{3,11},{11,3},{4,12},{12,4},... | collective-permute-start | bytes 393224 | tf_op jit(solution)/shard_map/ppermute | solution.py:475
